TPU v7x, 128 devices: a whole 4x4x4 slice. The times are simulated.
128 devices in a mesh: expert: 8 (over z, core), task: 4 (over y), shard: 4 (over x).
Axes of the slice: x: 4, y: 4, z: 4, core: 2. Of those that a mesh axis runs over, the one named last changes fastest.
Arguments:
- weights: bfloat16 [4, 8, 8192, 2048], P('task', None, ('expert', 'shard')), may hold values from -6 to 6
- fisher: bfloat16 [4, 8, 8192, 2048], P('task', None, ('expert', 'shard')), may hold values from 0.049804688 to 5
- base_weights: bfloat16 [8, 8192, 2048], P('expert', 'task', 'shard'), may hold values from -6 to 6
- tile_list: int32 [4, 8, 32, 1], P('task'), may hold values from 0 to 1, as said below
- tile_count: int32 [4, 8, 32], P('task'), may hold values from 0 to 1, as said below
Outputs:
- merged: bfloat16 [8, 8192, 2048], P('expert', 'task', 'shard')
Inputs may be any that keep to these rules, and one draw needn't show every extreme that they name: `tile_list`: for each fine-fit, expert and row block the first tile_count entries are distinct tiles of the block, numbered 0 to 1, in ascending order; the remaining entries are 0. `tile_count`: 1 is reached, and for each fine-fit some expert has 1 in every row block.
All inputs are finite; a program needn't handle non-finite values.
Results may differ from a plain program's by a relative error of at most 0.006.
Values may be sent and summed in bfloat16 or wider, within the bound.
No kernel may reach another device: no remote copies, remote signals or barrier semaphores. Data moves between devices by JAX's collectives and lax.ppermute only.
A program may use at most 128 MiB of HBM per device.

v0:
```python
import jax
import jax.numpy as jnp
from jax import lax
from jax.sharding import PartitionSpec as P

TILE = 128


PRIOR_WEIGHT = 0.5


def sent_together(arrays, axis, dim, along):
    ends, at = ([], 0)
    for a in arrays[:-1]:
        at += a.shape[along]
        ends.append(at)
    both = jnp.concatenate(arrays, axis=along)
    return tuple(
        jnp.split(lax.psum_scatter(both, axis, scatter_dimension=dim, tiled=True), ends, axis=along)
    )


def split_up(x, dim, devices):
    before, after = (x.shape[:dim], x.shape[dim + 1 :])
    return jnp.moveaxis(x.reshape(*before, devices, -1, *after), dim, 0)


def in_order(blocks, dim):
    shape = list(blocks.shape[1:])
    shape[dim] *= blocks.shape[0]
    return jnp.moveaxis(blocks, 0, dim).reshape(shape)


def one_exchange(x, axis, axes, splits, concats):
    sizes = [lax.axis_size(a) for a in axes]
    blocks = split_up(x, splits[0], sizes[0])
    blocks = jnp.moveaxis(split_up(blocks, splits[1] + 1, sizes[1]), 0, 1)
    inside = blocks.shape[2:]
    blocks = blocks.reshape(-1, *inside)
    blocks = lax.all_to_all(blocks, axis, split_axis=0, concat_axis=0, tiled=True)
    blocks = in_order(blocks.reshape(*sizes, *inside), concats[0] + 1)
    return in_order(blocks, concats[1])


def side_by_side(arrays, axis, split_dim, concat_dim, along):
    widths = [a.shape[along] for a in arrays]
    both = jnp.concatenate(arrays, axis=along)
    whole = lax.all_to_all(both, axis, split_axis=split_dim, concat_axis=concat_dim, tiled=True)
    return tuple(jnp.split(whole, [sum(widths[:k]) for k in range(1, len(widths))], axis=along))


def selection(listed, counts, per_block):
    slot_number = jnp.arange(listed.shape[-1], dtype=jnp.int32)
    slot_live = slot_number[None, :] < counts[:, None]
    matches = (
        listed[:, :, None] == jnp.arange(per_block, dtype=jnp.int32)[None, None, :]
    ) & slot_live[:, :, None]
    return matches.astype(jnp.bfloat16)


def masked_terms(picked, weight_tiles, fisher_tiles):
    kept_tiles = jnp.sum(picked.astype(jnp.float32), axis=1)[:, :, None, None]
    fisher_now = fisher_tiles.astype(jnp.float32) * kept_tiles
    term_full = (fisher_now * weight_tiles.astype(jnp.float32)).astype(jnp.bfloat16)
    share_full = fisher_now.astype(jnp.bfloat16)
    return (term_full, share_full)


def local(weights, fisher, base_weights, tile_list, tile_count):
    experts = weights.shape[1]
    block_rows = weights.shape[2]
    columns = weights.shape[3]
    per_block = block_rows // TILE
    shard_count = lax.axis_size("shard")
    expert_count = lax.axis_size("expert")
    task_count = lax.axis_size("task")
    block_count = expert_count * shard_count
    column_piece = columns // shard_count
    block_index = lax.axis_index("expert") * shard_count + lax.axis_index("shard")
    own_list = lax.dynamic_index_in_dim(tile_list[0], block_index, 1, keepdims=False)
    own_count = lax.dynamic_index_in_dim(tile_count[0], block_index, 1, keepdims=False)
    picked = selection(own_list, own_count, per_block)
    weight_tiles = weights[0].reshape(experts, per_block, TILE, columns)
    fisher_tiles = fisher[0].reshape(experts, per_block, TILE, columns)
    sub_rows = block_rows // task_count
    term_full, share_full = masked_terms(picked, weight_tiles, fisher_tiles)
    term_rows = term_full.reshape(experts, block_rows, columns).astype(jnp.float32)
    share_rows = share_full.reshape(experts, block_rows, columns).astype(jnp.float32)
    summed_term, summed_share = tuple(
        (
            part.astype(jnp.float32)
            for part in sent_together(
                (term_rows.astype(jnp.bfloat16), share_rows.astype(jnp.bfloat16)), "task", 1, 0
            )
        )
    )
    sent_term = summed_term.reshape(experts, 1, 1, sub_rows, shard_count, column_piece)
    sent_share = summed_share.reshape(experts, 1, 1, sub_rows, shard_count, column_piece)
    moved_term, moved_share = (
        one_exchange(
            sent_term.astype(jnp.bfloat16), ("expert", "shard"), ("expert", "shard"), (0, 4), (1, 2)
        ).astype(sent_term.dtype),
        one_exchange(
            sent_share.astype(jnp.bfloat16),
            ("expert", "shard"),
            ("expert", "shard"),
            (0, 4),
            (1, 2),
        ).astype(sent_share.dtype),
    )
    group = block_count // task_count
    moved_term = moved_term.reshape(task_count, group, 1, sub_rows, column_piece)
    moved_share = moved_share.reshape(task_count, group, 1, sub_rows, column_piece)
    final_term, final_share = tuple(
        (
            part.astype(jnp.float32)
            for part in side_by_side(
                (moved_term.astype(jnp.bfloat16), moved_share.astype(jnp.bfloat16)), "task", 0, 2, 1
            )
        )
    )
    numerator = final_term.reshape(1, group * task_count * sub_rows, column_piece)
    denominator = final_share.reshape(1, group * task_count * sub_rows, column_piece)
    merged = (numerator + PRIOR_WEIGHT * base_weights.astype(jnp.float32)) / (
        denominator + PRIOR_WEIGHT
    )
    return merged.astype(jnp.bfloat16)


def solution(mesh):
    in_specs = (
        P("task", None, ("expert", "shard"), None),
        P("task", None, ("expert", "shard"), None),
        P("expert", "task", "shard"),
        P("task", None, None, None),
        P("task", None, None),
    )
    out_specs = P("expert", "task", "shard")
    return jax.shard_map(local, mesh=mesh, in_specs=in_specs, out_specs=out_specs, check_vma=False)
```

profile of v0, /device:TPU:0, one launch (start us, length us, event | category | flops | bytes accessed | tf_op | source)
XLA Modules:
  0.0 316.8 jit_solution(10990819741044119428)
XLA Ops:
  6.5 0.0 copy-start
  6.5 0.0 reduce-scatter.2.cloned.1.call-start
  6.5 0.7 copy-done
  7.2 0.3 dynamic-slice_reduce_fusion
  7.5 0.9 fusion.4
  8.4 0.1 broadcast_bitcast_fusion
  8.5 8.5 %fusion = (bf16[8,256,2048]{2,1,0:T(8,128)(2,1)S(1)}, bf16[8,256,2048]{2,1,0:T(8,128)(2,1)S(1)}) fusion(bf16[1,8,256,2048]{3,2,1,0:T(8,128)(2,1)} %param.5, bf16[1,8,256,2048]{3,2,1,0:T(8,128)(2,1)} %param.6, f32[8,256]{1,0:T(8,128)S(1)} %broadcast_bitcast_fusion), kind=kLoop, calls=%fused_computation.2 | loop fusion | flops 25165824 | bytes 33562624 | tf_op jit(solution)/shard_map/convert_element_type | solution.py:64
  17.0 6.6 %pad_maximum_fusion = bf16[16,256,2048]{2,1,0:T(8,128)(2,1)} fusion(bf16[8,256,2048]{2,1,0:T(8,128)(2,1)S(1)} %get-tuple-element.6, bf16[8,256,2048]{2,1,0:T(8,128)(2,1)S(1)} %get-tuple-element.5), kind=kLoop, calls=%fused_computation | loop fusion | flops 8388608 | bytes 33554432 | tf_op jit(solution)/shard_map/concatenate | solution.py:17
  23.6 0.0 reduce-scatter.2.cloned.1.call-update
  23.7 150.5 %reduce-scatter.2.cloned.1.call-done = bf16[16,64,2048]{2,1,0:T(8,128)(2,1)} async-done(((bf16[16,256,2048]{2,1,0:T(8,128)(2,1)}), bf16[16,64,2048]{2,1,0:T(8,128)(2,1)}) %reduce-scatter.2.cloned.1.call-update) | async-done | bytes 4194320 | tf_op jit(solution)/shard_map/reduce_scatter | solution.py:19
  174.2 4.8 %fusion.6 = (bf16[8,64,2048]{2,1,0:T(8,128)(2,1)}, bf16[8,64,2048]{2,1,0:T(8,128)(2,1)}) fusion(bf16[16,64,2048]{2,1,0:T(8,128)(2,1)} %reduce-scatter.2.cloned.1.call-done), kind=kLoop, calls=%fused_computation.17 | loop fusion | bytes 8388608 | tf_op jit(solution)/shard_map/split | solution.py:19
  179.0 3.3 %convert_element_type.107 = bf16[8,1,1,1,64,4,1,512]{7,5,4,0,6,3,2,1:T(4,128)(2,1)S(1)} reshape(bf16[8,64,2048]{2,1,0:T(8,128)(2,1)} %get-tuple-element.7) | data formatting | bytes 4194304 | tf_op jit(solution)/shard_map/convert_element_type | solution.py:101
  182.3 1.8 copy.10
  184.2 0.0 copy-start.2
  184.2 7.5 %all-to-all-start = ((bf16[32,1,1,1,64,1,512]{6,4,5,3,2,1,0:T(8,128)(2,1)}), bf16[32,1,1,1,64,1,512]{6,4,5,3,2,1,0:T(8,128)(2,1)}, u32[]{:S(2)}, u32[]{:S(2)}) async-start(bf16[32,1,1,1,64,1,512]{6,4,5,3,2,1,0:T(8,128)(2,1)} %bitcast.5), calls=%async_computation.1 | async-start | bytes 4194304 | tf_op jit(solution)/shard_map/all_to_all | solution.py:40
  191.7 0.0 copy-done.2
  191.7 2.8 convert_element_type.108
  194.5 2.1 copy.12
  196.6 22.6 %all-to-all-done = bf16[32,1,1,1,64,1,512]{6,4,5,3,2,1,0:T(8,128)(2,1)} async-done(((bf16[32,1,1,1,64,1,512]{6,4,5,3,2,1,0:T(8,128)(2,1)}), bf16[32,1,1,1,64,1,512]{6,4,5,3,2,1,0:T(8,128)(2,1)}, u32[]{:S(2)}, u32[]{:S(2)}) %all-to-all-start) | async-done | bytes 2097184 | tf_op jit(solution)/shard_map/all_to_all | solution.py:40
  219.2 33.0 %all_to_all.28 = bf16[32,1,1,1,64,1,512]{6,4,5,3,2,1,0:T(8,128)(2,1)S(1)} all-to-all(bf16[32,1,1,1,64,1,512]{6,4,5,3,2,1,0:T(8,128)(2,1)S(1)} %bitcast.51), channel_id=1, replica_groups=mesh['expert'=8,'task'=4,'shard'=4] {'expert','shard'}, dimensions={0} | all-to-all | bytes 4194304 | tf_op jit(solution)/shard_map/all_to_all | solution.py:40
  252.1 2.0 maximum_bitcast_fusion
  254.1 51.0 %all_to_all.29 = bf16[4,16,1,64,512]{4,3,1,2,0:T(8,128)(2,1)S(1)} all-to-all(bf16[4,16,1,64,512]{4,3,1,2,0:T(8,128)(2,1)S(1)} %maximum_bitcast_fusion), channel_id=1, replica_groups=mesh['expert'=8,'task'=4,'shard'=4] {'task'}, dimensions={0} | all-to-all | bytes 8388608 | tf_op jit(solution)/shard_map/all_to_all | solution.py:48
  305.1 0.5 copy.17
  305.6 0.2 split.18
  305.8 0.0 copy-start.3
  305.8 0.0 copy-start.1
  305.9 0.6 convert_add_fusion.1
  306.4 1.0 copy-done.3
  307.4 2.5 fusion.3
  309.9 0.0 copy-done.1
  (1 shorter events, 0.0 us)
Async XLA Ops:
  6.5 0.7 copy-start
  6.5 167.7 %reduce-scatter.2.cloned.1.call-start = ((), (), s32[]{:S(2)}) async-start(), calls=%async_computation.4 | async-start | bytes 20971520 | tf_op jit(solution)/shard_map/reduce_scatter | solution.py:19
  184.2 7.5 %copy-start.2 = (bf16[8,64,2048]{2,1,0:T(8,128)(2,1)S(1)}, bf16[8,64,2048]{2,1,0:T(8,128)(2,1)}, u32[]{:S(2)}) copy-start(bf16[8,64,2048]{2,1,0:T(8,128)(2,1)} %get-tuple-element.8) | copy-start | bytes 6291460
  184.2 35.0 %all-to-all-start = ((bf16[32,1,1,1,64,1,512]{6,4,5,3,2,1,0:T(8,128)(2,1)}), bf16[32,1,1,1,64,1,512]{6,4,5,3,2,1,0:T(8,128)(2,1)}, u32[]{:S(2)}, u32[]{:S(2)}) async-start(bf16[32,1,1,1,64,1,512]{6,4,5,3,2,1,0:T(8,128)(2,1)} %bitcast.5), calls=%async_computation.1 | async-start | bytes 4194304 | tf_op jit(solution)/shard_map/all_to_all | solution.py:40
  305.8 1.6 copy-start.3
  305.8 4.1 %copy-start.1 = (s32[1,8,32,1]{2,3,1,0:T(1,128)S(1)}, s32[1,8,32,1]{2,3,1,0:T(1,128)}, u32[]{:S(2)}) copy-start(s32[1,8,32,1]{2,3,1,0:T(1,128)} %param.8) | copy-start | bytes 3076
Sparse Core Ops, SparseCore 0:
  23.8 150.3 reduce-scatter.1
where the time goes:
time: 317 us
  waiting for transfers between devices  173 us (55%)
  blocking collectives  84 us (26%)
  other arithmetic  21.1 us (7%)
  local copies, waits for them, and re-layouts  17.6 us (6%)
  between operations  13.5 us (4%)
  starting transfers between devices  7.51 us (2%)
    reduce_scatter x1, waiting for transfers between devices, sent_together(): lax.psum_scatter(both, axis, scatter_dimension=dim, tiled=True)  151 us
    all_to_all x1, blocking collectives, side_by_side(): lax.all_to_all(both, axis, split_axis=split_dim, concat_axis=concat_dim,...  51 us
    all_to_all x1, blocking collectives, one_exchange(): lax.all_to_all(blocks, axis, split_axis=0, concat_axis=0, tiled=True)  33 us
    all_to_all x1, waiting for transfers between devices, one_exchange(): lax.all_to_all(blocks, axis, split_axis=0, concat_axis=0, tiled=True)  22.6 us
    convert_element_type x1, other arithmetic, masked_terms(): (fisher_now * weight_tiles.astype(jnp.float32)).astype(jnp.bfloat16)  8.53 us
    all_to_all x1, starting transfers between devices, one_exchange(): lax.all_to_all(blocks, axis, split_axis=0, concat_axis=0, tiled=True)  7.51 us
    concatenate x1, other arithmetic, sent_together(): both = jnp.concatenate(arrays, axis=along)  6.6 us
  transfers between devices with their start and end apart: 2, of which 2 were waited for; matrix products, arithmetic and copies ran while one was open for 2% of the time, Pallas kernels for 0%

commit v1 on v0

v1 whole, which is shorter than its diff:
```python
import functools

import jax
import jax.numpy as jnp
from jax import lax
from jax.experimental import pallas as pl
from jax.experimental.pallas import tpu as pltpu
from jax.sharding import Mesh, PartitionSpec as P

TILE = 128
PRIOR_WEIGHT = 0.5
CHUNKS = (32, 32, 32, 32)
ANY = pl.BlockSpec(memory_space=pl.ANY)
SMEM = pl.BlockSpec(memory_space=pltpu.SMEM)


def run_all(copies):
    for c in copies:
        c.start()
    for c in copies:
        c.wait()


def pack_body(start, rows, blocks, code, weights, fisher, *rest):
    outs, sem = rest[:-1], rest[-1]
    n = len(outs)
    z = lax.axis_index("z")
    block = (z * 2 + lax.axis_index("core")) * lax.axis_size("shard") + lax.axis_index("shard")
    copies = []
    for d, out in enumerate(outs):
        for ec in range(2):
            e = lax.rem(z + d, n) * 2 + ec
            tile = jnp.maximum(code[e * blocks + block] - 1, 0)
            at = pl.ds(pl.multiple_of(tile * TILE + start, 16), rows)
            for a, src in enumerate((weights, fisher)):
                copies.append(
                    pltpu.make_async_copy(src.at[e, at], out.at[ec, a], sem.at[len(copies)])
                )
    run_all(copies)


def pack(code, weights, fisher, start, rows, n):
    blocks = code.shape[0] // weights.shape[0]
    cols = weights.shape[2]
    out = jax.ShapeDtypeStruct((2, 2, rows, cols), weights.dtype)
    return pl.pallas_call(
        functools.partial(pack_body, start, rows, blocks),
        out_shape=[out] * n,
        in_specs=[SMEM, ANY, ANY],
        out_specs=[ANY] * n,
        scratch_shapes=[pltpu.SemaphoreType.DMA((4 * n,))],
        name="pack",
    )(code, weights, fisher)


def order_body(*refs):
    n = len(refs) - 2
    out, sem = refs[n], refs[n + 1]
    z = lax.axis_index("z")
    copies = []
    for d in range(n):
        came = lax.rem(z + n - d, n)
        for ec in range(2):
            copies.append(
                pltpu.make_async_copy(refs[d].at[ec], out.at[ec * n + came], sem.at[len(copies)])
            )
    run_all(copies)


def order(pieces):
    n = len(pieces)
    p = pieces[0]
    return pl.pallas_call(
        order_body,
        out_shape=jax.ShapeDtypeStruct((2 * n, *p.shape[1:]), p.dtype),
        in_specs=[ANY] * n,
        out_specs=ANY,
        scratch_shapes=[pltpu.SemaphoreType.DMA((2 * n,))],
        name="order",
    )(*pieces)


def merge_body(blocks, code, got, base, *outs):
    n = len(outs)
    experts = code.shape[0] // (blocks * got.shape[1])
    tasks = got.shape[1]
    rows, cols = outs[0].shape[2:]
    x = lax.axis_index("shard")
    e = lax.axis_index("z") * 2 + lax.axis_index("core")
    block = (lax.axis_index("task") * 2 + pl.program_id(0)) * n + x
    codes = [code[(t * experts + e) * blocks + block] for t in range(tasks)]
    keep = [[jnp.where(c == j + 1, 1.0, 0.0).astype(jnp.float32) for j in range(2)] for c in codes]
    step = 16
    for d, out in enumerate(outs):
        column = lax.rem(x + d, n)
        at = pl.ds(pl.multiple_of(column * cols, cols), cols)
        for r in range(0, rows, step):
            num = [0.0, 0.0]
            den = [0.0, 0.0]
            for t in range(tasks):
                w = got[0, t, 0, pl.ds(r, step), at].astype(jnp.float32)
                f = got[0, t, 1, pl.ds(r, step), at].astype(jnp.float32)
                term = (f * w).astype(jnp.bfloat16).astype(jnp.float32)
                for j in range(2):
                    num[j] = num[j] + keep[t][j] * term
                    den[j] = den[j] + keep[t][j] * f
            for j in range(2):
                prior = base[column, 0, j, pl.ds(r, step), :].astype(jnp.float32)
                out[0, j, pl.ds(r, step), :] = (
                    (num[j] + PRIOR_WEIGHT * prior) / (den[j] + PRIOR_WEIGHT)
                ).astype(out.dtype)


def merge(code, got, base, start, blocks):
    _, tasks, _, rows, cols = got.shape
    n, _, _, _, piece = base.shape
    out = jax.ShapeDtypeStruct((2, 2, rows, piece), base.dtype)
    at = start // rows
    return pl.pallas_call(
        functools.partial(merge_body, blocks),
        out_shape=[out] * n,
        grid=(2,),
        in_specs=[
            SMEM,
            pl.BlockSpec((1, tasks, 2, rows, cols), lambda i: (i, 0, 0, 0, 0)),
            pl.BlockSpec((n, 1, 2, rows, piece), lambda i: (0, i, 0, at, 0)),
        ],
        out_specs=[pl.BlockSpec((1, 2, rows, piece), lambda i: (i, 0, 0, 0))] * n,
        name="merge",
    )(code, got, base)


def place_body(start, n, *refs):
    pieces, out, sem = refs[:n], refs[-2], refs[-1]
    rows = pieces[0].shape[2]
    x = lax.axis_index("shard")
    copies = []
    for d, piece in enumerate(pieces):
        came = lax.rem(x + n - d, n)
        for c in range(2):
            copies.append(
                pltpu.make_async_copy(
                    piece.at[c], out.at[c, came, :, pl.ds(start, rows)], sem.at[len(copies)]
                )
            )
    run_all(copies)


def place(pieces, whole, start):
    n = len(pieces)
    piece = pieces[0].shape[3]
    shape = jax.ShapeDtypeStruct((2, n, 2, TILE, piece), pieces[0].dtype)
    more = [] if whole is None else [whole]
    return pl.pallas_call(
        functools.partial(place_body, start, n),
        out_shape=shape,
        in_specs=[ANY] * (n + len(more)),
        out_specs=ANY,
        scratch_shapes=[pltpu.SemaphoreType.DMA((2 * n,))],
        input_output_aliases={n: 0} if more else {},
        name="place",
    )(*pieces, *more)


def shifted(x, axis, by):
    n = lax.axis_size(axis)
    return lax.ppermute(x, axis, [(i, (i + by) % n) for i in range(n)])


def local(weights, fisher, base_weights, tile_list, tile_count):
    weights, fisher = weights[0], fisher[0]
    nz, nx = lax.axis_size("z"), lax.axis_size("shard")
    blocks = tile_list.shape[2]
    cols = base_weights.shape[2]
    own = jnp.where(tile_count[0] > 0, tile_list[0, :, :, 0] + 1, 0).reshape(-1)
    base = jnp.swapaxes(base_weights.reshape(2, nx, 2 * TILE, cols), 0, 1)
    base = lax.all_to_all(base, "shard", 0, 0, tiled=True).reshape(nx, 2, 2, TILE, cols)
    codes = lax.all_gather(own, "task", axis=0, tiled=True)
    whole = None
    start = 0
    for rows in CHUNKS:
        packed = pack(own, weights, fisher, start, rows, nz)
        pieces = [packed[0]] + [shifted(packed[d], "z", d) for d in range(1, nz)]
        ready = order(pieces)
        got = lax.all_to_all(ready, ("core", "task"), 0, 0, tiled=True)
        got = got.reshape(2, -1, *got.shape[1:])
        merged = merge(codes, got, base, start, blocks)
        back = [merged[0]] + [shifted(merged[d], "shard", d) for d in range(1, nx)]
        whole = place(back, whole, start)
        start += rows
    return whole.reshape(base_weights.shape)


def solution(mesh):
    split = Mesh(
        mesh.devices.reshape(mesh.devices.shape[0] // 2, 2, *mesh.devices.shape[1:]),
        ("z", "core", "task", "shard"),
    )
    rows = ("z", "core")
    in_specs = (
        P("task", None, ("z", "core", "shard"), None),
        P("task", None, ("z", "core", "shard"), None),
        P(rows, "task", "shard"),
        P("task", None, None, None),
        P("task", None, None),
    )
    return jax.shard_map(
        local, mesh=split, in_specs=in_specs, out_specs=P(rows, "task", "shard"), check_vma=False
    )
```

time: 317 us -> 797 us (2.51)
  Pallas kernels: 0 us -> 601 us
  waiting for transfers between devices: 173 us -> 93.2 us
  blocking collectives: 84 us -> 29.8 us
  starting transfers between devices: 7.51 us -> 58.9 us
  other arithmetic: 21.1 us -> 0.61 us
  between operations: 13.5 us -> 0.36 us
    pallas_call x0 -> x16, Pallas kernels: none -> 601 us  [the longest x4 262 us: pack(): pl.pallas_call(functools.partial(pack_body, start, rows, blocks), out_sha...]
    reduce_scatter x1 -> x0, waiting for transfers between devices: 151 us -> none  [sent_together(): lax.psum_scatter(both, axis, scatter_dimension=dim, tiled=True)]
    ppermute x0 -> x24, waiting for transfers between devices: none -> 93.2 us  [shifted(): return lax.ppermute(x, axis, [(i, (i + by) % n) for i in range(n)])]
    all_to_all x2 -> x0, blocking collectives: 84 us -> none  [the longest x1 51 us: side_by_side(): lax.all_to_all(both, axis, split_axis=split_dim, concat_axis=concat_dim,...]
    ppermute x0 -> x24, starting transfers between devices: none -> 36.6 us  [shifted(): return lax.ppermute(x, axis, [(i, (i + by) % n) for i in range(n)])]
    all_gather x0 -> x1, blocking collectives: none -> 29.8 us  [local(): codes = lax.all_gather(own, 'task', axis=0, tiled=True)]
    all_to_all x1 -> x5, waiting for transfers between devices: 22.6 us -> 0.01 us  [the longest x4 0.01 us: local(): got = lax.all_to_all(ready, ('core', 'task'), 0, 0, tiled=True)]
    all_to_all x1 -> x5, starting transfers between devices: 7.51 us -> 22.3 us  [the longest x4 17.8 us: local(): got = lax.all_to_all(ready, ('core', 'task'), 0, 0, tiled=True)]
  transfers between devices with their start and end apart: 2 -> 29, of which waited for: 2 -> 9; matrix products, arithmetic and copies ran while one was open for 2% -> 0% of each run, Pallas kernels for 0% -> 73%
where the time goes in v1:
time: 797 us; the launch traced here: 796 us
  Pallas kernels  601 us (75%)
  waiting for transfers between devices  93.2 us (12%)
  starting transfers between devices  58.9 us (7%)
  blocking collectives  29.8 us (4%)
  local copies, waits for them, and re-layouts  11.9 us (1%)
    pallas_call x4, Pallas kernels, pack(): pl.pallas_call(functools.partial(pack_body, start, rows, blocks), out_sha...  262 us
    pallas_call x4, Pallas kernels, order(): pl.pallas_call(order_body, out_shape=jax.ShapeDtypeStruct((2 * n, *p.shap...  259 us
    ppermute x24, waiting for transfers between devices, shifted(): return lax.ppermute(x, axis, [(i, (i + by) % n) for i in range(n)])  93.2 us
    pallas_call x4, Pallas kernels, place(): pl.pallas_call(functools.partial(place_body, start, n), out_shape=shape,...  68.2 us
    ppermute x24, starting transfers between devices, shifted(): return lax.ppermute(x, axis, [(i, (i + by) % n) for i in range(n)])  36.6 us
    all_gather x1, blocking collectives, local(): codes = lax.all_gather(own, 'task', axis=0, tiled=True)  29.8 us
    all_to_all x4, starting transfers between devices, local(): got = lax.all_to_all(ready, ('core', 'task'), 0, 0, tiled=True)  17.8 us
  transfers between devices with their start and end apart: 29, of which 9 were waited for; matrix products, arithmetic and copies ran while one was open for 0% of the time, Pallas kernels for 73%

profile of v1, /device:TPU:0, one launch (start us, length us, event | category | flops | bytes accessed | tf_op | source)
XLA Modules:
  0.0 796.1 jit_solution(11301159589008199469)
XLA Ops:
  3.0 4.5 all-to-all-start.1
  8.3 65.5 %pack.5 = (bf16[2,2,32,2048]{3,2,1,0:T(8,128)(2,1)}, bf16[2,2,32,2048]{3,2,1,0:T(8,128)(2,1)}, bf16[2,2,32,2048]{3,2,1,0:T(8,128)(2,1)}, bf16[2,2,32,2048]{3,2,1,0:T(8,128)(2,1)}) custom-call(s32[256]{0:T(256)} %broadcast_select_fusion.code, bf16[8,256,2048]{2,1,0:T(8,128)(2,1)} %bitcast.14, bf16[8,256,2048]{2,1,0:T(8,128)(2,1)} %bitcast.18), custom_call_target="tpu_custom_call" | custom-call | tf_op jit(solution)/shard_map/pack/pallas_call | solution.py:46
  75.8 3.6 collective-permute-start.7
  80.4 9.7 %collective-permute-done.6.refs_1_ = bf16[2,2,32,2048]{3,2,1,0:T(8,128)(2,1)S(1)} collective-permute-done((bf16[2,2,32,2048]{3,2,1,0:T(8,128)(2,1)}, bf16[2,2,32,2048]{3,2,1,0:T(8,128)(2,1)S(1)}, u32[]{:S(2)}, u32[]{:S(2)}) %collective-permute-start.6) | collective-permute-done | bytes 524320 | tf_op jit(solution)/shard_map/ppermute | solution.py:167
  90.1 12.1 %collective-permute-done.7.refs_2_ = bf16[2,2,32,2048]{3,2,1,0:T(8,128)(2,1)S(1)} collective-permute-done((bf16[2,2,32,2048]{3,2,1,0:T(8,128)(2,1)}, bf16[2,2,32,2048]{3,2,1,0:T(8,128)(2,1)S(1)}, u32[]{:S(2)}, u32[]{:S(2)}) %collective-permute-start.7) | collective-permute-done | bytes 524320 | tf_op jit(solution)/shard_map/ppermute | solution.py:167
  103.0 64.7 %order.5 = bf16[8,2,32,2048]{3,2,1,0:T(8,128)(2,1)} custom-call(bf16[2,2,32,2048]{3,2,1,0:T(8,128)(2,1)} %get-tuple-element.45.refs_0_, bf16[2,2,32,2048]{3,2,1,0:T(8,128)(2,1)} %copy-done.3, bf16[2,2,32,2048]{3,2,1,0:T(8,128)(2,1)} %copy-done.7, bf16[2,2,32,2048]{3,2,1,0:T(8,128)(2,1)} %collective-permute-done.8.refs_3_), custom_call_target="tpu_custom_call" | custom-call | tf_op jit(solution)/shard_map/order/pallas_call | solution.py:73
  169.1 4.5 all-to-all-start.2
  173.5 65.5 %pack.6 = (bf16[2,2,32,2048]{3,2,1,0:T(8,128)(2,1)}, bf16[2,2,32,2048]{3,2,1,0:T(8,128)(2,1)}, bf16[2,2,32,2048]{3,2,1,0:T(8,128)(2,1)}, bf16[2,2,32,2048]{3,2,1,0:T(8,128)(2,1)}) custom-call(s32[256]{0:T(256)} %broadcast_select_fusion.code, bf16[8,256,2048]{2,1,0:T(8,128)(2,1)} %bitcast.15, bf16[8,256,2048]{2,1,0:T(8,128)(2,1)} %bitcast.19), custom_call_target="tpu_custom_call" | custom-call | tf_op jit(solution)/shard_map/pack/pallas_call | solution.py:46
  243.3 22.8 %collective-permute-done.12.refs_1_ = bf16[2,2,32,2048]{3,2,1,0:T(8,128)(2,1)S(1)} collective-permute-done((bf16[2,2,32,2048]{3,2,1,0:T(8,128)(2,1)}, bf16[2,2,32,2048]{3,2,1,0:T(8,128)(2,1)S(1)}, u32[]{:S(2)}, u32[]{:S(2)}) %collective-permute-start.12) | collective-permute-done | bytes 524320 | tf_op jit(solution)/shard_map/ppermute | solution.py:167
  267.5 64.7 %order.6 = bf16[8,2,32,2048]{3,2,1,0:T(8,128)(2,1)} custom-call(bf16[2,2,32,2048]{3,2,1,0:T(8,128)(2,1)} %get-tuple-element.53.refs_0_, bf16[2,2,32,2048]{3,2,1,0:T(8,128)(2,1)} %copy-done.4, bf16[2,2,32,2048]{3,2,1,0:T(8,128)(2,1)} %copy-done.8, bf16[2,2,32,2048]{3,2,1,0:T(8,128)(2,1)} %copy-done.11), custom_call_target="tpu_custom_call" | custom-call | tf_op jit(solution)/shard_map/order/pallas_call | solution.py:73
  332.3 4.5 all-to-all-start.3
  336.7 65.5 %pack.7 = (bf16[2,2,32,2048]{3,2,1,0:T(8,128)(2,1)}, bf16[2,2,32,2048]{3,2,1,0:T(8,128)(2,1)}, bf16[2,2,32,2048]{3,2,1,0:T(8,128)(2,1)}, bf16[2,2,32,2048]{3,2,1,0:T(8,128)(2,1)}) custom-call(s32[256]{0:T(256)} %broadcast_select_fusion.code, bf16[8,256,2048]{2,1,0:T(8,128)(2,1)} %bitcast.16, bf16[8,256,2048]{2,1,0:T(8,128)(2,1)} %bitcast.20), custom_call_target="tpu_custom_call" | custom-call | tf_op jit(solution)/shard_map/pack/pallas_call | solution.py:46
  403.2 3.2 collective-permute-start.19
  406.5 11.6 %collective-permute-done.18.refs_1_ = bf16[2,2,32,2048]{3,2,1,0:T(8,128)(2,1)S(1)} collective-permute-done((bf16[2,2,32,2048]{3,2,1,0:T(8,128)(2,1)}, bf16[2,2,32,2048]{3,2,1,0:T(8,128)(2,1)S(1)}, u32[]{:S(2)}, u32[]{:S(2)}) %collective-permute-start.18) | collective-permute-done | bytes 524320 | tf_op jit(solution)/shard_map/ppermute | solution.py:167
  418.0 12.1 %collective-permute-done.19.refs_2_ = bf16[2,2,32,2048]{3,2,1,0:T(8,128)(2,1)S(1)} collective-permute-done((bf16[2,2,32,2048]{3,2,1,0:T(8,128)(2,1)}, bf16[2,2,32,2048]{3,2,1,0:T(8,128)(2,1)S(1)}, u32[]{:S(2)}, u32[]{:S(2)}) %collective-permute-start.19) | collective-permute-done | bytes 524320 | tf_op jit(solution)/shard_map/ppermute | solution.py:167
  430.9 64.7 %order.7 = bf16[8,2,32,2048]{3,2,1,0:T(8,128)(2,1)} custom-call(bf16[2,2,32,2048]{3,2,1,0:T(8,128)(2,1)} %get-tuple-element.61.refs_0_, bf16[2,2,32,2048]{3,2,1,0:T(8,128)(2,1)} %copy-done.5, bf16[2,2,32,2048]{3,2,1,0:T(8,128)(2,1)} %copy-done.9, bf16[2,2,32,2048]{3,2,1,0:T(8,128)(2,1)} %collective-permute-done.20.refs_3_), custom_call_target="tpu_custom_call" | custom-call | tf_op jit(solution)/shard_map/order/pallas_call | solution.py:73
  497.0 4.4 all-to-all-start.4
  501.4 65.5 %pack.4 = (bf16[2,2,32,2048]{3,2,1,0:T(8,128)(2,1)}, bf16[2,2,32,2048]{3,2,1,0:T(8,128)(2,1)}, bf16[2,2,32,2048]{3,2,1,0:T(8,128)(2,1)}, bf16[2,2,32,2048]{3,2,1,0:T(8,128)(2,1)}) custom-call(s32[256]{0:T(256)} %broadcast_select_fusion.code, bf16[8,256,2048]{2,1,0:T(8,128)(2,1)} %bitcast.17, bf16[8,256,2048]{2,1,0:T(8,128)(2,1)} %bitcast.21), custom_call_target="tpu_custom_call" | custom-call | tf_op jit(solution)/shard_map/pack/pallas_call | solution.py:46
  567.0 3.2 collective-permute-start.1
  570.3 12.9 %collective-permute-done.refs_1_ = bf16[2,2,32,2048]{3,2,1,0:T(8,128)(2,1)S(1)} collective-permute-done((bf16[2,2,32,2048]{3,2,1,0:T(8,128)(2,1)}, bf16[2,2,32,2048]{3,2,1,0:T(8,128)(2,1)S(1)}, u32[]{:S(2)}, u32[]{:S(2)}) %collective-permute-start) | collective-permute-done | bytes 524320 | tf_op jit(solution)/shard_map/ppermute | solution.py:167
  583.2 10.8 %collective-permute-done.1.refs_2_ = bf16[2,2,32,2048]{3,2,1,0:T(8,128)(2,1)S(1)} collective-permute-done((bf16[2,2,32,2048]{3,2,1,0:T(8,128)(2,1)}, bf16[2,2,32,2048]{3,2,1,0:T(8,128)(2,1)S(1)}, u32[]{:S(2)}, u32[]{:S(2)}) %collective-permute-start.1) | collective-permute-done | bytes 524320 | tf_op jit(solution)/shard_map/ppermute | solution.py:167
  595.4 64.7 %order.4 = bf16[8,2,32,2048]{3,2,1,0:T(8,128)(2,1)} custom-call(bf16[2,2,32,2048]{3,2,1,0:T(8,128)(2,1)} %get-tuple-element.37.refs_0_, bf16[2,2,32,2048]{3,2,1,0:T(8,128)(2,1)} %copy-done.6, bf16[2,2,32,2048]{3,2,1,0:T(8,128)(2,1)} %copy-done.10, bf16[2,2,32,2048]{3,2,1,0:T(8,128)(2,1)} %copy-done.12), custom_call_target="tpu_custom_call" | custom-call | tf_op jit(solution)/shard_map/order/pallas_call | solution.py:73
  660.2 4.5 all-to-all-start
  664.6 29.8 %all-gather = s32[4,1,256]{2,1,0:T(1,128)} all-gather(s32[1,1,256]{2,1,0:T(1,128)S(1)} %bitcast.34), channel_id=1, replica_groups=mesh['z'=4,'core'=2,'task'=4,'shard'=4] {'task'}, dimensions={0}, use_global_device_ids=true | all-gather | bytes 5120 | tf_op jit(solution)/shard_map/all_gather | solution.py:178
  694.4 3.1 merge.5
  699.3 3.1 merge.6
  707.6 3.1 merge.7
  715.5 3.1 merge.4
  726.4 17.1 %place.4.refs_4_ = bf16[2,4,2,128,512]{4,3,2,1,0:T(8,128)(2,1)} custom-call(bf16[2,2,32,512]{3,2,1,0:T(8,128)(2,1)} %get-tuple-element.65.refs_0_, bf16[2,2,32,512]{3,2,1,0:T(8,128)(2,1)} %copy-done.18, bf16[2,2,32,512]{3,2,1,0:T(8,128)(2,1)} %copy-done.19, bf16[2,2,32,512]{3,2,1,0:T(8,128)(2,1)} %copy-done.20), custom_call_target="tpu_custom_call" | custom-call | tf_op jit(solution)/shard_map/place/pallas_call | solution.py:154
  743.4 17.1 %place.5.refs_4_ = bf16[2,4,2,128,512]{4,3,2,1,0:T(8,128)(2,1)} custom-call(bf16[2,2,32,512]{3,2,1,0:T(8,128)(2,1)} %get-tuple-element.57.refs_0_, bf16[2,2,32,512]{3,2,1,0:T(8,128)(2,1)} %copy-done.14, bf16[2,2,32,512]{3,2,1,0:T(8,128)(2,1)} %copy-done.15, bf16[2,2,32,512]{3,2,1,0:T(8,128)(2,1)} %copy-done.16, ...), custom_call_target="tpu_custom_call", output_to_operand_aliasing={{}: (4, {})} | custom-call | tf_op jit(solution)/shard_map/place/pallas_call | solution.py:154
  761.2 17.1 %place.6.refs_4_ = bf16[2,4,2,128,512]{4,3,2,1,0:T(8,128)(2,1)} custom-call(bf16[2,2,32,512]{3,2,1,0:T(8,128)(2,1)} %get-tuple-element.49.refs_0_, bf16[2,2,32,512]{3,2,1,0:T(8,128)(2,1)} %copy-done.13, bf16[2,2,32,512]{3,2,1,0:T(8,128)(2,1)} %copy-done.22, bf16[2,2,32,512]{3,2,1,0:T(8,128)(2,1)} %copy-done.24, ...), custom_call_target="tpu_custom_call", output_to_operand_aliasing={{}: (4, {})} | custom-call | tf_op jit(solution)/shard_map/place/pallas_call | solution.py:154
  779.1 17.1 %place.7 = bf16[2,4,2,128,512]{4,3,2,1,0:T(8,128)(2,1)} custom-call(bf16[2,2,32,512]{3,2,1,0:T(8,128)(2,1)} %get-tuple-element.41.refs_0_, bf16[2,2,32,512]{3,2,1,0:T(8,128)(2,1)} %copy-done.17, bf16[2,2,32,512]{3,2,1,0:T(8,128)(2,1)} %copy-done.21, bf16[2,2,32,512]{3,2,1,0:T(8,128)(2,1)} %copy-done.23, ...), custom_call_target="tpu_custom_call", output_to_operand_aliasing={{}: (4, {})} | custom-call | tf_op jit(solution)/shard_map/place/pallas_call | solution.py:154
  (109 shorter events, 40.4 us)
Async XLA Ops:
  3.0 164.7 %all-to-all-start.1 = ((bf16[4,2,256,512]{3,2,1,0:T(8,128)(2,1)}), bf16[4,2,256,512]{3,2,1,0:T(8,128)(2,1)S(1)}, u32[]{:S(2)}, u32[]{:S(2)}) async-start(bf16[4,2,256,512]{3,2,1,0:T(8,128)(2,1)} %bitcast.28), calls=%async_computation.1 | async-start | bytes 4194304 | tf_op jit(solution)/shard_map/all_to_all | solution.py:177
  73.8 16.2 %collective-permute-start.6 = (bf16[2,2,32,2048]{3,2,1,0:T(8,128)(2,1)}, bf16[2,2,32,2048]{3,2,1,0:T(8,128)(2,1)S(1)}, u32[]{:S(2)}, u32[]{:S(2)}) collective-permute-start(bf16[2,2,32,2048]{3,2,1,0:T(8,128)(2,1)} %get-tuple-element.46), channel_id=1, source_target_pairs={{0,32},{32,64},{64,96},{96,0},{1,33},{33,65},{65,97},{97,1},{2,34}... | collective-permute-start | bytes 1572872 | tf_op jit(solution)/shard_map/ppermute | solution.py:167
  75.8 26.4 %collective-permute-start.7 = (bf16[2,2,32,2048]{3,2,1,0:T(8,128)(2,1)}, bf16[2,2,32,2048]{3,2,1,0:T(8,128)(2,1)S(1)}, u32[]{:S(2)}, u32[]{:S(2)}) collective-permute-start(bf16[2,2,32,2048]{3,2,1,0:T(8,128)(2,1)} %get-tuple-element.47), channel_id=1, source_target_pairs={{0,64},{32,96},{64,0},{96,32},{1,65},{33,97},{65,1},{97,33},{2,66}... | collective-permute-start | bytes 1572872 | tf_op jit(solution)/shard_map/ppermute | solution.py:167
  79.4 22.8 %collective-permute-start.8 = (bf16[2,2,32,2048]{3,2,1,0:T(8,128)(2,1)}, bf16[2,2,32,2048]{3,2,1,0:T(8,128)(2,1)}, u32[]{:S(2)}, u32[]{:S(2)}) collective-permute-start(bf16[2,2,32,2048]{3,2,1,0:T(8,128)(2,1)} %get-tuple-element.48), channel_id=1, source_target_pairs={{0,96},{32,0},{64,32},{96,64},{1,97},{33,1},{65,33},{97,65},{2,98}... | collective-permute-start | bytes 1572872 | tf_op jit(solution)/shard_map/ppermute | solution.py:167
  169.1 163.2 %all-to-all-start.2 = ((bf16[8,2,32,2048]{3,2,1,0:T(8,128)(2,1)}), bf16[8,2,32,2048]{3,2,1,0:T(8,128)(2,1)}, u32[]{:S(2)}, u32[]{:S(2)}) async-start(bf16[8,2,32,2048]{3,2,1,0:T(8,128)(2,1)} %order.5), calls=%async_computation.2 | async-start | bytes 4194304 | tf_op jit(solution)/shard_map/all_to_all | solution.py:185
  239.0 27.1 %collective-permute-start.12 = (bf16[2,2,32,2048]{3,2,1,0:T(8,128)(2,1)}, bf16[2,2,32,2048]{3,2,1,0:T(8,128)(2,1)S(1)}, u32[]{:S(2)}, u32[]{:S(2)}) collective-permute-start(bf16[2,2,32,2048]{3,2,1,0:T(8,128)(2,1)} %get-tuple-element.54), channel_id=1, source_target_pairs={{0,32},{32,64},{64,96},{96,0},{1,33},{33,65},{65,97},{97,1},{2,34}... | collective-permute-start | bytes 1572872 | tf_op jit(solution)/shard_map/ppermute | solution.py:167
  239.6 26.4 %collective-permute-start.13 = (bf16[2,2,32,2048]{3,2,1,0:T(8,128)(2,1)}, bf16[2,2,32,2048]{3,2,1,0:T(8,128)(2,1)S(1)}, u32[]{:S(2)}, u32[]{:S(2)}) collective-permute-start(bf16[2,2,32,2048]{3,2,1,0:T(8,128)(2,1)} %get-tuple-element.55), channel_id=1, source_target_pairs={{0,64},{32,96},{64,0},{96,32},{1,65},{33,97},{65,1},{97,33},{2,66}... | collective-permute-start | bytes 1572872 | tf_op jit(solution)/shard_map/ppermute | solution.py:167
  242.0 24.7 %collective-permute-start.14 = (bf16[2,2,32,2048]{3,2,1,0:T(8,128)(2,1)}, bf16[2,2,32,2048]{3,2,1,0:T(8,128)(2,1)S(1)}, u32[]{:S(2)}, u32[]{:S(2)}) collective-permute-start(bf16[2,2,32,2048]{3,2,1,0:T(8,128)(2,1)} %get-tuple-element.56), channel_id=1, source_target_pairs={{0,96},{32,0},{64,32},{96,64},{1,97},{33,1},{65,33},{97,65},{2,98}... | collective-permute-start | bytes 1572872 | tf_op jit(solution)/shard_map/ppermute | solution.py:167
  332.3 163.3 %all-to-all-start.3 = ((bf16[8,2,32,2048]{3,2,1,0:T(8,128)(2,1)}), bf16[8,2,32,2048]{3,2,1,0:T(8,128)(2,1)S(1)}, u32[]{:S(2)}, u32[]{:S(2)}) async-start(bf16[8,2,32,2048]{3,2,1,0:T(8,128)(2,1)} %order.6), calls=%async_computation.3 | async-start | bytes 4194304 | tf_op jit(solution)/shard_map/all_to_all | solution.py:185
  402.2 15.8 %collective-permute-start.18 = (bf16[2,2,32,2048]{3,2,1,0:T(8,128)(2,1)}, bf16[2,2,32,2048]{3,2,1,0:T(8,128)(2,1)S(1)}, u32[]{:S(2)}, u32[]{:S(2)}) collective-permute-start(bf16[2,2,32,2048]{3,2,1,0:T(8,128)(2,1)} %get-tuple-element.62), channel_id=1, source_target_pairs={{0,32},{32,64},{64,96},{96,0},{1,33},{33,65},{65,97},{97,1},{2,34}... | collective-permute-start | bytes 1572872 | tf_op jit(solution)/shard_map/ppermute | solution.py:167
  403.2 26.9 %collective-permute-start.19 = (bf16[2,2,32,2048]{3,2,1,0:T(8,128)(2,1)}, bf16[2,2,32,2048]{3,2,1,0:T(8,128)(2,1)S(1)}, u32[]{:S(2)}, u32[]{:S(2)}) collective-permute-start(bf16[2,2,32,2048]{3,2,1,0:T(8,128)(2,1)} %get-tuple-element.63), channel_id=1, source_target_pairs={{0,64},{32,96},{64,0},{96,32},{1,65},{33,97},{65,1},{97,33},{2,66}... | collective-permute-start | bytes 1572872 | tf_op jit(solution)/shard_map/ppermute | solution.py:167
  406.4 23.8 %collective-permute-start.20 = (bf16[2,2,32,2048]{3,2,1,0:T(8,128)(2,1)}, bf16[2,2,32,2048]{3,2,1,0:T(8,128)(2,1)}, u32[]{:S(2)}, u32[]{:S(2)}) collective-permute-start(bf16[2,2,32,2048]{3,2,1,0:T(8,128)(2,1)} %get-tuple-element.64), channel_id=1, source_target_pairs={{0,96},{32,0},{64,32},{96,64},{1,97},{33,1},{65,33},{97,65},{2,98}... | collective-permute-start | bytes 1572872 | tf_op jit(solution)/shard_map/ppermute | solution.py:167
  497.0 163.2 %all-to-all-start.4 = ((bf16[8,2,32,2048]{3,2,1,0:T(8,128)(2,1)}), bf16[8,2,32,2048]{3,2,1,0:T(8,128)(2,1)}, u32[]{:S(2)}, u32[]{:S(2)}) async-start(bf16[8,2,32,2048]{3,2,1,0:T(8,128)(2,1)} %order.7), calls=%async_computation.4 | async-start | bytes 4194304 | tf_op jit(solution)/shard_map/all_to_all | solution.py:185
  566.9 16.2 %collective-permute-start = (bf16[2,2,32,2048]{3,2,1,0:T(8,128)(2,1)}, bf16[2,2,32,2048]{3,2,1,0:T(8,128)(2,1)S(1)}, u32[]{:S(2)}, u32[]{:S(2)}) collective-permute-start(bf16[2,2,32,2048]{3,2,1,0:T(8,128)(2,1)} %get-tuple-element.38), channel_id=1, source_target_pairs={{0,32},{32,64},{64,96},{96,0},{1,33},{33,65},{65,97},{97,1},{2,34}... | collective-permute-start | bytes 1572872 | tf_op jit(solution)/shard_map/ppermute | solution.py:167
  567.0 27.0 %collective-permute-start.1 = (bf16[2,2,32,2048]{3,2,1,0:T(8,128)(2,1)}, bf16[2,2,32,2048]{3,2,1,0:T(8,128)(2,1)S(1)}, u32[]{:S(2)}, u32[]{:S(2)}) collective-permute-start(bf16[2,2,32,2048]{3,2,1,0:T(8,128)(2,1)} %get-tuple-element.39), channel_id=1, source_target_pairs={{0,64},{32,96},{64,0},{96,32},{1,65},{33,97},{65,1},{97,33},{2,66}... | collective-permute-start | bytes 1572872 | tf_op jit(solution)/shard_map/ppermute | solution.py:167
  570.2 24.4 %collective-permute-start.2 = (bf16[2,2,32,2048]{3,2,1,0:T(8,128)(2,1)}, bf16[2,2,32,2048]{3,2,1,0:T(8,128)(2,1)S(1)}, u32[]{:S(2)}, u32[]{:S(2)}) collective-permute-start(bf16[2,2,32,2048]{3,2,1,0:T(8,128)(2,1)} %get-tuple-element.40), channel_id=1, source_target_pairs={{0,96},{32,0},{64,32},{96,64},{1,97},{33,1},{65,33},{97,65},{2,98}... | collective-permute-start | bytes 1572872 | tf_op jit(solution)/shard_map/ppermute | solution.py:167
  660.2 54.0 %all-to-all-start = ((bf16[8,2,32,2048]{3,2,1,0:T(8,128)(2,1)}), bf16[8,2,32,2048]{3,2,1,0:T(8,128)(2,1)S(1)}, u32[]{:S(2)}, u32[]{:S(2)}) async-start(bf16[8,2,32,2048]{3,2,1,0:T(8,128)(2,1)} %order.4), calls=%async_computation | async-start | bytes 4194304 | tf_op jit(solution)/shard_map/all_to_all | solution.py:185
  697.5 13.2 %collective-permute-start.9 = (bf16[2,2,32,512]{3,2,1,0:T(8,128)(2,1)}, bf16[2,2,32,512]{3,2,1,0:T(8,128)(2,1)S(1)}, u32[]{:S(2)}, u32[]{:S(2)}) collective-permute-start(bf16[2,2,32,512]{3,2,1,0:T(8,128)(2,1)} %get-tuple-element.50), channel_id=1, source_target_pairs={{0,1},{1,2},{2,3},{3,0},{4,5},{5,6},{6,7},{7,4},{8,9},{9,10},{10,1... | collective-permute-start | bytes 393224 | tf_op jit(solution)/shard_map/ppermute | solution.py:167
  702.3 10.1 %collective-permute-start.15 = (bf16[2,2,32,512]{3,2,1,0:T(8,128)(2,1)}, bf16[2,2,32,512]{3,2,1,0:T(8,128)(2,1)S(1)}, u32[]{:S(2)}, u32[]{:S(2)}) collective-permute-start(bf16[2,2,32,512]{3,2,1,0:T(8,128)(2,1)} %get-tuple-element.58), channel_id=1, source_target_pairs={{0,1},{1,2},{2,3},{3,0},{4,5},{5,6},{6,7},{7,4},{8,9},{9,10},{10,1... | collective-permute-start | bytes 393224 | tf_op jit(solution)/shard_map/ppermute | solution.py:167
  703.8 14.9 %collective-permute-start.16 = (bf16[2,2,32,512]{3,2,1,0:T(8,128)(2,1)}, bf16[2,2,32,512]{3,2,1,0:T(8,128)(2,1)S(1)}, u32[]{:S(2)}, u32[]{:S(2)}) collective-permute-start(bf16[2,2,32,512]{3,2,1,0:T(8,128)(2,1)} %get-tuple-element.59), channel_id=1, source_target_pairs={{0,2},{1,3},{2,0},{3,1},{4,6},{5,7},{6,4},{7,5},{8,10},{9,11},{10,... | collective-permute-start | bytes 393224 | tf_op jit(solution)/shard_map/ppermute | solution.py:167
  705.3 14.1 %collective-permute-start.17 = (bf16[2,2,32,512]{3,2,1,0:T(8,128)(2,1)}, bf16[2,2,32,512]{3,2,1,0:T(8,128)(2,1)S(1)}, u32[]{:S(2)}, u32[]{:S(2)}) collective-permute-start(bf16[2,2,32,512]{3,2,1,0:T(8,128)(2,1)} %get-tuple-element.60), channel_id=1, source_target_pairs={{0,3},{1,0},{2,1},{3,2},{4,7},{5,4},{6,5},{7,6},{8,11},{9,8},{10,9... | collective-permute-start | bytes 393224 | tf_op jit(solution)/shard_map/ppermute | solution.py:167
  710.7 10.8 %collective-permute-start.21 = (bf16[2,2,32,512]{3,2,1,0:T(8,128)(2,1)}, bf16[2,2,32,512]{3,2,1,0:T(8,128)(2,1)S(1)}, u32[]{:S(2)}, u32[]{:S(2)}) collective-permute-start(bf16[2,2,32,512]{3,2,1,0:T(8,128)(2,1)} %get-tuple-element.66), channel_id=1, source_target_pairs={{0,1},{1,2},{2,3},{3,0},{4,5},{5,6},{6,7},{7,4},{8,9},{9,10},{10,1... | collective-permute-start | bytes 393224 | tf_op jit(solution)/shard_map/ppermute | solution.py:167
  710.7 49.8 %copy-start.13 = (bf16[2,2,32,512]{3,2,1,0:T(8,128)(2,1)}, bf16[2,2,32,512]{3,2,1,0:T(8,128)(2,1)S(1)}, u32[]{:S(2)}) copy-start(bf16[2,2,32,512]{3,2,1,0:T(8,128)(2,1)S(1)} %collective-permute-done.9.refs_1_) | copy-start | bytes 393220
  710.7 13.5 %collective-permute-start.22 = (bf16[2,2,32,512]{3,2,1,0:T(8,128)(2,1)}, bf16[2,2,32,512]{3,2,1,0:T(8,128)(2,1)S(1)}, u32[]{:S(2)}, u32[]{:S(2)}) collective-permute-start(bf16[2,2,32,512]{3,2,1,0:T(8,128)(2,1)} %get-tuple-element.67), channel_id=1, source_target_pairs={{0,2},{1,3},{2,0},{3,1},{4,6},{5,7},{6,4},{7,5},{8,10},{9,11},{10,... | collective-permute-start | bytes 393224 | tf_op jit(solution)/shard_map/ppermute | solution.py:167
  712.4 31.0 %copy-start.14 = (bf16[2,2,32,512]{3,2,1,0:T(8,128)(2,1)}, bf16[2,2,32,512]{3,2,1,0:T(8,128)(2,1)S(1)}, u32[]{:S(2)}) copy-start(bf16[2,2,32,512]{3,2,1,0:T(8,128)(2,1)S(1)} %collective-permute-done.15.refs_1_) | copy-start | bytes 393220
  712.4 12.7 %collective-permute-start.23 = (bf16[2,2,32,512]{3,2,1,0:T(8,128)(2,1)}, bf16[2,2,32,512]{3,2,1,0:T(8,128)(2,1)S(1)}, u32[]{:S(2)}, u32[]{:S(2)}) collective-permute-start(bf16[2,2,32,512]{3,2,1,0:T(8,128)(2,1)} %get-tuple-element.68), channel_id=1, source_target_pairs={{0,3},{1,0},{2,1},{3,2},{4,7},{5,4},{6,5},{7,6},{8,11},{9,8},{10,9... | collective-permute-start | bytes 393224 | tf_op jit(solution)/shard_map/ppermute | solution.py:167
  718.7 24.7 %copy-start.15 = (bf16[2,2,32,512]{3,2,1,0:T(8,128)(2,1)}, bf16[2,2,32,512]{3,2,1,0:T(8,128)(2,1)S(1)}, u32[]{:S(2)}) copy-start(bf16[2,2,32,512]{3,2,1,0:T(8,128)(2,1)S(1)} %collective-permute-done.16.refs_2_) | copy-start | bytes 393220
  718.7 59.6 %collective-permute-start.3 = (bf16[2,2,32,512]{3,2,1,0:T(8,128)(2,1)}, bf16[2,2,32,512]{3,2,1,0:T(8,128)(2,1)S(1)}, u32[]{:S(2)}, u32[]{:S(2)}) collective-permute-start(bf16[2,2,32,512]{3,2,1,0:T(8,128)(2,1)} %get-tuple-element.42), channel_id=1, source_target_pairs={{0,1},{1,2},{2,3},{3,0},{4,5},{5,6},{6,7},{7,4},{8,9},{9,10},{10,1... | collective-permute-start | bytes 393224 | tf_op jit(solution)/shard_map/ppermute | solution.py:167
  719.4 41.1 %collective-permute-start.10 = (bf16[2,2,32,512]{3,2,1,0:T(8,128)(2,1)S(1)}, bf16[2,2,32,512]{3,2,1,0:T(8,128)(2,1)S(1)}, u32[]{:S(2)}, u32[]{:S(2)}) collective-permute-start(bf16[2,2,32,512]{3,2,1,0:T(8,128)(2,1)S(1)} %copy-done.29), channel_id=1, source_target_pairs={{0,2},{1,3},{2,0},{3,1},{4,6},{5,7},{6,4},{7,5},{8,10},{9,11},{10,... | collective-permute-start | bytes 393224 | tf_op jit(solution)/shard_map/ppermute | solution.py:167
  721.6 39.0 %collective-permute-start.11 = (bf16[2,2,32,512]{3,2,1,0:T(8,128)(2,1)S(1)}, bf16[2,2,32,512]{3,2,1,0:T(8,128)(2,1)S(1)}, u32[]{:S(2)}, u32[]{:S(2)}) collective-permute-start(bf16[2,2,32,512]{3,2,1,0:T(8,128)(2,1)S(1)} %copy-done.28), channel_id=1, source_target_pairs={{0,3},{1,0},{2,1},{3,2},{4,7},{5,4},{6,5},{7,6},{8,11},{9,8},{10,9... | collective-permute-start | bytes 393224 | tf_op jit(solution)/shard_map/ppermute | solution.py:167
  724.2 54.1 %collective-permute-start.4 = (bf16[2,2,32,512]{3,2,1,0:T(8,128)(2,1)}, bf16[2,2,32,512]{3,2,1,0:T(8,128)(2,1)S(1)}, u32[]{:S(2)}, u32[]{:S(2)}) collective-permute-start(bf16[2,2,32,512]{3,2,1,0:T(8,128)(2,1)} %get-tuple-element.43), channel_id=1, source_target_pairs={{0,2},{1,3},{2,0},{3,1},{4,6},{5,7},{6,4},{7,5},{8,10},{9,11},{10,... | collective-permute-start | bytes 393224 | tf_op jit(solution)/shard_map/ppermute | solution.py:167
  725.1 53.2 %collective-permute-start.5 = (bf16[2,2,32,512]{3,2,1,0:T(8,128)(2,1)}, bf16[2,2,32,512]{3,2,1,0:T(8,128)(2,1)S(1)}, u32[]{:S(2)}, u32[]{:S(2)}) collective-permute-start(bf16[2,2,32,512]{3,2,1,0:T(8,128)(2,1)} %get-tuple-element.44), channel_id=1, source_target_pairs={{0,3},{1,0},{2,1},{3,2},{4,7},{5,4},{6,5},{7,6},{8,11},{9,8},{10,9... | collective-permute-start | bytes 393224 | tf_op jit(solution)/shard_map/ppermute | solution.py:167
  (27 other events, 104.7 us)

commit v2 on v1

v2 whole, which is shorter than its diff:
```python
import functools

import jax
import jax.numpy as jnp
from jax import lax
from jax.experimental import pallas as pl
from jax.experimental.pallas import tpu as pltpu
from jax.sharding import Mesh, PartitionSpec as P

TILE = 128
PRIOR_WEIGHT = 0.5
LOW = 64
HINT = 400_000_000
GRANT = 16 << 20
MESH = ("z", "core", "task", "shard")
ANY = pl.BlockSpec(memory_space=pl.ANY)
HBM = pl.BlockSpec(memory_space=pltpu.HBM)
VMEM = pl.BlockSpec(memory_space=pltpu.VMEM)
SMEM = pl.BlockSpec(memory_space=pltpu.SMEM)
PARAMS = pltpu.CompilerParams(vmem_limit_bytes=GRANT)


def my_block():
    z, c, x = lax.axis_index("z"), lax.axis_index("core"), lax.axis_index("shard")
    return (z * 2 + c) * lax.axis_size("shard") + x


def copy_signed(items, held, sem):
    copies = [
        (
            pltpu.make_async_copy(src, held.at[i], sem.at[i]),
            pltpu.make_async_copy(held.at[i], dst, sem.at[i]),
            sign,
        )
        for i, (src, dst, sign) in enumerate(items)
    ]
    for read, _, _ in copies:
        read.start()
    for i, (read, write, sign) in enumerate(copies):
        read.wait()
        if sign is not None:
            held[i] = held[i] * sign
        write.start()
    for _, write, _ in copies:
        write.wait()


def listed(tiles, counts, e):
    tile = jnp.minimum(jnp.maximum(tiles[e, my_block()], 0), 1)
    sign = jnp.where(counts[e, my_block()] > 0, jnp.where(tile == 0, 1.0, -1.0), 0.0)
    return tile * TILE, sign.astype(jnp.bfloat16)


def pack_low_body(tiles, counts, weights, fisher, out, token, held, sem):
    token[0] = 0
    n, _, _, rows, _ = out.shape
    y = lax.axis_index("task")
    items = []
    for j in range(n):
        for ec in range(2):
            e = lax.rem(y + j, n) * 2 + ec
            row, sign = listed(tiles, counts, e)
            at = pl.ds(pl.multiple_of(row, TILE), rows)
            items.append((weights.at[e, at], out.at[j, ec, 0], None))
            items.append((fisher.at[e, at], out.at[j, ec, 1], sign))
    copy_signed(items, held, sem)


def pack_low(tiles, counts, weights, fisher, n):
    cols = weights.shape[2]
    return pl.pallas_call(
        pack_low_body,
        out_shape=[
            jax.ShapeDtypeStruct((n, 2, 2, LOW, cols), weights.dtype),
            jax.ShapeDtypeStruct((1,), jnp.int32),
        ],
        in_specs=[SMEM, SMEM, HBM, HBM],
        out_specs=[HBM, SMEM],
        scratch_shapes=[
            pltpu.VMEM((4 * n, LOW, cols), weights.dtype),
            pltpu.SemaphoreType.DMA((4 * n,)),
        ],
        name="pack_low",
    )(tiles, counts, weights, fisher)


def pack_high_body(tiles, counts, weights, fisher, after, *rest):
    outs, held, sem = rest[:-2], rest[-2], rest[-1]
    n = len(outs)
    experts, _, rows, _ = outs[0].shape
    y = lax.axis_index("task")
    items = []
    for d in (*range(1, n), 0):
        part = LOW + lax.rem(y + d, n) * rows
        for e in range(experts):
            row, sign = listed(tiles, counts, e)
            at = pl.ds(pl.multiple_of(row + part, 8), rows)
            items.append((weights.at[e, at], outs[d].at[e, 0], None))
            items.append((fisher.at[e, at], outs[d].at[e, 1], sign))
    copy_signed(items, held, sem)


def pack_high(tiles, counts, weights, fisher, n, after):
    experts, _, cols = weights.shape
    rows = (TILE - LOW) // n
    count = 2 * n * experts
    return pl.pallas_call(
        pack_high_body,
        out_shape=[jax.ShapeDtypeStruct((experts, 2, rows, cols), weights.dtype)] * n,
        in_specs=[SMEM, SMEM, HBM, HBM, SMEM],
        out_specs=[HBM] * n,
        scratch_shapes=[
            pltpu.VMEM((count, rows, cols), weights.dtype),
            pltpu.SemaphoreType.DMA((count,)),
        ],
        name="pack_high",
    )(tiles, counts, weights, fisher, after)


def sums(loads):
    num, den = [0.0, 0.0], [0.0, 0.0]
    for load in loads:
        w, f = (v.astype(jnp.float32) for v in load())
        term = (f * w).astype(jnp.bfloat16).astype(jnp.float32)
        term_0, share_0 = jnp.where(f > 0.0, term, 0.0), jnp.maximum(f, 0.0)
        num = [num[0] + term_0, num[1] + (term_0 - term)]
        den = [den[0] + share_0, den[1] + (share_0 - f)]
    return num, den


def merged_of(num, den, prior):
    return (num + PRIOR_WEIGHT * prior.astype(jnp.float32)) / (den + PRIOR_WEIGHT)


def merge_low_body(n, first, *rest):
    got, base, outs = (first, *rest[: n - 1]), rest[n - 1 : 2 * n - 1], rest[2 * n - 1 :]
    rows, cols = outs[0].shape[2:]
    x = lax.axis_index("shard")
    step = 16
    for d, out in enumerate(outs):
        at = pl.ds(pl.multiple_of(lax.rem(x + d, n) * cols, cols), cols)
        for r in range(0, rows, step):
            loads = [
                lambda g=g: (g[0, 0, pl.ds(r, step), at], g[0, 1, pl.ds(r, step), at]) for g in got
            ]
            num, den = sums(loads)
            for j in range(2):
                prior = base[(n - d) % n][0, j, pl.ds(r, step), :]
                out[0, j, pl.ds(r, step), :] = merged_of(num[j], den[j], prior).astype(out.dtype)


def merge_low(first, others, base):
    n = len(base)
    _, _, _, rows, cols = first.shape
    piece = base[0].shape[3]
    out = jax.ShapeDtypeStruct((2, 2, rows, piece), first.dtype)
    return pl.pallas_call(
        functools.partial(merge_low_body, n),
        out_shape=[out] * n,
        grid=(2,),
        in_specs=[pl.BlockSpec((None, 1, 2, rows, cols), lambda i: (0, i, 0, 0, 0))]
        + [pl.BlockSpec((1, 2, rows, cols), lambda i: (i, 0, 0, 0))] * (n - 1)
        + [pl.BlockSpec((1, 2, rows, piece), lambda i: (i, 0, 0, 0))] * n,
        out_specs=[pl.BlockSpec((1, 2, rows, piece), lambda i: (i, 0, 0, 0))] * n,
        compiler_params=PARAMS,
        cost_estimate=pl.CostEstimate(flops=0, bytes_accessed=HINT, transcendentals=0),
        name="merge_low",
    )(first, *others, *base)


def add_high_body(n, y, *refs):
    got, out = refs[:n], refs[n]
    cols = out.shape[-1]
    for x in range(n):
        at = pl.ds(x * cols, cols)
        num, den = sums([lambda g=g: (g[0, 0, :, at], g[0, 1, :, at]) for g in got])
        for j in range(2):
            out[0, x, j, 0] = num[j].astype(out.dtype)
            out[0, x, j, 1] = den[j].astype(out.dtype)


def add_high(y, got):
    n = len(got)
    experts, _, rows, cols = got[0].shape
    expert = lambda i, y: (lax.rem(y[0] + i // 2, n) * 2 + lax.rem(i, 2), 0, 0, 0)
    return pl.pallas_call(
        functools.partial(add_high_body, n),
        out_shape=jax.ShapeDtypeStruct((experts, n, 2, 2, rows, cols // n), got[0].dtype),
        grid_spec=pltpu.PrefetchScalarGridSpec(
            num_scalar_prefetch=1,
            grid=(experts,),
            in_specs=[pl.BlockSpec((1, 2, rows, cols), expert)] * n,
            out_specs=pl.BlockSpec((1, n, 2, 2, rows, cols // n), lambda i, y: (i, 0, 0, 0, 0, 0)),
        ),
        compiler_params=PARAMS,
        name="add_high",
    )(y, *got)


def place_body(n, *refs):
    pieces, out, sem = refs[:n], refs[-2], refs[-1]
    x = lax.axis_index("shard")
    copies = []
    for d, piece in enumerate(pieces):
        came = lax.rem(x + n - d, n)
        for c in range(2):
            copies.append(
                pltpu.make_async_copy(
                    piece.at[c], out.at[c, came, :, pl.ds(0, piece.shape[2])], sem.at[len(copies)]
                )
            )
    for c in copies:
        c.start()
    for c in copies:
        c.wait()


def place(pieces):
    n = len(pieces)
    return pl.pallas_call(
        functools.partial(place_body, n),
        out_shape=jax.ShapeDtypeStruct((2, n, 2, TILE, pieces[0].shape[3]), pieces[0].dtype),
        in_specs=[VMEM] * n,
        out_specs=HBM,
        scratch_shapes=[pltpu.SemaphoreType.DMA((2 * n,))],
        compiler_params=PARAMS,
        name="place",
    )(*pieces)


def merge_high_body(n, first, *rest):
    got, base, out = (first, *rest[: n - 1]), rest[n - 1], rest[-1]
    rows = first.shape[-2]
    y = lax.axis_index("task")
    for m, g in enumerate(got):
        at = pl.ds(pl.multiple_of(lax.rem(y + n - m, n) * rows, rows), rows)
        for x in range(n):
            for j in range(2):
                num, den = (g[0, x, j, k].astype(jnp.float32) for k in range(2))
                out[0, x, j, at, :] = merged_of(num, den, base[0, x, j, at, :]).astype(out.dtype)


def merge_high(first, others, base, whole):
    n = len(others) + 1
    _, c, _, _, _, rows, cols = first.shape
    block = (1, n, 2, 2, rows, cols)
    part = pl.BlockSpec((1, n, 2, TILE - LOW, cols), lambda i: (i, 0, 0, LOW // (TILE - LOW), 0))
    return pl.pallas_call(
        functools.partial(merge_high_body, n),
        out_shape=jax.ShapeDtypeStruct(whole.shape, whole.dtype),
        grid=(c,),
        in_specs=[pl.BlockSpec((None, *block), lambda i: (0, i, 0, 0, 0, 0, 0))]
        + [pl.BlockSpec(block, lambda i: (i, 0, 0, 0, 0, 0))] * (n - 1)
        + [part, HBM],
        out_specs=part,
        input_output_aliases={n + 1: 0},
        compiler_params=PARAMS,
        name="merge_high",
    )(first, *others, base, whole)


def shifted(x, axis, by):
    n = lax.axis_size(axis)
    return lax.ppermute(x, axis, [(i, (i + by) % n) for i in range(n)])


def spread(x, over_x):
    nz, ny, nx = (lax.axis_size(a) for a in ("z", "task", "shard"))
    number = lambda z, c, y, x: ((z * 2 + c) * ny + y) * nx + x
    groups = []
    for y in range(ny):
        turned = [((j + y) % nz, c) for j in range(nz) for c in range(2)]
        if over_x:
            groups.append([number(z, c, y, x) for z, c in turned for x in range(nx)])
        else:
            groups += [[number(z, c, y, x) for z, c in turned] for x in range(nx)]
    return lax.all_to_all(x, MESH, 0, 0, axis_index_groups=groups, tiled=True)


def local(weights, fisher, base_weights, tile_list, tile_count):
    weights, fisher = weights[0], fisher[0]
    nz, nx, ny = (lax.axis_size(a) for a in ("z", "shard", "task"))
    x, y = lax.axis_index("shard"), lax.axis_index("task").reshape(1)
    cols = base_weights.shape[2]
    hold = lax.optimization_barrier

    tiles, counts = tile_list[0, :, :, 0], tile_count[0]
    low, packed = pack_low(tiles, counts, weights, fisher, nz)
    high = pack_high(tiles, counts, weights, fisher, ny, packed)

    got_low = spread(low.reshape(2 * nz, *low.shape[2:]), False).reshape(low.shape)
    got_high = [high[0]] + [shifted(high[d], "task", d) for d in range(1, ny)]
    mine = [got_low[m] for m in range(1, ny)]
    mine, got_high, base = hold((mine, got_high, base_weights))
    others = [shifted(mine[m - 1], "task", m) for m in range(1, ny)]
    added = add_high(y, got_high)
    moved = spread(added.reshape(-1, *added.shape[2:]), True)
    moved = moved.reshape(nz, 2, nx, *moved.shape[1:])
    mine = [moved[m] for m in range(1, ny)]

    base = base.reshape(2, nx, 2, TILE, cols)
    prior = []
    for d in range(nx):
        part = lax.dynamic_index_in_dim(base[:, :, :, :LOW], lax.rem(x + d, nx), 1, keepdims=False)
        prior.append(shifted(part, "shard", d) if d else part)
    mine, others, prior = hold((mine, others, prior))
    rest = [shifted(mine[m - 1], "task", m) for m in range(1, ny)]

    merged = merge_low(got_low, others, prior)
    whole = place([merged[0]] + [shifted(merged[d], "shard", d) for d in range(1, nx)])
    whole = merge_high(moved, rest, base_weights.reshape(whole.shape), whole)
    return whole.reshape(base_weights.shape)


def solution(mesh):
    split = Mesh(
        mesh.devices.reshape(mesh.devices.shape[0] // 2, 2, *mesh.devices.shape[1:]), MESH
    )
    rows = ("z", "core")
    in_specs = (
        P("task", None, ("z", "core", "shard"), None),
        P("task", None, ("z", "core", "shard"), None),
        P(rows, "task", "shard"),
        P("task", None, None, None),
        P("task", None, None),
    )
    return jax.shard_map(
        local, mesh=split, in_specs=in_specs, out_specs=P(rows, "task", "shard"), check_vma=False
    )
```

time: 797 us -> 170 us (0.21)
  Pallas kernels: 601 us -> 22.5 us
  blocking collectives: 29.8 us -> 0 us
  starting transfers between devices: 58.9 us -> 43.3 us
    pallas_call x16 -> x6, Pallas kernels: 601 us -> 22.5 us  [the longest x1 5.93 us: pack_high(): pl.pallas_call(pack_high_body, out_shape=[jax.ShapeDtypeStruct((experts,...]
    ppermute x24 -> x15, waiting for transfers between devices: 93.2 us -> 55.5 us  [shifted(): return lax.ppermute(x, axis, [(i, (i + by) % n) for i in range(n)])]
    all_to_all x5 -> x2, waiting for transfers between devices: 0.01 us -> 34.9 us  [spread(): return lax.all_to_all(x, MESH, 0, 0, axis_index_groups=groups, tiled=True)]
    all_gather x1 -> x0, blocking collectives: 29.8 us -> none  [local(): codes = lax.all_gather(own, 'task', axis=0, tiled=True)]
    all_to_all x5 -> x2, starting transfers between devices: 22.3 us -> 11 us  [spread(): return lax.all_to_all(x, MESH, 0, 0, axis_index_groups=groups, tiled=True)]
    ppermute x24 -> x15, starting transfers between devices: 36.6 us -> 32.2 us  [shifted(): return lax.ppermute(x, axis, [(i, (i + by) % n) for i in range(n)])]
  transfers between devices with their start and end apart: 29 -> 17, of which waited for: 9 -> 10; matrix products, arithmetic and copies ran while one was open for 0% -> 4% of each run, Pallas kernels for 73% -> 4%
where the time goes in v2:
time: 170 us; the launch traced here: 169 us
  waiting for transfers between devices  90.5 us (53%)
  starting transfers between devices  43.3 us (25%)
  Pallas kernels  22.5 us (13%)
  local copies, waits for them, and re-layouts  12.6 us (7%)
    ppermute x15, waiting for transfers between devices, shifted(): return lax.ppermute(x, axis, [(i, (i + by) % n) for i in range(n)])  55.5 us
    all_to_all x2, waiting for transfers between devices, spread(): return lax.all_to_all(x, MESH, 0, 0, axis_index_groups=groups, tiled=True)  34.9 us
    ppermute x15, starting transfers between devices, shifted(): return lax.ppermute(x, axis, [(i, (i + by) % n) for i in range(n)])  32.2 us
    all_to_all x2, starting transfers between devices, spread(): return lax.all_to_all(x, MESH, 0, 0, axis_index_groups=groups, tiled=True)  11 us
    unnamed x18, local copies, waits for them, and re-layouts  6.56 us
    pallas_call x1, Pallas kernels, pack_high(): pl.pallas_call(pack_high_body, out_shape=[jax.ShapeDtypeStruct((experts,...  5.93 us
    pallas_call x1, Pallas kernels, pack_low(): pl.pallas_call(pack_low_body, out_shape=[jax.ShapeDtypeStruct((n, 2, 2, L...  5.07 us
    pallas_call x1, Pallas kernels, add_high(): pl.pallas_call(functools.partial(add_high_body, n), out_shape=jax.ShapeDt...  5.06 us
  transfers between devices with their start and end apart: 17, of which 10 were waited for; matrix products, arithmetic and copies ran while one was open for 4% of the time, Pallas kernels for 4%

profile of v2, /device:TPU:0, one launch (start us, length us, event | category | flops | bytes accessed | tf_op | source)
XLA Modules:
  0.0 168.9 jit_solution(12070794664695283697)
XLA Ops:
  0.0 5.1 %pack_low.1 = (bf16[4,2,2,64,2048]{4,3,2,1,0:T(8,128)(2,1)}, s32[1]{0:T(128)}) custom-call(s32[8,32]{1,0:T(8,128)} %bitcast.43, s32[8,32]{1,0:T(8,128)} %bitcast.45, bf16[8,256,2048]{2,1,0:T(8,128)(2,1)} %bitcast.35, bf16[8,256,2048]{2,1,0:T(8,128)(2,1)} %bitcast.37), custom_call_target="tpu_custom_call" | custom-call | tf_op jit(solution)/shard_map/pack_low/pallas_call | solution.py:71
  5.1 5.4 %all-to-all-start = ((bf16[8,2,64,2048]{3,2,1,0:T(8,128)(2,1)}), bf16[8,2,64,2048]{3,2,1,0:T(8,128)(2,1)}, u32[]{:S(2)}, u32[]{:S(2)}) async-start(bf16[8,2,64,2048]{3,2,1,0:T(8,128)(2,1)} %bitcast.39), calls=%async_computation | async-start | bytes 8388608 | tf_op jit(solution)/shard_map/all_to_all | solution.py:277
  10.5 5.9 %pack_high.1 = (bf16[8,2,16,2048]{3,2,1,0:T(8,128)(2,1)}, bf16[8,2,16,2048]{3,2,1,0:T(8,128)(2,1)}, bf16[8,2,16,2048]{3,2,1,0:T(8,128)(2,1)}, bf16[8,2,16,2048]{3,2,1,0:T(8,128)(2,1)}) custom-call(s32[8,32]{1,0:T(8,128)} %bitcast.44, s32[8,32]{1,0:T(8,128)} %bitcast.46, bf16[8,256,2048]{2,1,0:T(8,128)(2,1)} %bitcast.36, bf16[8,256,2048]{2,1,0:T(8,128)(2,1)} %bitcast.38, ...), custom_call_target="tpu_custom_call" | custom-call | tf_op jit(solution)/shard_map/pack_high/pallas_call | solution.py:107
  16.4 2.7 %collective-permute-start = (bf16[8,2,16,2048]{3,2,1,0:T(8,128)(2,1)}, bf16[8,2,16,2048]{3,2,1,0:T(8,128)(2,1)S(1)}, u32[]{:S(2)}, u32[]{:S(2)}) collective-permute-start(bf16[8,2,16,2048]{3,2,1,0:T(8,128)(2,1)} %get-tuple-element.36), channel_id=1, source_target_pairs={{0,4},{4,8},{8,12},{12,0},{1,5},{5,9},{9,13},{13,1},{2,6},{6,10},{... | collective-permute-start | bytes 3145736 | tf_op jit(solution)/shard_map/ppermute | solution.py:264
  19.1 5.0 %collective-permute-start.1 = (bf16[8,2,16,2048]{3,2,1,0:T(8,128)(2,1)}, bf16[8,2,16,2048]{3,2,1,0:T(8,128)(2,1)S(1)}, u32[]{:S(2)}, u32[]{:S(2)}) collective-permute-start(bf16[8,2,16,2048]{3,2,1,0:T(8,128)(2,1)} %get-tuple-element.37), channel_id=1, source_target_pairs={{0,8},{4,12},{8,0},{12,4},{1,9},{5,13},{9,1},{13,5},{2,10},{6,14},... | collective-permute-start | bytes 3145736 | tf_op jit(solution)/shard_map/ppermute | solution.py:264
  25.3 34.9 %all-to-all-done = bf16[8,2,64,2048]{3,2,1,0:T(8,128)(2,1)} async-done(((bf16[8,2,64,2048]{3,2,1,0:T(8,128)(2,1)}), bf16[8,2,64,2048]{3,2,1,0:T(8,128)(2,1)}, u32[]{:S(2)}, u32[]{:S(2)}) %all-to-all-start) | async-done | bytes 4194336 | tf_op jit(solution)/shard_map/all_to_all | solution.py:277
  60.3 3.6 %fusion = (bf16[2,2,64,2048]{3,2,1,0:T(8,128)(2,1)}, bf16[2,2,64,2048]{3,2,1,0:T(8,128)(2,1)}, bf16[2,2,64,2048]{3,2,1,0:T(8,128)(2,1)}) fusion(bf16[8,2,64,2048]{3,2,1,0:T(8,128)(2,1)} %all-to-all-done), kind=kLoop, calls=%fused_computation.4 | loop fusion | bytes 6291456 | tf_op jit(solution)/shard_map/slice | solution.py:293
  65.0 5.0 %collective-permute-done.1.refs_2_ = bf16[8,2,16,2048]{3,2,1,0:T(8,128)(2,1)S(1)} collective-permute-done((bf16[8,2,16,2048]{3,2,1,0:T(8,128)(2,1)}, bf16[8,2,16,2048]{3,2,1,0:T(8,128)(2,1)S(1)}, u32[]{:S(2)}, u32[]{:S(2)}) %collective-permute-start.1) | collective-permute-done | bytes 1048608 | tf_op jit(solution)/shard_map/ppermute | solution.py:264
  71.0 1.2 copy-done.4
  72.2 1.2 copy-done.6
  73.4 5.1 %add_high.1 = bf16[8,4,2,2,16,512]{5,4,3,2,1,0:T(8,128)(2,1)S(1)} custom-call(s32[1]{0:T(128)} %bitcast.y, bf16[8,2,16,2048]{3,2,1,0:T(8,128)(2,1)S(1)} %copy-done.2, bf16[8,2,16,2048]{3,2,1,0:T(8,128)(2,1)S(1)} %copy-done.4, bf16[8,2,16,2048]{3,2,1,0:T(8,128)(2,1)S(1)} %copy-done.6, bf16[8,2,16,2048]{3,2,1,0:T(8,128)(2,1)} %collective-permute-done.2.refs_3_), custom_call_target="tpu_custom_call" | custom-call | tf_op jit(solution)/shard_map/add_high/pallas_call | solution.py:186
  78.5 1.3 copy-done
  79.8 5.6 %all-to-all-start.1 = ((bf16[32,2,2,16,512]{4,3,2,1,0:T(8,128)(2,1)}), bf16[32,2,2,16,512]{4,3,2,1,0:T(8,128)(2,1)S(1)}, u32[]{:S(2)}, u32[]{:S(2)}) async-start(bf16[32,2,2,16,512]{4,3,2,1,0:T(8,128)(2,1)} %bitcast.32), calls=%async_computation.1 | async-start | bytes 4194304 | tf_op jit(solution)/shard_map/all_to_all | solution.py:277
  86.2 3.9 %collective-permute-start.4 = (bf16[2,2,64,2048]{3,2,1,0:T(8,128)(2,1)}, bf16[2,2,64,2048]{3,2,1,0:T(8,128)(2,1)}, u32[]{:S(2)}, u32[]{:S(2)}) collective-permute-start(bf16[2,2,64,2048]{3,2,1,0:T(8,128)(2,1)} %get-tuple-element.44), channel_id=1, source_target_pairs={{0,8},{4,12},{8,0},{12,4},{1,9},{5,13},{9,1},{13,5},{2,10},{6,14},... | collective-permute-start | bytes 3145736 | tf_op jit(solution)/shard_map/ppermute | solution.py:264
  90.1 1.6 collective-permute-start.5
  91.6 1.3 slice.43
  93.9 1.5 collective-permute-start.6
  95.3 2.7 %collective-permute-start.7 = (bf16[2,2,64,512]{3,2,1,0:T(8,128)(2,1)}, bf16[2,2,64,512]{3,2,1,0:T(8,128)(2,1)}, u32[]{:S(2)}, u32[]{:S(2)}) collective-permute-start(bf16[2,2,64,512]{3,2,1,0:T(8,128)(2,1)} %get-tuple-element.68), channel_id=1, source_target_pairs={{0,2},{1,3},{2,0},{3,1},{4,6},{5,7},{6,4},{7,5},{8,10},{9,11},{10,... | collective-permute-start | bytes 786440 | tf_op jit(solution)/shard_map/ppermute | solution.py:264
  98.0 19.6 %collective-permute-done.6.rest_4_ = bf16[2,2,64,512]{3,2,1,0:T(8,128)(2,1)S(1)} collective-permute-done((bf16[2,2,64,512]{3,2,1,0:T(8,128)(2,1)S(1)}, bf16[2,2,64,512]{3,2,1,0:T(8,128)(2,1)S(1)}, u32[]{:S(2)}, u32[]{:S(2)}) %collective-permute-start.6) | collective-permute-done | bytes 262176 | tf_op jit(solution)/shard_map/ppermute | solution.py:264
  118.4 1.6 collective-permute-start.8
  120.2 3.7 %collective-permute-done.7.rest_5_ = bf16[2,2,64,512]{3,2,1,0:T(8,128)(2,1)} collective-permute-done((bf16[2,2,64,512]{3,2,1,0:T(8,128)(2,1)}, bf16[2,2,64,512]{3,2,1,0:T(8,128)(2,1)}, u32[]{:S(2)}, u32[]{:S(2)}) %collective-permute-start.7) | collective-permute-done | bytes 262176 | tf_op jit(solution)/shard_map/ppermute | solution.py:264
  124.0 2.7 %collective-permute-done.8.rest_6_ = bf16[2,2,64,512]{3,2,1,0:T(8,128)(2,1)} collective-permute-done((bf16[2,2,64,512]{3,2,1,0:T(8,128)(2,1)}, bf16[2,2,64,512]{3,2,1,0:T(8,128)(2,1)}, u32[]{:S(2)}, u32[]{:S(2)}) %collective-permute-start.8) | collective-permute-done | bytes 262176 | tf_op jit(solution)/shard_map/ppermute | solution.py:264
  126.6 9.4 %collective-permute-done.4.rest_1_ = bf16[2,2,64,2048]{3,2,1,0:T(8,128)(2,1)} collective-permute-done((bf16[2,2,64,2048]{3,2,1,0:T(8,128)(2,1)}, bf16[2,2,64,2048]{3,2,1,0:T(8,128)(2,1)}, u32[]{:S(2)}, u32[]{:S(2)}) %collective-permute-start.4) | collective-permute-done | bytes 1048608 | tf_op jit(solution)/shard_map/ppermute | solution.py:264
  136.1 3.9 %merge_low.1 = (bf16[2,2,64,512]{3,2,1,0:T(8,128)(2,1)S(1)}, bf16[2,2,64,512]{3,2,1,0:T(8,128)(2,1)S(1)}, bf16[2,2,64,512]{3,2,1,0:T(8,128)(2,1)S(1)}, bf16[2,2,64,512]{3,2,1,0:T(8,128)(2,1)S(1)}) custom-call(bf16[4,2,2,64,2048]{4,3,2,1,0:T(8,128)(2,1)} %bitcast.17.first, bf16[2,2,64,2048]{3,2,1,0:T(8,128)(2,1)S(1)} %collective-permute-done.3.rest_0_, ...), custom_call_target="tpu_custom_call" | custom-call | bytes 400000000 | tf_op jit(solution)/shard_map/merge_low/pallas_call | solution.py:157
  140.0 1.5 collective-permute-start.12
  141.5 2.8 %collective-permute-start.10 = (bf16[2,4,2,2,16,512]{5,4,3,2,1,0:T(8,128)(2,1)S(1)}, bf16[2,4,2,2,16,512]{5,4,3,2,1,0:T(8,128)(2,1)S(1)}, u32[]{:S(2)}, u32[]{:S(2)}) collective-permute-start(bf16[2,4,2,2,16,512]{5,4,3,2,1,0:T(8,128)(2,1)S(1)} %bitcast.42), channel_id=1, source_target_pairs={{0,8},{4,12},{8,0},{12,4},{1,9},{5,13},{9,1},{13,5},{2,10},{6,14},... | collective-permute-start | bytes 1572872 | tf_op jit(solution)/shard_map/ppermute | solution.py:264
  146.3 2.7 %collective-permute-start.13 = (bf16[2,2,64,512]{3,2,1,0:T(8,128)(2,1)S(1)}, bf16[2,2,64,512]{3,2,1,0:T(8,128)(2,1)S(1)}, u32[]{:S(2)}, u32[]{:S(2)}) collective-permute-start(bf16[2,2,64,512]{3,2,1,0:T(8,128)(2,1)S(1)} %get-tuple-element.59), channel_id=1, source_target_pairs={{0,2},{1,3},{2,0},{3,1},{4,6},{5,7},{6,4},{7,5},{8,10},{9,11},{10,... | collective-permute-start | bytes 786440 | tf_op jit(solution)/shard_map/ppermute | solution.py:264
  149.2 2.4 %collective-permute-start.14 = (bf16[2,2,64,512]{3,2,1,0:T(8,128)(2,1)S(1)}, bf16[2,2,64,512]{3,2,1,0:T(8,128)(2,1)S(1)}, u32[]{:S(2)}, u32[]{:S(2)}) collective-permute-start(bf16[2,2,64,512]{3,2,1,0:T(8,128)(2,1)S(1)} %get-tuple-element.60), channel_id=1, source_target_pairs={{0,3},{1,0},{2,1},{3,2},{4,7},{5,4},{6,5},{7,6},{8,11},{9,8},{10,9... | collective-permute-start | bytes 786440 | tf_op jit(solution)/shard_map/ppermute | solution.py:264
  151.5 3.8 %collective-permute-done.13.refs_2_ = bf16[2,2,64,512]{3,2,1,0:T(8,128)(2,1)S(1)} collective-permute-done((bf16[2,2,64,512]{3,2,1,0:T(8,128)(2,1)S(1)}, bf16[2,2,64,512]{3,2,1,0:T(8,128)(2,1)S(1)}, u32[]{:S(2)}, u32[]{:S(2)}) %collective-permute-start.13) | collective-permute-done | bytes 262176 | tf_op jit(solution)/shard_map/ppermute | solution.py:264
  155.3 3.4 %collective-permute-done.14.refs_3_ = bf16[2,2,64,512]{3,2,1,0:T(8,128)(2,1)S(1)} collective-permute-done((bf16[2,2,64,512]{3,2,1,0:T(8,128)(2,1)S(1)}, bf16[2,2,64,512]{3,2,1,0:T(8,128)(2,1)S(1)}, u32[]{:S(2)}, u32[]{:S(2)}) %collective-permute-start.14) | collective-permute-done | bytes 262176 | tf_op jit(solution)/shard_map/ppermute | solution.py:264
  159.7 7.7 %collective-permute-done.11.rest_2_ = bf16[2,4,2,2,16,512]{5,4,3,2,1,0:T(8,128)(2,1)S(1)} collective-permute-done((bf16[2,4,2,2,16,512]{5,4,3,2,1,0:T(8,128)(2,1)S(1)}, bf16[2,4,2,2,16,512]{5,4,3,2,1,0:T(8,128)(2,1)S(1)}, u32[]{:S(2)}, u32[]{:S(2)}) %collective-permute-start.11) | collective-permute-done | bytes 524320 | tf_op jit(solution)/shard_map/ppermute | solution.py:264
  167.4 1.5 merge_high.1
  (30 shorter events, 9.1 us)
Async XLA Ops:
  5.1 55.2 %all-to-all-start = ((bf16[8,2,64,2048]{3,2,1,0:T(8,128)(2,1)}), bf16[8,2,64,2048]{3,2,1,0:T(8,128)(2,1)}, u32[]{:S(2)}, u32[]{:S(2)}) async-start(bf16[8,2,64,2048]{3,2,1,0:T(8,128)(2,1)} %bitcast.39), calls=%async_computation | async-start | bytes 8388608 | tf_op jit(solution)/shard_map/all_to_all | solution.py:277
  16.4 47.4 %collective-permute-start = (bf16[8,2,16,2048]{3,2,1,0:T(8,128)(2,1)}, bf16[8,2,16,2048]{3,2,1,0:T(8,128)(2,1)S(1)}, u32[]{:S(2)}, u32[]{:S(2)}) collective-permute-start(bf16[8,2,16,2048]{3,2,1,0:T(8,128)(2,1)} %get-tuple-element.36), channel_id=1, source_target_pairs={{0,4},{4,8},{8,12},{12,0},{1,5},{5,9},{9,13},{13,1},{2,6},{6,10},{... | collective-permute-start | bytes 3145736 | tf_op jit(solution)/shard_map/ppermute | solution.py:264
  19.1 50.9 %collective-permute-start.1 = (bf16[8,2,16,2048]{3,2,1,0:T(8,128)(2,1)}, bf16[8,2,16,2048]{3,2,1,0:T(8,128)(2,1)S(1)}, u32[]{:S(2)}, u32[]{:S(2)}) collective-permute-start(bf16[8,2,16,2048]{3,2,1,0:T(8,128)(2,1)} %get-tuple-element.37), channel_id=1, source_target_pairs={{0,8},{4,12},{8,0},{12,4},{1,9},{5,13},{9,1},{13,5},{2,10},{6,14},... | collective-permute-start | bytes 3145736 | tf_op jit(solution)/shard_map/ppermute | solution.py:264
  24.1 46.9 %collective-permute-start.2 = (bf16[8,2,16,2048]{3,2,1,0:T(8,128)(2,1)}, bf16[8,2,16,2048]{3,2,1,0:T(8,128)(2,1)}, u32[]{:S(2)}, u32[]{:S(2)}) collective-permute-start(bf16[8,2,16,2048]{3,2,1,0:T(8,128)(2,1)} %get-tuple-element.38), channel_id=1, source_target_pairs={{0,12},{4,0},{8,4},{12,8},{1,13},{5,1},{9,5},{13,9},{2,14},{6,2},{... | collective-permute-start | bytes 3145736 | tf_op jit(solution)/shard_map/ppermute | solution.py:264
  25.3 45.7 %copy-start.2 = (bf16[8,2,16,2048]{3,2,1,0:T(8,128)(2,1)S(1)}, bf16[8,2,16,2048]{3,2,1,0:T(8,128)(2,1)}, u32[]{:S(2)}) copy-start(bf16[8,2,16,2048]{3,2,1,0:T(8,128)(2,1)} %get-tuple-element.39.refs_0_) | copy-start | bytes 3145732
  63.9 1.1 copy-start.3
  70.0 1.0 copy-start.5
  71.0 1.2 copy-start.4
  72.2 1.2 copy-start.6
  78.5 1.3 copy-start
  79.8 40.2 %all-to-all-start.1 = ((bf16[32,2,2,16,512]{4,3,2,1,0:T(8,128)(2,1)}), bf16[32,2,2,16,512]{4,3,2,1,0:T(8,128)(2,1)S(1)}, u32[]{:S(2)}, u32[]{:S(2)}) async-start(bf16[32,2,2,16,512]{4,3,2,1,0:T(8,128)(2,1)} %bitcast.32), calls=%async_computation.1 | async-start | bytes 4194304 | tf_op jit(solution)/shard_map/all_to_all | solution.py:277
  85.5 41.2 %collective-permute-start.3 = (bf16[2,2,64,2048]{3,2,1,0:T(8,128)(2,1)}, bf16[2,2,64,2048]{3,2,1,0:T(8,128)(2,1)S(1)}, u32[]{:S(2)}, u32[]{:S(2)}) collective-permute-start(bf16[2,2,64,2048]{3,2,1,0:T(8,128)(2,1)} %get-tuple-element.43), channel_id=1, source_target_pairs={{0,4},{4,8},{8,12},{12,0},{1,5},{5,9},{9,13},{13,1},{2,6},{6,10},{... | collective-permute-start | bytes 3145736 | tf_op jit(solution)/shard_map/ppermute | solution.py:264
  86.2 49.8 %collective-permute-start.4 = (bf16[2,2,64,2048]{3,2,1,0:T(8,128)(2,1)}, bf16[2,2,64,2048]{3,2,1,0:T(8,128)(2,1)}, u32[]{:S(2)}, u32[]{:S(2)}) collective-permute-start(bf16[2,2,64,2048]{3,2,1,0:T(8,128)(2,1)} %get-tuple-element.44), channel_id=1, source_target_pairs={{0,8},{4,12},{8,0},{12,4},{1,9},{5,13},{9,1},{13,5},{2,10},{6,14},... | collective-permute-start | bytes 3145736 | tf_op jit(solution)/shard_map/ppermute | solution.py:264
  90.1 46.0 %collective-permute-start.5 = (bf16[2,2,64,2048]{3,2,1,0:T(8,128)(2,1)}, bf16[2,2,64,2048]{3,2,1,0:T(8,128)(2,1)}, u32[]{:S(2)}, u32[]{:S(2)}) collective-permute-start(bf16[2,2,64,2048]{3,2,1,0:T(8,128)(2,1)} %get-tuple-element.45), channel_id=1, source_target_pairs={{0,12},{4,0},{8,4},{12,8},{1,13},{5,1},{9,5},{13,9},{2,14},{6,2},{... | collective-permute-start | bytes 3145736 | tf_op jit(solution)/shard_map/ppermute | solution.py:264
  93.9 23.8 %collective-permute-start.6 = (bf16[2,2,64,512]{3,2,1,0:T(8,128)(2,1)S(1)}, bf16[2,2,64,512]{3,2,1,0:T(8,128)(2,1)S(1)}, u32[]{:S(2)}, u32[]{:S(2)}) collective-permute-start(bf16[2,2,64,512]{3,2,1,0:T(8,128)(2,1)S(1)} %get-tuple-element.69), channel_id=1, source_target_pairs={{0,1},{1,2},{2,3},{3,0},{4,5},{5,6},{6,7},{7,4},{8,9},{9,10},{10,1... | collective-permute-start | bytes 786440 | tf_op jit(solution)/shard_map/ppermute | solution.py:264
  95.3 28.6 %collective-permute-start.7 = (bf16[2,2,64,512]{3,2,1,0:T(8,128)(2,1)}, bf16[2,2,64,512]{3,2,1,0:T(8,128)(2,1)}, u32[]{:S(2)}, u32[]{:S(2)}) collective-permute-start(bf16[2,2,64,512]{3,2,1,0:T(8,128)(2,1)} %get-tuple-element.68), channel_id=1, source_target_pairs={{0,2},{1,3},{2,0},{3,1},{4,6},{5,7},{6,4},{7,5},{8,10},{9,11},{10,... | collective-permute-start | bytes 786440 | tf_op jit(solution)/shard_map/ppermute | solution.py:264
  117.6 0.7 copy-start.7
  118.4 8.3 %collective-permute-start.8 = (bf16[2,2,64,512]{3,2,1,0:T(8,128)(2,1)}, bf16[2,2,64,512]{3,2,1,0:T(8,128)(2,1)}, u32[]{:S(2)}, u32[]{:S(2)}) collective-permute-start(bf16[2,2,64,512]{3,2,1,0:T(8,128)(2,1)} %get-tuple-element.67), channel_id=1, source_target_pairs={{0,3},{1,0},{2,1},{3,2},{4,7},{5,4},{6,5},{7,6},{8,11},{9,8},{10,9... | collective-permute-start | bytes 786440 | tf_op jit(solution)/shard_map/ppermute | solution.py:264
  120.0 16.1 %copy-start.8 = (bf16[2,2,64,512]{3,2,1,0:T(8,128)(2,1)S(1)}, bf16[2,2,64,512]{3,2,1,0:T(8,128)(2,1)}, u32[]{:S(2)}) copy-start(bf16[2,2,64,512]{3,2,1,0:T(8,128)(2,1)} %copy-done.7) | copy-start | bytes 786436
  140.0 27.5 %copy-start.1 = (bf16[1,2048,512]{2,1,0:T(8,128)(2,1)S(1)}, bf16[1,2048,512]{2,1,0:T(8,128)(2,1)}, u32[]{:S(2)}) copy-start(bf16[1,2048,512]{2,1,0:T(8,128)(2,1)} %param.7) | copy-start | bytes 6291460
  140.0 9.2 %collective-permute-start.12 = (bf16[2,2,64,512]{3,2,1,0:T(8,128)(2,1)S(1)}, bf16[2,2,64,512]{3,2,1,0:T(8,128)(2,1)S(1)}, u32[]{:S(2)}, u32[]{:S(2)}) collective-permute-start(bf16[2,2,64,512]{3,2,1,0:T(8,128)(2,1)S(1)} %get-tuple-element.58), channel_id=1, source_target_pairs={{0,1},{1,2},{2,3},{3,0},{4,5},{5,6},{6,7},{7,4},{8,9},{9,10},{10,1... | collective-permute-start | bytes 786440 | tf_op jit(solution)/shard_map/ppermute | solution.py:264
  141.5 18.2 %collective-permute-start.10 = (bf16[2,4,2,2,16,512]{5,4,3,2,1,0:T(8,128)(2,1)S(1)}, bf16[2,4,2,2,16,512]{5,4,3,2,1,0:T(8,128)(2,1)S(1)}, u32[]{:S(2)}, u32[]{:S(2)}) collective-permute-start(bf16[2,4,2,2,16,512]{5,4,3,2,1,0:T(8,128)(2,1)S(1)} %bitcast.42), channel_id=1, source_target_pairs={{0,8},{4,12},{8,0},{12,4},{1,9},{5,13},{9,1},{13,5},{2,10},{6,14},... | collective-permute-start | bytes 1572872 | tf_op jit(solution)/shard_map/ppermute | solution.py:264
  144.3 23.1 %collective-permute-start.11 = (bf16[2,4,2,2,16,512]{5,4,3,2,1,0:T(8,128)(2,1)S(1)}, bf16[2,4,2,2,16,512]{5,4,3,2,1,0:T(8,128)(2,1)S(1)}, u32[]{:S(2)}, u32[]{:S(2)}) collective-permute-start(bf16[2,4,2,2,16,512]{5,4,3,2,1,0:T(8,128)(2,1)S(1)} %bitcast.41), channel_id=1, source_target_pairs={{0,12},{4,0},{8,4},{12,8},{1,13},{5,1},{9,5},{13,9},{2,14},{6,2},{... | collective-permute-start | bytes 1572872 | tf_op jit(solution)/shard_map/ppermute | solution.py:264
  145.5 21.9 %collective-permute-start.9 = (bf16[2,4,2,2,16,512]{5,4,3,2,1,0:T(8,128)(2,1)S(1)}, bf16[2,4,2,2,16,512]{5,4,3,2,1,0:T(8,128)(2,1)S(1)}, u32[]{:S(2)}, u32[]{:S(2)}) collective-permute-start(bf16[2,4,2,2,16,512]{5,4,3,2,1,0:T(8,128)(2,1)S(1)} %bitcast.40), channel_id=1, source_target_pairs={{0,4},{4,8},{8,12},{12,0},{1,5},{5,9},{9,13},{13,1},{2,6},{6,10},{... | collective-permute-start | bytes 1572872 | tf_op jit(solution)/shard_map/ppermute | solution.py:264
  146.3 9.0 %collective-permute-start.13 = (bf16[2,2,64,512]{3,2,1,0:T(8,128)(2,1)S(1)}, bf16[2,2,64,512]{3,2,1,0:T(8,128)(2,1)S(1)}, u32[]{:S(2)}, u32[]{:S(2)}) collective-permute-start(bf16[2,2,64,512]{3,2,1,0:T(8,128)(2,1)S(1)} %get-tuple-element.59), channel_id=1, source_target_pairs={{0,2},{1,3},{2,0},{3,1},{4,6},{5,7},{6,4},{7,5},{8,10},{9,11},{10,... | collective-permute-start | bytes 786440 | tf_op jit(solution)/shard_map/ppermute | solution.py:264
  149.2 9.5 %collective-permute-start.14 = (bf16[2,2,64,512]{3,2,1,0:T(8,128)(2,1)S(1)}, bf16[2,2,64,512]{3,2,1,0:T(8,128)(2,1)S(1)}, u32[]{:S(2)}, u32[]{:S(2)}) collective-permute-start(bf16[2,2,64,512]{3,2,1,0:T(8,128)(2,1)S(1)} %get-tuple-element.60), channel_id=1, source_target_pairs={{0,3},{1,0},{2,1},{3,2},{4,7},{5,4},{6,5},{7,6},{8,11},{9,8},{10,9... | collective-permute-start | bytes 786440 | tf_op jit(solution)/shard_map/ppermute | solution.py:264

commit v3 on v2

v3 whole, which is shorter than its diff:
```python
import functools

import jax
import jax.numpy as jnp
from jax import lax
from jax.experimental import pallas as pl
from jax.experimental.pallas import tpu as pltpu
from jax.sharding import Mesh, PartitionSpec as P

TILE = 128
PRIOR_WEIGHT = 0.5
LOW = 64
LONG = pl.CostEstimate(flops=100_000_000_000, bytes_accessed=0, transcendentals=0)
SHORT = pl.CostEstimate(flops=0, bytes_accessed=0, transcendentals=0)
GRANT = 16 << 20
MESH = ("z", "core", "task", "shard")
ANY = pl.BlockSpec(memory_space=pl.ANY)
HBM = pl.BlockSpec(memory_space=pltpu.HBM)
VMEM = pl.BlockSpec(memory_space=pltpu.VMEM)
SMEM = pl.BlockSpec(memory_space=pltpu.SMEM)
PARAMS = pltpu.CompilerParams(vmem_limit_bytes=GRANT)


def my_block():
    z, c, x = lax.axis_index("z"), lax.axis_index("core"), lax.axis_index("shard")
    return (z * 2 + c) * lax.axis_size("shard") + x


def listed(tiles, counts, e):
    tile = jnp.minimum(jnp.maximum(tiles[e, my_block()], 0), 1)
    sign = jnp.where(counts[e, my_block()] > 0, jnp.where(tile == 0, 1.0, -1.0), 0.0)
    return tile * TILE, sign.astype(jnp.bfloat16)


def pack_body(tiles, counts, weights, fisher, low, *rest):
    high, (held, came, sent) = rest[:-3], rest[-3:]
    n, rows = len(high), high[0].shape[2]
    y = lax.axis_index("task")
    reads, signs, experts = [], [], []
    for j in range(n):
        for ec in range(2):
            e = lax.rem(y + j, n) * 2 + ec
            row, sign = listed(tiles, counts, e)
            at = pl.ds(pl.multiple_of(row, TILE), TILE)
            for a, src in enumerate((weights, fisher)):
                i = len(reads)
                reads.append(pltpu.make_async_copy(src.at[e, at], held.at[i], came.at[i]))
                signs.append(sign if a else None)
                experts.append(e)
    for read in reads:
        read.start()
    writes = []
    for i, read in enumerate(reads):
        read.wait()
        if signs[i] is not None:
            held[i] = held[i] * signs[i]
        at = low.at[i // 4, i // 2 % 2, i % 2]
        parts = [(pl.ds(0, LOW), at)]
        for d in range(n):
            row = pl.multiple_of(LOW + lax.rem(y + d, n) * rows, 8)
            parts.append((pl.ds(row, rows), high[d].at[experts[i], i % 2]))
        for src, dst in parts:
            k = len(writes)
            writes.append(pltpu.make_async_copy(held.at[i, src], dst, sent.at[k]))
            writes[-1].start()
    for write in writes:
        write.wait()


def pack(tiles, counts, weights, fisher, n):
    experts, _, cols = weights.shape
    rows = (TILE - LOW) // n
    count = 2 * experts
    return pl.pallas_call(
        pack_body,
        out_shape=[jax.ShapeDtypeStruct((n, 2, 2, LOW, cols), weights.dtype)]
        + [jax.ShapeDtypeStruct((experts, 2, rows, cols), weights.dtype)] * n,
        in_specs=[SMEM, SMEM, HBM, HBM],
        out_specs=[HBM] * (n + 1),
        scratch_shapes=[
            pltpu.VMEM((count, TILE, cols), weights.dtype),
            pltpu.SemaphoreType.DMA((count,)),
            pltpu.SemaphoreType.DMA((count * (n + 1),)),
        ],
        name="pack",
    )(tiles, counts, weights, fisher)


def sums(loads):
    num, den = [0.0, 0.0], [0.0, 0.0]
    for load in loads:
        w, f = (v.astype(jnp.float32) for v in load())
        term = (f * w).astype(jnp.bfloat16).astype(jnp.float32)
        term_0, share_0 = jnp.where(f > 0.0, term, 0.0), jnp.maximum(f, 0.0)
        num = [num[0] + term_0, num[1] + (term_0 - term)]
        den = [den[0] + share_0, den[1] + (share_0 - f)]
    return num, den


def merged_of(num, den, prior):
    return (num + PRIOR_WEIGHT * prior.astype(jnp.float32)) / (den + PRIOR_WEIGHT)


def merge_low_body(n, passed, first, *rest):
    got, base, outs = (first, *rest[: n - 1]), rest[n - 1 : 2 * n - 1], rest[2 * n - 1 :]
    rows, cols = outs[0].shape[2:]
    x = lax.axis_index("shard")
    step = 16
    for d, out in enumerate(outs):
        at = pl.ds(pl.multiple_of(lax.rem(x + d, n) * cols, cols), cols)
        for r in range(0, rows, step):
            loads = [
                lambda g=g: (g[0, 0, pl.ds(r, step), at], g[0, 1, pl.ds(r, step), at]) for g in got
            ]
            num, den = sums(loads)
            for j in range(2):
                prior = base[(n - d) % n][0, j, pl.ds(r, step), :]
                out[0, j, pl.ds(r, step), :] = merged_of(num[j], den[j], prior).astype(out.dtype)


def merge_low(first, others, base, passed):
    n = len(base)
    _, _, _, rows, cols = first.shape
    piece = base[0].shape[3]
    out = jax.ShapeDtypeStruct((2, 2, rows, piece), first.dtype)
    return pl.pallas_call(
        functools.partial(merge_low_body, n),
        out_shape=[out] * n,
        grid=(2,),
        in_specs=[SMEM, pl.BlockSpec((None, 1, 2, rows, cols), lambda i: (0, i, 0, 0, 0))]
        + [pl.BlockSpec((1, 2, rows, cols), lambda i: (i, 0, 0, 0))] * (n - 1)
        + [pl.BlockSpec((1, 2, rows, piece), lambda i: (i, 0, 0, 0))] * n,
        out_specs=[pl.BlockSpec((1, 2, rows, piece), lambda i: (i, 0, 0, 0))] * n,
        compiler_params=PARAMS,
        cost_estimate=LONG,
        name="merge_low",
    )(passed, first, *others, *base)


def add_high_body(n, *refs):
    got, out = refs[:n], refs[n]
    cols = out.shape[-1]
    for e in range(out.shape[0]):
        for x in range(n):
            at = pl.ds(x * cols, cols)
            num, den = sums([lambda g=g: (g[e, 0, :, at], g[e, 1, :, at]) for g in got])
            for j in range(2):
                out[e, x, j, 0] = num[j].astype(out.dtype)
                out[e, x, j, 1] = den[j].astype(out.dtype)


def add_high(got):
    n = len(got)
    experts, _, rows, cols = got[0].shape
    step = 2
    return pl.pallas_call(
        functools.partial(add_high_body, n),
        out_shape=jax.ShapeDtypeStruct((experts, n, 2, 2, rows, cols // n), got[0].dtype),
        grid=(experts // step,),
        in_specs=[pl.BlockSpec((step, 2, rows, cols), lambda i: (i, 0, 0, 0))] * n,
        out_specs=pl.BlockSpec((step, n, 2, 2, rows, cols // n), lambda i: (i, 0, 0, 0, 0, 0)),
        compiler_params=PARAMS,
        cost_estimate=SHORT,
        name="add_high",
    )(*got)


def place_body(n, *refs):
    pieces, out, sem = refs[:n], refs[-2], refs[-1]
    x = lax.axis_index("shard")
    copies = []
    for d, piece in enumerate(pieces):
        came = lax.rem(x + n - d, n)
        for c in range(2):
            copies.append(
                pltpu.make_async_copy(
                    piece.at[c], out.at[c, came, :, pl.ds(0, piece.shape[2])], sem.at[len(copies)]
                )
            )
    for c in copies:
        c.start()
    for c in copies:
        c.wait()


def place(pieces):
    n = len(pieces)
    return pl.pallas_call(
        functools.partial(place_body, n),
        out_shape=jax.ShapeDtypeStruct((2, n, 2, TILE, pieces[0].shape[3]), pieces[0].dtype),
        in_specs=[VMEM] * n,
        out_specs=HBM,
        scratch_shapes=[pltpu.SemaphoreType.DMA((2 * n,))],
        compiler_params=PARAMS,
        cost_estimate=SHORT,
        name="place",
    )(*pieces)


def merge_high_body(got, base, *rest):
    out = rest[-1]
    n, _, _, _, _, rows, _ = got.shape
    for m in range(n):
        at = pl.ds(m * rows, rows)
        for x in range(n):
            for j in range(2):
                num, den = (got[m, 0, x, j, k].astype(jnp.float32) for k in range(2))
                out[0, x, j, at, :] = merged_of(num, den, base[0, x, j, at, :]).astype(out.dtype)


def merge_high(got, base, whole, passed):
    n, c, _, _, _, rows, cols = got.shape
    part = pl.BlockSpec((1, n, 2, TILE - LOW, cols), lambda i: (i, 0, 0, LOW // (TILE - LOW), 0))
    return pl.pallas_call(
        merge_high_body,
        out_shape=jax.ShapeDtypeStruct(whole.shape, whole.dtype),
        grid=(c,),
        in_specs=[
            pl.BlockSpec((n, 1, n, 2, 2, rows, cols), lambda i: (0, i, 0, 0, 0, 0, 0)),
            part,
            HBM,
            SMEM,
        ],
        out_specs=part,
        input_output_aliases={2: 0},
        compiler_params=PARAMS,
        name="merge_high",
    )(got, base, whole, passed)


def fence_body(*refs):
    refs[-1][0] = 0


def fence(arrays):
    return pl.pallas_call(
        fence_body,
        out_shape=jax.ShapeDtypeStruct((1,), jnp.int32),
        in_specs=[ANY] * len(arrays),
        out_specs=SMEM,
        compiler_params=PARAMS,
        cost_estimate=LONG,
        name="fence",
    )(*arrays)


def shifted(x, axis, by):
    n = lax.axis_size(axis)
    return lax.ppermute(x, axis, [(i, (i + by) % n) for i in range(n)])


def all_shifted(pieces, axis):
    n = lax.axis_size(axis)
    moved = {d: shifted(pieces[d], axis, d) for d in (*range(1, n, 2), *range(2, n, 2))}
    return [moved[d] for d in range(1, n)]


def over_z(x):
    nz, ny, nx = (lax.axis_size(a) for a in ("z", "task", "shard"))
    groups = [
        [(((j + y) % nz * 2 + c) * ny + y) * nx + x for j in range(nz) for c in range(2)]
        for y in range(ny)
        for x in range(nx)
    ]
    flat = x.reshape(2 * nz, *x.shape[2:])
    return lax.all_to_all(flat, MESH, 0, 0, axis_index_groups=groups, tiled=True).reshape(x.shape)


def local(weights, fisher, base_weights, tile_list, tile_count):
    weights, fisher = weights[0], fisher[0]
    nz, nx, ny = (lax.axis_size(a) for a in ("z", "shard", "task"))
    x = lax.axis_index("shard")
    cols = base_weights.shape[2]
    hold = lax.optimization_barrier

    tiles, counts = tile_list[0, :, :, 0], tile_count[0]
    low, *high = pack(tiles, counts, weights, fisher, nz)
    got_low = over_z(low)
    got_high = [high[0]] + all_shifted(high, "task")
    mine = [got_low[m] for m in range(1, ny)]
    base = base_weights.reshape(2, nx, 2, TILE, cols)
    base, packed = hold((base, high[1]))
    prior = []
    for d in range(nx):
        part = lax.dynamic_index_in_dim(base[:, :, :, :LOW], lax.rem(x + d, nx), 1, keepdims=False)
        prior.append(shifted(part, "shard", d) if d else part)
    mine, got_high, prior = hold((mine, got_high, prior))
    others = all_shifted([None, *mine], "task")
    added = add_high(got_high)
    moved = lax.all_to_all(
        added.reshape(-1, *added.shape[2:]), ("z", "core", "shard"), 0, 0, tiled=True
    )
    moved, passed = hold((moved, fence(others)))
    moved = lax.all_to_all(
        moved.reshape(nz, 2, nx, *moved.shape[1:]), "task", 0, 0, tiled=True
    )

    merged = merge_low(got_low, others, prior, passed)
    whole = place([merged[0]] + all_shifted(merged, "shard"))
    whole = merge_high(moved, base_weights.reshape(whole.shape), whole, passed)
    return whole.reshape(base_weights.shape)


def solution(mesh):
    split = Mesh(
        mesh.devices.reshape(mesh.devices.shape[0] // 2, 2, *mesh.devices.shape[1:]), MESH
    )
    rows = ("z", "core")
    in_specs = (
        P("task", None, ("z", "core", "shard"), None),
        P("task", None, ("z", "core", "shard"), None),
        P(rows, "task", "shard"),
        P("task", None, None, None),
        P("task", None, None),
    )
    return jax.shard_map(
        local, mesh=split, in_specs=in_specs, out_specs=P(rows, "task", "shard"), check_vma=False
    )
```

time: 170 us -> 155 us (0.912)
  waiting for transfers between devices: 90.5 us -> 80.3 us
  starting transfers between devices: 43.3 us -> 40.1 us
    ppermute x15 -> x12, starting transfers between devices: 32.2 us -> 23.3 us  [shifted(): return lax.ppermute(x, axis, [(i, (i + by) % n) for i in range(n)])]
    all_to_all x2 -> x3, waiting for transfers between devices: 34.9 us -> 27.3 us  [the longest x1 24.9 us: over_z(): lax.all_to_all(flat, MESH, 0, 0, axis_index_groups=groups, tiled=True)]
    all_to_all x2 -> x3, starting transfers between devices: 11 us -> 16.7 us  [the longest x1 7.44 us: local(): lax.all_to_all(added.reshape(-1, *added.shape[2:]), ('z', 'core', 'shard'...]
    ppermute x15 -> x12, waiting for transfers between devices: 55.5 us -> 53.1 us  [shifted(): return lax.ppermute(x, axis, [(i, (i + by) % n) for i in range(n)])]
    pallas_call x3, Pallas kernels: 12.5 us -> 10.7 us  [the longest x1 7.88 us: pack(): pl.pallas_call(pack_body, out_shape=[jax.ShapeDtypeStruct((n, 2, 2, LOW,...]
    unnamed x18 -> x22, local copies, waits for them, and re-layouts: 6.56 us -> 6.59 us
  transfers between devices with their start and end apart: 17 -> 15, of which waited for: 10 -> 7; matrix products, arithmetic and copies ran while one was open for 4% -> 4% of each run, Pallas kernels for 4% -> 7%
where the time goes in v3:
time: 155 us; the launch traced here: 154 us
  waiting for transfers between devices  80.3 us (52%)
  starting transfers between devices  40.1 us (26%)
  Pallas kernels  20.8 us (13%)
  local copies, waits for them, and re-layouts  12.6 us (8%)
    ppermute x12, waiting for transfers between devices, shifted(): return lax.ppermute(x, axis, [(i, (i + by) % n) for i in range(n)])  53.1 us
    all_to_all x1, waiting for transfers between devices, over_z(): lax.all_to_all(flat, MESH, 0, 0, axis_index_groups=groups, tiled=True)  24.9 us
    ppermute x12, starting transfers between devices, shifted(): return lax.ppermute(x, axis, [(i, (i + by) % n) for i in range(n)])  23.3 us
    pallas_call x1, Pallas kernels, pack(): pl.pallas_call(pack_body, out_shape=[jax.ShapeDtypeStruct((n, 2, 2, LOW,...  7.88 us
    all_to_all x1, starting transfers between devices, local(): lax.all_to_all(added.reshape(-1, *added.shape[2:]), ('z', 'core', 'shard'...  7.44 us
    unnamed x22, local copies, waits for them, and re-layouts  6.59 us
    all_to_all x1, starting transfers between devices, over_z(): lax.all_to_all(flat, MESH, 0, 0, axis_index_groups=groups, tiled=True)  5.54 us
    pallas_call x1, Pallas kernels, add_high(): pl.pallas_call(functools.partial(add_high_body, n), out_shape=jax.ShapeDt...  4.7 us
  transfers between devices with their start and end apart: 15, of which 7 were waited for; matrix products, arithmetic and copies ran while one was open for 4% of the time, Pallas kernels for 7%

profile of v3, /device:TPU:0, one launch (start us, length us, event | category | flops | bytes accessed | tf_op | source)
XLA Modules:
  0.0 154.0 jit_solution(2305028405301834847)
XLA Ops:
  0.0 7.9 %pack.1 = (bf16[4,2,2,64,2048]{4,3,2,1,0:T(8,128)(2,1)}, bf16[8,2,16,2048]{3,2,1,0:T(8,128)(2,1)}, bf16[8,2,16,2048]{3,2,1,0:T(8,128)(2,1)}, bf16[8,2,16,2048]{3,2,1,0:T(8,128)(2,1)}, bf16[8,2,16,2048]{3,2,1,0:T(8,128)(2,1)}) custom-call(s32[8,32]{1,0:T(8,128)} %bitcast.23, s32[8,32]{1,0:T(8,128)} %bitcast.24, bf16[8,256,2048]{2,1,0:T(8,128)(2,1)} %bitcast.20, ...), custom_call_target="tpu_custom_call" | custom-call | tf_op jit(solution)/shard_map/pack/pallas_call | solution.py:74
  7.9 5.5 %all-to-all-start = ((bf16[8,2,64,2048]{3,2,1,0:T(8,128)(2,1)}), bf16[8,2,64,2048]{3,2,1,0:T(8,128)(2,1)}, u32[]{:S(2)}, u32[]{:S(2)}) async-start(bf16[8,2,64,2048]{3,2,1,0:T(8,128)(2,1)} %bitcast.22), calls=%async_computation | async-start | bytes 8388608 | tf_op jit(solution)/shard_map/all_to_all | solution.py:266
  13.4 6.2 %collective-permute-start.1 = (bf16[8,2,16,2048]{3,2,1,0:T(8,128)(2,1)}, bf16[8,2,16,2048]{3,2,1,0:T(8,128)(2,1)S(1)}, u32[]{:S(2)}, u32[]{:S(2)}) collective-permute-start(bf16[8,2,16,2048]{3,2,1,0:T(8,128)(2,1)} %get-tuple-element.31), channel_id=1, source_target_pairs={{0,8},{4,12},{8,0},{12,4},{1,9},{5,13},{9,1},{13,5},{2,10},{6,14},... | collective-permute-start | bytes 3145736 | tf_op jit(solution)/shard_map/ppermute | solution.py:249
  19.7 2.0 %collective-permute-start = (bf16[8,2,16,2048]{3,2,1,0:T(8,128)(2,1)}, bf16[8,2,16,2048]{3,2,1,0:T(8,128)(2,1)}, u32[]{:S(2)}, u32[]{:S(2)}) collective-permute-start(bf16[8,2,16,2048]{3,2,1,0:T(8,128)(2,1)} %get-tuple-element.30), channel_id=1, source_target_pairs={{0,4},{4,8},{8,12},{12,0},{1,5},{5,9},{9,13},{13,1},{2,6},{6,10},{... | collective-permute-start | bytes 3145736 | tf_op jit(solution)/shard_map/ppermute | solution.py:249
  21.7 1.1 slice.21
  22.8 1.3 dynamic-slice_bitcast_fusion
  24.0 2.8 %collective-permute-start.5 = (bf16[2,2,64,512]{3,2,1,0:T(8,128)(2,1)S(1)}, bf16[2,2,64,512]{3,2,1,0:T(8,128)(2,1)S(1)}, u32[]{:S(2)}, u32[]{:S(2)}) collective-permute-start(bf16[2,2,64,512]{3,2,1,0:T(8,128)(2,1)S(1)} %get-tuple-element.54), channel_id=1, source_target_pairs={{0,3},{1,0},{2,1},{3,2},{4,7},{5,4},{6,5},{7,6},{8,11},{9,8},{10,9... | collective-permute-start | bytes 786440 | tf_op jit(solution)/shard_map/ppermute | solution.py:249
  26.9 0.8 collective-permute-start.4
  27.7 9.9 %collective-permute-done.5.rest_6_ = bf16[2,2,64,512]{3,2,1,0:T(8,128)(2,1)S(1)} collective-permute-done((bf16[2,2,64,512]{3,2,1,0:T(8,128)(2,1)S(1)}, bf16[2,2,64,512]{3,2,1,0:T(8,128)(2,1)S(1)}, u32[]{:S(2)}, u32[]{:S(2)}) %collective-permute-start.5) | collective-permute-done | bytes 262176 | tf_op jit(solution)/shard_map/ppermute | solution.py:249
  38.3 24.9 %all-to-all-done = bf16[8,2,64,2048]{3,2,1,0:T(8,128)(2,1)} async-done(((bf16[8,2,64,2048]{3,2,1,0:T(8,128)(2,1)}), bf16[8,2,64,2048]{3,2,1,0:T(8,128)(2,1)}, u32[]{:S(2)}, u32[]{:S(2)}) %all-to-all-start) | async-done | bytes 4194336 | tf_op jit(solution)/shard_map/all_to_all | solution.py:266
  63.2 3.7 %fusion = (bf16[2,2,64,2048]{3,2,1,0:T(8,128)(2,1)}, bf16[2,2,64,2048]{3,2,1,0:T(8,128)(2,1)}, bf16[2,2,64,2048]{3,2,1,0:T(8,128)(2,1)}) fusion(bf16[8,2,64,2048]{3,2,1,0:T(8,128)(2,1)} %all-to-all-done), kind=kLoop, calls=%fused_computation.4 | loop fusion | bytes 6291456 | tf_op jit(solution)/shard_map/slice | solution.py:280
  66.9 0.7 copy-done.7
  68.4 1.3 collective-permute-start.6
  69.7 4.4 %collective-permute-start.7 = (bf16[2,2,64,2048]{3,2,1,0:T(8,128)(2,1)}, bf16[2,2,64,2048]{3,2,1,0:T(8,128)(2,1)}, u32[]{:S(2)}, u32[]{:S(2)}) collective-permute-start(bf16[2,2,64,2048]{3,2,1,0:T(8,128)(2,1)} %get-tuple-element.39), channel_id=1, source_target_pairs={{0,8},{4,12},{8,0},{12,4},{1,9},{5,13},{9,1},{13,5},{2,10},{6,14},... | collective-permute-start | bytes 3145736 | tf_op jit(solution)/shard_map/ppermute | solution.py:249
  74.1 4.7 %add_high.1 = bf16[8,4,2,2,16,512]{5,4,3,2,1,0:T(8,128)(2,1)} custom-call(bf16[8,2,16,2048]{3,2,1,0:T(8,128)(2,1)S(1)} %copy-done.2, bf16[8,2,16,2048]{3,2,1,0:T(8,128)(2,1)} %collective-permute-done.refs_1_, bf16[8,2,16,2048]{3,2,1,0:T(8,128)(2,1)S(1)} %collective-permute-done.1.refs_2_, bf16[8,2,16,2048]{3,2,1,0:T(8,128)(2,1)} %collective-permute-done.2.refs_3_), custom_call_target="tpu_custom_call" | custom-call | tf_op jit(solution)/shard_map/add_high/pallas_call | solution.py:156
  78.8 7.4 %all-to-all-start.1 = ((bf16[32,2,2,16,512]{4,3,2,1,0:T(8,128)(2,1)}), bf16[32,2,2,16,512]{4,3,2,1,0:T(8,128)(2,1)}, u32[]{:S(2)}, u32[]{:S(2)}) async-start(bf16[32,2,2,16,512]{4,3,2,1,0:T(8,128)(2,1)} %bitcast.10), calls=%async_computation.1 | async-start | bytes 4194304 | tf_op jit(solution)/shard_map/all_to_all | solution.py:290
  86.3 9.7 %collective-permute-done.6.refs_0_.rest_0_ = bf16[2,2,64,2048]{3,2,1,0:T(8,128)(2,1)S(1)} collective-permute-done((bf16[2,2,64,2048]{3,2,1,0:T(8,128)(2,1)}, bf16[2,2,64,2048]{3,2,1,0:T(8,128)(2,1)S(1)}, u32[]{:S(2)}, u32[]{:S(2)}) %collective-permute-start.6) | collective-permute-done | bytes 1048608 | tf_op jit(solution)/shard_map/ppermute | solution.py:249
  95.9 23.6 %collective-permute-done.7.refs_1_.rest_1_ = bf16[2,2,64,2048]{3,2,1,0:T(8,128)(2,1)} collective-permute-done((bf16[2,2,64,2048]{3,2,1,0:T(8,128)(2,1)}, bf16[2,2,64,2048]{3,2,1,0:T(8,128)(2,1)}, u32[]{:S(2)}, u32[]{:S(2)}) %collective-permute-start.7) | collective-permute-done | bytes 1048608 | tf_op jit(solution)/shard_map/ppermute | solution.py:249
  120.1 3.8 %all-to-all-start.2 = ((bf16[4,2,4,2,2,16,512]{6,5,4,3,2,1,0:T(8,128)(2,1)}), bf16[4,2,4,2,2,16,512]{6,5,4,3,2,1,0:T(8,128)(2,1)S(1)}, u32[]{:S(2)}, u32[]{:S(2)}) async-start(bf16[4,2,4,2,2,16,512]{6,5,4,3,2,1,0:T(8,128)(2,1)} %bitcast.11), calls=%async_computation.2 | async-start | bytes 4194304 | tf_op jit(solution)/shard_map/all_to_all | solution.py:294
  123.8 0.9 copy-done.6
  124.8 0.9 copy-done.8
  125.7 0.9 copy-done.10
  126.7 4.5 %merge_low.1 = (bf16[2,2,64,512]{3,2,1,0:T(8,128)(2,1)S(1)}, bf16[2,2,64,512]{3,2,1,0:T(8,128)(2,1)S(1)}, bf16[2,2,64,512]{3,2,1,0:T(8,128)(2,1)S(1)}, bf16[2,2,64,512]{3,2,1,0:T(8,128)(2,1)S(1)}) custom-call(s32[1]{0:T(128)} %fence.1.passed.rest_1_, bf16[4,2,2,64,2048]{4,3,2,1,0:T(8,128)(2,1)} %bitcast.12.first, bf16[2,2,64,2048]{3,2,1,0:T(8,128)(2,1)S(1)} %copy-done.4, ...), custom_call_target="tpu_custom_call" | custom-call | flops 99999997952 | tf_op jit(solution)/shard_map/merge_low/pallas_call | solution.py:126
  131.2 1.6 %collective-permute-start.9 = (bf16[2,2,64,512]{3,2,1,0:T(8,128)(2,1)S(1)}, bf16[2,2,64,512]{3,2,1,0:T(8,128)(2,1)S(1)}, u32[]{:S(2)}, u32[]{:S(2)}) collective-permute-start(bf16[2,2,64,512]{3,2,1,0:T(8,128)(2,1)S(1)} %get-tuple-element.48), channel_id=1, source_target_pairs={{0,1},{1,2},{2,3},{3,0},{4,5},{5,6},{6,7},{7,4},{8,9},{9,10},{10,1... | collective-permute-start | bytes 786440 | tf_op jit(solution)/shard_map/ppermute | solution.py:249
  132.7 2.7 %collective-permute-start.10 = (bf16[2,2,64,512]{3,2,1,0:T(8,128)(2,1)S(1)}, bf16[2,2,64,512]{3,2,1,0:T(8,128)(2,1)S(1)}, u32[]{:S(2)}, u32[]{:S(2)}) collective-permute-start(bf16[2,2,64,512]{3,2,1,0:T(8,128)(2,1)S(1)} %get-tuple-element.49), channel_id=1, source_target_pairs={{0,2},{1,3},{2,0},{3,1},{4,6},{5,7},{6,4},{7,5},{8,10},{9,11},{10,... | collective-permute-start | bytes 786440 | tf_op jit(solution)/shard_map/ppermute | solution.py:249
  135.5 1.4 collective-permute-start.11
  136.9 3.8 %collective-permute-done.9.refs_1_ = bf16[2,2,64,512]{3,2,1,0:T(8,128)(2,1)S(1)} collective-permute-done((bf16[2,2,64,512]{3,2,1,0:T(8,128)(2,1)S(1)}, bf16[2,2,64,512]{3,2,1,0:T(8,128)(2,1)S(1)}, u32[]{:S(2)}, u32[]{:S(2)}) %collective-permute-start.9) | collective-permute-done | bytes 262176 | tf_op jit(solution)/shard_map/ppermute | solution.py:249
  140.7 6.1 %collective-permute-done.10.refs_2_ = bf16[2,2,64,512]{3,2,1,0:T(8,128)(2,1)S(1)} collective-permute-done((bf16[2,2,64,512]{3,2,1,0:T(8,128)(2,1)S(1)}, bf16[2,2,64,512]{3,2,1,0:T(8,128)(2,1)S(1)}, u32[]{:S(2)}, u32[]{:S(2)}) %collective-permute-start.10) | collective-permute-done | bytes 262176 | tf_op jit(solution)/shard_map/ppermute | solution.py:249
  146.8 1.0 place.1.rest_0_
  147.8 2.3 %all-to-all-done.2.got = bf16[4,2,4,2,2,16,512]{6,5,4,3,2,1,0:T(8,128)(2,1)S(1)} async-done(((bf16[4,2,4,2,2,16,512]{6,5,4,3,2,1,0:T(8,128)(2,1)}), bf16[4,2,4,2,2,16,512]{6,5,4,3,2,1,0:T(8,128)(2,1)S(1)}, u32[]{:S(2)}, u32[]{:S(2)}) %all-to-all-start.2) | async-done | bytes 2097184 | tf_op jit(solution)/shard_map/all_to_all | solution.py:294
  150.1 1.6 %copy-done.1 = bf16[1,2048,512]{2,1,0:T(8,128)(2,1)S(1)} copy-done((bf16[1,2048,512]{2,1,0:T(8,128)(2,1)S(1)}, bf16[1,2048,512]{2,1,0:T(8,128)(2,1)}, u32[]{:S(2)}) %copy-start.1) | copy-done | bytes 2097176
  151.7 2.3 %merge_high.1 = bf16[2,4,2,128,512]{4,3,2,1,0:T(8,128)(2,1)} custom-call(bf16[4,2,4,2,2,16,512]{6,5,4,3,2,1,0:T(8,128)(2,1)S(1)} %all-to-all-done.2.got, bf16[2,4,2,128,512]{4,3,2,1,0:T(8,128)(2,1)S(1)} %bitcast.19, bf16[2,4,2,128,512]{4,3,2,1,0:T(8,128)(2,1)} %place.1.rest_0_, s32[1]{0:T(128)} %fence.1.passed.rest_1_), custom_call_target="tpu_custom_call", output_to_operand_aliasing={{}: (2, {})} | custom-call | tf_op jit(solution)/shard_map/merge_high/pallas_call | solution.py:214
  (29 shorter events, 2.0 us)
Async XLA Ops:
  7.9 13.8 %copy-start = (bf16[1,2048,512]{2,1,0:T(8,128)(2,1)S(1)}, bf16[1,2048,512]{2,1,0:T(8,128)(2,1)}, u32[]{:S(2)}) copy-start(bf16[1,2048,512]{2,1,0:T(8,128)(2,1)} %param.7) | copy-start | bytes 6291460
  7.9 55.3 %all-to-all-start = ((bf16[8,2,64,2048]{3,2,1,0:T(8,128)(2,1)}), bf16[8,2,64,2048]{3,2,1,0:T(8,128)(2,1)}, u32[]{:S(2)}, u32[]{:S(2)}) async-start(bf16[8,2,64,2048]{3,2,1,0:T(8,128)(2,1)} %bitcast.22), calls=%async_computation | async-start | bytes 8388608 | tf_op jit(solution)/shard_map/all_to_all | solution.py:266
  13.4 54.9 %collective-permute-start.1 = (bf16[8,2,16,2048]{3,2,1,0:T(8,128)(2,1)}, bf16[8,2,16,2048]{3,2,1,0:T(8,128)(2,1)S(1)}, u32[]{:S(2)}, u32[]{:S(2)}) collective-permute-start(bf16[8,2,16,2048]{3,2,1,0:T(8,128)(2,1)} %get-tuple-element.31), channel_id=1, source_target_pairs={{0,8},{4,12},{8,0},{12,4},{1,9},{5,13},{9,1},{13,5},{2,10},{6,14},... | collective-permute-start | bytes 3145736 | tf_op jit(solution)/shard_map/ppermute | solution.py:249
  19.7 48.7 %collective-permute-start.2 = (bf16[8,2,16,2048]{3,2,1,0:T(8,128)(2,1)}, bf16[8,2,16,2048]{3,2,1,0:T(8,128)(2,1)}, u32[]{:S(2)}, u32[]{:S(2)}) collective-permute-start(bf16[8,2,16,2048]{3,2,1,0:T(8,128)(2,1)} %get-tuple-element.32), channel_id=1, source_target_pairs={{0,12},{4,0},{8,4},{12,8},{1,13},{5,1},{9,5},{13,9},{2,14},{6,2},{... | collective-permute-start | bytes 3145736 | tf_op jit(solution)/shard_map/ppermute | solution.py:249
  19.7 48.7 %collective-permute-start = (bf16[8,2,16,2048]{3,2,1,0:T(8,128)(2,1)}, bf16[8,2,16,2048]{3,2,1,0:T(8,128)(2,1)}, u32[]{:S(2)}, u32[]{:S(2)}) collective-permute-start(bf16[8,2,16,2048]{3,2,1,0:T(8,128)(2,1)} %get-tuple-element.30), channel_id=1, source_target_pairs={{0,4},{4,8},{8,12},{12,0},{1,5},{5,9},{9,13},{13,1},{2,6},{6,10},{... | collective-permute-start | bytes 3145736 | tf_op jit(solution)/shard_map/ppermute | solution.py:249
  24.0 13.5 %collective-permute-start.5 = (bf16[2,2,64,512]{3,2,1,0:T(8,128)(2,1)S(1)}, bf16[2,2,64,512]{3,2,1,0:T(8,128)(2,1)S(1)}, u32[]{:S(2)}, u32[]{:S(2)}) collective-permute-start(bf16[2,2,64,512]{3,2,1,0:T(8,128)(2,1)S(1)} %get-tuple-element.54), channel_id=1, source_target_pairs={{0,3},{1,0},{2,1},{3,2},{4,7},{5,4},{6,5},{7,6},{8,11},{9,8},{10,9... | collective-permute-start | bytes 786440 | tf_op jit(solution)/shard_map/ppermute | solution.py:249
  26.9 40.0 %collective-permute-start.4 = (bf16[2,2,64,512]{3,2,1,0:T(8,128)(2,1)S(1)}, bf16[2,2,64,512]{3,2,1,0:T(8,128)(2,1)S(1)}, u32[]{:S(2)}, u32[]{:S(2)}) collective-permute-start(bf16[2,2,64,512]{3,2,1,0:T(8,128)(2,1)S(1)} %get-tuple-element.55), channel_id=1, source_target_pairs={{0,2},{1,3},{2,0},{3,1},{4,6},{5,7},{6,4},{7,5},{8,10},{9,11},{10,... | collective-permute-start | bytes 786440 | tf_op jit(solution)/shard_map/ppermute | solution.py:249
  37.6 0.7 copy-start.5
  38.3 35.8 %copy-start.2 = (bf16[8,2,16,2048]{3,2,1,0:T(8,128)(2,1)S(1)}, bf16[8,2,16,2048]{3,2,1,0:T(8,128)(2,1)}, u32[]{:S(2)}) copy-start(bf16[8,2,16,2048]{3,2,1,0:T(8,128)(2,1)} %get-tuple-element.34.refs_0_) | copy-start | bytes 3145732
  38.3 29.4 %collective-permute-start.3 = (bf16[2,2,64,512]{3,2,1,0:T(8,128)(2,1)S(1)}, bf16[2,2,64,512]{3,2,1,0:T(8,128)(2,1)S(1)}, u32[]{:S(2)}, u32[]{:S(2)}) collective-permute-start(bf16[2,2,64,512]{3,2,1,0:T(8,128)(2,1)S(1)} %get-tuple-element.56), channel_id=1, source_target_pairs={{0,1},{1,2},{2,3},{3,0},{4,5},{5,6},{6,7},{7,4},{8,9},{9,10},{10,1... | collective-permute-start | bytes 786440 | tf_op jit(solution)/shard_map/ppermute | solution.py:249
  66.9 0.7 copy-start.7
  67.6 0.7 copy-start.9
  68.4 27.6 %collective-permute-start.6 = (bf16[2,2,64,2048]{3,2,1,0:T(8,128)(2,1)}, bf16[2,2,64,2048]{3,2,1,0:T(8,128)(2,1)S(1)}, u32[]{:S(2)}, u32[]{:S(2)}) collective-permute-start(bf16[2,2,64,2048]{3,2,1,0:T(8,128)(2,1)} %get-tuple-element.38), channel_id=1, source_target_pairs={{0,4},{4,8},{8,12},{12,0},{1,5},{5,9},{9,13},{13,1},{2,6},{6,10},{... | collective-permute-start | bytes 3145736 | tf_op jit(solution)/shard_map/ppermute | solution.py:249
  69.7 49.8 %collective-permute-start.7 = (bf16[2,2,64,2048]{3,2,1,0:T(8,128)(2,1)}, bf16[2,2,64,2048]{3,2,1,0:T(8,128)(2,1)}, u32[]{:S(2)}, u32[]{:S(2)}) collective-permute-start(bf16[2,2,64,2048]{3,2,1,0:T(8,128)(2,1)} %get-tuple-element.39), channel_id=1, source_target_pairs={{0,8},{4,12},{8,0},{12,4},{1,9},{5,13},{9,1},{13,5},{2,10},{6,14},... | collective-permute-start | bytes 3145736 | tf_op jit(solution)/shard_map/ppermute | solution.py:249
  74.0 45.5 %collective-permute-start.8 = (bf16[2,2,64,2048]{3,2,1,0:T(8,128)(2,1)}, bf16[2,2,64,2048]{3,2,1,0:T(8,128)(2,1)}, u32[]{:S(2)}, u32[]{:S(2)}) collective-permute-start(bf16[2,2,64,2048]{3,2,1,0:T(8,128)(2,1)} %get-tuple-element.40), channel_id=1, source_target_pairs={{0,12},{4,0},{8,4},{12,8},{1,13},{5,1},{9,5},{13,9},{2,14},{6,2},{... | collective-permute-start | bytes 3145736 | tf_op jit(solution)/shard_map/ppermute | solution.py:249
  78.8 41.2 %all-to-all-start.1 = ((bf16[32,2,2,16,512]{4,3,2,1,0:T(8,128)(2,1)}), bf16[32,2,2,16,512]{4,3,2,1,0:T(8,128)(2,1)}, u32[]{:S(2)}, u32[]{:S(2)}) async-start(bf16[32,2,2,16,512]{4,3,2,1,0:T(8,128)(2,1)} %bitcast.10), calls=%async_computation.1 | async-start | bytes 4194304 | tf_op jit(solution)/shard_map/all_to_all | solution.py:290
  95.9 24.1 %copy-start.3 = (bf16[2,2,64,2048]{3,2,1,0:T(8,128)(2,1)}, bf16[2,2,64,2048]{3,2,1,0:T(8,128)(2,1)S(1)}, u32[]{:S(2)}) copy-start(bf16[2,2,64,2048]{3,2,1,0:T(8,128)(2,1)S(1)} %collective-permute-done.6.refs_0_.rest_0_) | copy-start | bytes 3145732
  120.1 3.8 %copy-start.4 = (bf16[2,2,64,2048]{3,2,1,0:T(8,128)(2,1)S(1)}, bf16[2,2,64,2048]{3,2,1,0:T(8,128)(2,1)}, u32[]{:S(2)}) copy-start(bf16[2,2,64,2048]{3,2,1,0:T(8,128)(2,1)} %copy-done.3) | copy-start | bytes 3145732
  120.1 30.1 %all-to-all-start.2 = ((bf16[4,2,4,2,2,16,512]{6,5,4,3,2,1,0:T(8,128)(2,1)}), bf16[4,2,4,2,2,16,512]{6,5,4,3,2,1,0:T(8,128)(2,1)S(1)}, u32[]{:S(2)}, u32[]{:S(2)}) async-start(bf16[4,2,4,2,2,16,512]{6,5,4,3,2,1,0:T(8,128)(2,1)} %bitcast.11), calls=%async_computation.2 | async-start | bytes 4194304 | tf_op jit(solution)/shard_map/all_to_all | solution.py:294
  123.8 1.0 copy-start.6
  124.8 0.9 copy-start.8
  125.7 0.9 copy-start.10
  131.2 9.5 %collective-permute-start.9 = (bf16[2,2,64,512]{3,2,1,0:T(8,128)(2,1)S(1)}, bf16[2,2,64,512]{3,2,1,0:T(8,128)(2,1)S(1)}, u32[]{:S(2)}, u32[]{:S(2)}) collective-permute-start(bf16[2,2,64,512]{3,2,1,0:T(8,128)(2,1)S(1)} %get-tuple-element.48), channel_id=1, source_target_pairs={{0,1},{1,2},{2,3},{3,0},{4,5},{5,6},{6,7},{7,4},{8,9},{9,10},{10,1... | collective-permute-start | bytes 786440 | tf_op jit(solution)/shard_map/ppermute | solution.py:249
  132.7 14.1 %collective-permute-start.10 = (bf16[2,2,64,512]{3,2,1,0:T(8,128)(2,1)S(1)}, bf16[2,2,64,512]{3,2,1,0:T(8,128)(2,1)S(1)}, u32[]{:S(2)}, u32[]{:S(2)}) collective-permute-start(bf16[2,2,64,512]{3,2,1,0:T(8,128)(2,1)S(1)} %get-tuple-element.49), channel_id=1, source_target_pairs={{0,2},{1,3},{2,0},{3,1},{4,6},{5,7},{6,4},{7,5},{8,10},{9,11},{10,... | collective-permute-start | bytes 786440 | tf_op jit(solution)/shard_map/ppermute | solution.py:249
  135.5 11.3 %collective-permute-start.11 = (bf16[2,2,64,512]{3,2,1,0:T(8,128)(2,1)S(1)}, bf16[2,2,64,512]{3,2,1,0:T(8,128)(2,1)S(1)}, u32[]{:S(2)}, u32[]{:S(2)}) collective-permute-start(bf16[2,2,64,512]{3,2,1,0:T(8,128)(2,1)S(1)} %get-tuple-element.50), channel_id=1, source_target_pairs={{0,3},{1,0},{2,1},{3,2},{4,7},{5,4},{6,5},{7,6},{8,11},{9,8},{10,9... | collective-permute-start | bytes 786440 | tf_op jit(solution)/shard_map/ppermute | solution.py:249
  150.1 1.6 %copy-start.1 = (bf16[1,2048,512]{2,1,0:T(8,128)(2,1)S(1)}, bf16[1,2048,512]{2,1,0:T(8,128)(2,1)}, u32[]{:S(2)}) copy-start(bf16[1,2048,512]{2,1,0:T(8,128)(2,1)} %param.7) | copy-start | bytes 6291460

commit v4 on v3

--- a/solution.py
+++ b/solution.py
@@ -32,58 +32,63 @@
     return tile * TILE, sign.astype(jnp.bfloat16)
 
 
-def pack_body(tiles, counts, weights, fisher, low, *rest):
-    high, (held, came, sent) = rest[:-3], rest[-3:]
-    n, rows = len(high), high[0].shape[2]
+def pack_body(start, rows, shifts, after, tiles, counts, weights, fisher, *refs):
+    outs, (token, held, came, sent) = refs[after:-4], refs[-4:]
+    token[0] = 0
+    n = held.shape[0]
     y = lax.axis_index("task")
-    reads, signs, experts = [], [], []
+    reads = []
     for j in range(n):
+        first = lax.rem(y + j, n) * 2
         for ec in range(2):
-            e = lax.rem(y + j, n) * 2 + ec
-            row, sign = listed(tiles, counts, e)
-            at = pl.ds(pl.multiple_of(row, TILE), TILE)
+            row, sign = listed(tiles, counts, first + ec)
+            if len(shifts) == 1:
+                row = row + lax.rem(y + shifts[0], n) * rows
+            at = pl.ds(pl.multiple_of(row + start, 8), held.shape[3])
             for a, src in enumerate((weights, fisher)):
-                i = len(reads)
-                reads.append(pltpu.make_async_copy(src.at[e, at], held.at[i], came.at[i]))
-                signs.append(sign if a else None)
-                experts.append(e)
-    for read in reads:
-        read.start()
+                read = pltpu.make_async_copy(
+                    src.at[first + ec, at], held.at[j, ec, a], came.at[len(reads)]
+                )
+                reads.append((read, sign))
+                read.start()
     writes = []
-    for i, read in enumerate(reads):
-        read.wait()
-        if signs[i] is not None:
-            held[i] = held[i] * signs[i]
-        at = low.at[i // 4, i // 2 % 2, i % 2]
-        parts = [(pl.ds(0, LOW), at)]
-        for d in range(n):
-            row = pl.multiple_of(LOW + lax.rem(y + d, n) * rows, 8)
-            parts.append((pl.ds(row, rows), high[d].at[experts[i], i % 2]))
+    for j in range(n):
+        first = lax.rem(y + j, n) * 2
+        for ec in range(2):
+            (read, _), (read_fisher, sign) = reads[4 * j + 2 * ec : 4 * j + 2 * ec + 2]
+            read.wait()
+            read_fisher.wait()
+            held[j, ec, 1] = held[j, ec, 1] * sign
+        parts = [(held.at[j], outs[0].at[j])] if not shifts else []
+        for d, out in zip(shifts, outs):
+            row = pl.multiple_of(lax.rem(y + d, n) * rows, 8) if len(shifts) > 1 else 0
+            parts.append((held.at[j, :, :, pl.ds(row, rows)], out.at[pl.ds(first, 2)]))
         for src, dst in parts:
-            k = len(writes)
-            writes.append(pltpu.make_async_copy(held.at[i, src], dst, sent.at[k]))
-            writes[-1].start()
+            write = pltpu.make_async_copy(src, dst, sent.at[len(writes)])
+            writes.append(write)
+            write.start()
     for write in writes:
         write.wait()
 
 
-def pack(tiles, counts, weights, fisher, n):
+def pack(tiles, counts, weights, fisher, n, start, rows, shifts, after):
     experts, _, cols = weights.shape
-    rows = (TILE - LOW) // n
-    count = 2 * experts
-    return pl.pallas_call(
-        pack_body,
-        out_shape=[jax.ShapeDtypeStruct((n, 2, 2, LOW, cols), weights.dtype)]
-        + [jax.ShapeDtypeStruct((experts, 2, rows, cols), weights.dtype)] * n,
-        in_specs=[SMEM, SMEM, HBM, HBM],
-        out_specs=[HBM] * (n + 1),
+    read = n * rows if len(shifts) > 1 else rows
+    shape = (experts, 2, rows, cols) if shifts else (n, 2, 2, rows, cols)
+    count = max(len(shifts), 1)
+    return pl.pallas_call(
+        functools.partial(pack_body, start, rows, shifts, len(after)),
+        out_shape=[jax.ShapeDtypeStruct(shape, weights.dtype)] * count
+        + [jax.ShapeDtypeStruct((1,), jnp.int32)],
+        in_specs=[SMEM, SMEM, HBM, HBM] + [SMEM] * len(after),
+        out_specs=[HBM] * count + [SMEM],
         scratch_shapes=[
-            pltpu.VMEM((count, TILE, cols), weights.dtype),
-            pltpu.SemaphoreType.DMA((count,)),
-            pltpu.SemaphoreType.DMA((count * (n + 1),)),
+            pltpu.VMEM((n, 2, 2, read, cols), weights.dtype),
+            pltpu.SemaphoreType.DMA((2 * experts,)),
+            pltpu.SemaphoreType.DMA((n * count,)),
         ],
         name="pack",
-    )(tiles, counts, weights, fisher)
+    )(tiles, counts, weights, fisher, *after)
 
 
 def sums(loads):
@@ -223,7 +228,6 @@
         ],
         out_specs=part,
         input_output_aliases={2: 0},
-        compiler_params=PARAMS,
         name="merge_high",
     )(got, base, whole, passed)
 
@@ -274,7 +278,13 @@
     hold = lax.optimization_barrier
 
     tiles, counts = tile_list[0, :, :, 0], tile_count[0]
-    low, *high = pack(tiles, counts, weights, fisher, nz)
+    rows = (TILE - LOW) // ny
+    args = (tiles, counts, weights, fisher, nz)
+    low, token = pack(*args, 0, LOW, (), ())
+    high_2, token = pack(*args, LOW, rows, (2,), (token,))
+    high_1, high_3, high_0, _ = pack(*args, LOW, rows, (1, 3, 0), (token,))
+    high = [high_0, high_1, high_2, high_3]
+
     got_low = over_z(low)
     got_high = [high[0]] + all_shifted(high, "task")
     mine = [got_low[m] for m in range(1, ny)]
@@ -290,7 +300,7 @@
     moved = lax.all_to_all(
         added.reshape(-1, *added.shape[2:]), ("z", "core", "shard"), 0, 0, tiled=True
     )
-    moved, passed = hold((moved, fence(others)))
+    moved, passed = hold((moved, fence(others[1:2])))
     moved = lax.all_to_all(
         moved.reshape(nz, 2, nx, *moved.shape[1:]), "task", 0, 0, tiled=True
     )

time: 155 us -> 143 us (0.923)
  waiting for transfers between devices: 80.3 us -> 68.7 us
  Pallas kernels: 20.8 us -> 28.3 us
  local copies, waits for them, and re-layouts: 12.6 us -> 6.57 us
  starting transfers between devices: 40.1 us -> 38.5 us
    ppermute x12, waiting for transfers between devices: 53.1 us -> 41.2 us  [shifted(): return lax.ppermute(x, axis, [(i, (i + by) % n) for i in range(n)])]
    all_to_all x1, waiting for transfers between devices: 0.01 us -> 11.1 us  [local(): lax.all_to_all(added.reshape(-1, *added.shape[2:]), ('z', 'core', 'shard'...]
    all_to_all x1, waiting for transfers between devices: 24.9 us -> 15.5 us  [over_z(): lax.all_to_all(flat, MESH, 0, 0, axis_index_groups=groups, tiled=True)]
    pallas_call x1 -> x3, Pallas kernels: 7.88 us -> 14.2 us  [pack(): pl.pallas_call(functools.partial(pack_body, start, rows, shifts, len(afte...]
    unnamed x22 -> x6, local copies, waits for them, and re-layouts: 6.59 us -> 0.71 us
    all_to_all x1, starting transfers between devices: 7.44 us -> 4.82 us  [local(): lax.all_to_all(added.reshape(-1, *added.shape[2:]), ('z', 'core', 'shard'...]
  transfers between devices with their start and end apart: 15 -> 15, of which waited for: 7 -> 10; matrix products, arithmetic and copies ran while one was open for 4% -> 4% of each run, Pallas kernels for 7% -> 14%
where the time goes in v4:
time: 143 us; the launch traced here: 142 us
  waiting for transfers between devices  68.7 us (48%)
  starting transfers between devices  38.5 us (27%)
  Pallas kernels  28.3 us (20%)
  local copies, waits for them, and re-layouts  6.57 us (5%)
    ppermute x12, waiting for transfers between devices, shifted(): return lax.ppermute(x, axis, [(i, (i + by) % n) for i in range(n)])  41.2 us
    ppermute x12, starting transfers between devices, shifted(): return lax.ppermute(x, axis, [(i, (i + by) % n) for i in range(n)])  23.7 us
    all_to_all x1, waiting for transfers between devices, over_z(): lax.all_to_all(flat, MESH, 0, 0, axis_index_groups=groups, tiled=True)  15.5 us
    pallas_call x3, Pallas kernels, pack(): pl.pallas_call(functools.partial(pack_body, start, rows, shifts, len(afte...  14.2 us
    all_to_all x1, waiting for transfers between devices, local(): lax.all_to_all(added.reshape(-1, *added.shape[2:]), ('z', 'core', 'shard'...  11.1 us
    all_to_all x1, starting transfers between devices, over_z(): lax.all_to_all(flat, MESH, 0, 0, axis_index_groups=groups, tiled=True)  5.41 us
    all_to_all x1, starting transfers between devices, local(): lax.all_to_all(added.reshape(-1, *added.shape[2:]), ('z', 'core', 'shard'...  4.82 us
    all_to_all x1, starting transfers between devices, local(): lax.all_to_all(moved.reshape(nz, 2, nx, *moved.shape[1:]), 'task', 0, 0,...  4.59 us
  transfers between devices with their start and end apart: 15, of which 10 were waited for; matrix products, arithmetic and copies ran while one was open for 4% of the time, Pallas kernels for 14%

profile of v4, /device:TPU:0, one launch (start us, length us, event | category | flops | bytes accessed | tf_op | source)
XLA Modules:
  0.0 142.3 jit_solution(8177592240305731472)
XLA Ops:
  0.0 4.8 %pack.3 = (bf16[4,2,2,64,2048]{4,3,2,1,0:T(8,128)(2,1)}, s32[1]{0:T(128)}) custom-call(s32[8,32]{1,0:T(8,128)} %bitcast.27, s32[8,32]{1,0:T(8,128)} %bitcast.30, bf16[8,256,2048]{2,1,0:T(8,128)(2,1)} %bitcast.18, bf16[8,256,2048]{2,1,0:T(8,128)(2,1)} %bitcast.21), custom_call_target="tpu_custom_call" | custom-call | tf_op jit(solution)/shard_map/pack/pallas_call | solution.py:79
  4.8 5.4 %all-to-all-start = ((bf16[8,2,64,2048]{3,2,1,0:T(8,128)(2,1)}), bf16[8,2,64,2048]{3,2,1,0:T(8,128)(2,1)}, u32[]{:S(2)}, u32[]{:S(2)}) async-start(bf16[8,2,64,2048]{3,2,1,0:T(8,128)(2,1)} %bitcast.26), calls=%async_computation | async-start | bytes 8388608 | tf_op jit(solution)/shard_map/all_to_all | solution.py:270
  10.2 4.1 %pack.4 = (bf16[8,2,16,2048]{3,2,1,0:T(8,128)(2,1)}, s32[1]{0:T(128)}) custom-call(s32[8,32]{1,0:T(8,128)} %bitcast.28, s32[8,32]{1,0:T(8,128)} %bitcast.31, bf16[8,256,2048]{2,1,0:T(8,128)(2,1)} %bitcast.19, bf16[8,256,2048]{2,1,0:T(8,128)(2,1)} %bitcast.22, s32[1]{0:T(128)} %get-tuple-element.31.refs_0_), custom_call_target="tpu_custom_call" | custom-call | tf_op jit(solution)/shard_map/pack/pallas_call | solution.py:79
  14.3 6.3 %collective-permute-start.1 = (bf16[8,2,16,2048]{3,2,1,0:T(8,128)(2,1)}, bf16[8,2,16,2048]{3,2,1,0:T(8,128)(2,1)S(1)}, u32[]{:S(2)}, u32[]{:S(2)}) collective-permute-start(bf16[8,2,16,2048]{3,2,1,0:T(8,128)(2,1)} %get-tuple-element.35), channel_id=1, source_target_pairs={{0,8},{4,12},{8,0},{12,4},{1,9},{5,13},{9,1},{13,5},{2,10},{6,14},... | collective-permute-start | bytes 3145736 | tf_op jit(solution)/shard_map/ppermute | solution.py:253
  20.6 5.4 %pack.5 = (bf16[8,2,16,2048]{3,2,1,0:T(8,128)(2,1)}, bf16[8,2,16,2048]{3,2,1,0:T(8,128)(2,1)}, bf16[8,2,16,2048]{3,2,1,0:T(8,128)(2,1)}, s32[1]{0:T(128)}) custom-call(s32[8,32]{1,0:T(8,128)} %bitcast.29, s32[8,32]{1,0:T(8,128)} %bitcast.32, bf16[8,256,2048]{2,1,0:T(8,128)(2,1)} %bitcast.20, bf16[8,256,2048]{2,1,0:T(8,128)(2,1)} %bitcast.23, ...), custom_call_target="tpu_custom_call" | custom-call | tf_op jit(solution)/shard_map/pack/pallas_call | solution.py:79
  26.0 2.0 %collective-permute-start = (bf16[8,2,16,2048]{3,2,1,0:T(8,128)(2,1)}, bf16[8,2,16,2048]{3,2,1,0:T(8,128)(2,1)}, u32[]{:S(2)}, u32[]{:S(2)}) collective-permute-start(bf16[8,2,16,2048]{3,2,1,0:T(8,128)(2,1)} %get-tuple-element.34), channel_id=1, source_target_pairs={{0,4},{4,8},{8,12},{12,0},{1,5},{5,9},{9,13},{13,1},{2,6},{6,10},{... | collective-permute-start | bytes 3145736 | tf_op jit(solution)/shard_map/ppermute | solution.py:253
  28.1 1.3 slice.21
  29.4 0.9 dynamic-slice_bitcast_fusion
  30.3 2.8 %collective-permute-start.5 = (bf16[2,2,64,512]{3,2,1,0:T(8,128)(2,1)S(1)}, bf16[2,2,64,512]{3,2,1,0:T(8,128)(2,1)S(1)}, u32[]{:S(2)}, u32[]{:S(2)}) collective-permute-start(bf16[2,2,64,512]{3,2,1,0:T(8,128)(2,1)S(1)} %get-tuple-element.58), channel_id=1, source_target_pairs={{0,3},{1,0},{2,1},{3,2},{4,7},{5,4},{6,5},{7,6},{8,11},{9,8},{10,9... | collective-permute-start | bytes 786440 | tf_op jit(solution)/shard_map/ppermute | solution.py:253
  33.9 9.9 %collective-permute-done.5.rest_6_ = bf16[2,2,64,512]{3,2,1,0:T(8,128)(2,1)S(1)} collective-permute-done((bf16[2,2,64,512]{3,2,1,0:T(8,128)(2,1)S(1)}, bf16[2,2,64,512]{3,2,1,0:T(8,128)(2,1)S(1)}, u32[]{:S(2)}, u32[]{:S(2)}) %collective-permute-start.5) | collective-permute-done | bytes 262176 | tf_op jit(solution)/shard_map/ppermute | solution.py:253
  44.5 15.5 %all-to-all-done = bf16[8,2,64,2048]{3,2,1,0:T(8,128)(2,1)} async-done(((bf16[8,2,64,2048]{3,2,1,0:T(8,128)(2,1)}), bf16[8,2,64,2048]{3,2,1,0:T(8,128)(2,1)}, u32[]{:S(2)}, u32[]{:S(2)}) %all-to-all-start) | async-done | bytes 4194336 | tf_op jit(solution)/shard_map/all_to_all | solution.py:270
  59.9 3.6 %fusion = (bf16[2,2,64,2048]{3,2,1,0:T(8,128)(2,1)}, bf16[2,2,64,2048]{3,2,1,0:T(8,128)(2,1)}, bf16[2,2,64,2048]{3,2,1,0:T(8,128)(2,1)}) fusion(bf16[8,2,64,2048]{3,2,1,0:T(8,128)(2,1)} %all-to-all-done), kind=kLoop, calls=%fused_computation.4 | loop fusion | bytes 6291456 | tf_op jit(solution)/shard_map/slice | solution.py:290
  63.6 3.7 %collective-permute-done.2.refs_3_ = bf16[8,2,16,2048]{3,2,1,0:T(8,128)(2,1)S(1)} collective-permute-done((bf16[8,2,16,2048]{3,2,1,0:T(8,128)(2,1)}, bf16[8,2,16,2048]{3,2,1,0:T(8,128)(2,1)S(1)}, u32[]{:S(2)}, u32[]{:S(2)}) %collective-permute-start.2) | collective-permute-done | bytes 1048608 | tf_op jit(solution)/shard_map/ppermute | solution.py:253
  67.3 2.8 %collective-permute-start.6 = (bf16[2,2,64,2048]{3,2,1,0:T(8,128)(2,1)}, bf16[2,2,64,2048]{3,2,1,0:T(8,128)(2,1)}, u32[]{:S(2)}, u32[]{:S(2)}) collective-permute-start(bf16[2,2,64,2048]{3,2,1,0:T(8,128)(2,1)} %get-tuple-element.42), channel_id=1, source_target_pairs={{0,8},{4,12},{8,0},{12,4},{1,9},{5,13},{9,1},{13,5},{2,10},{6,14},... | collective-permute-start | bytes 3145736 | tf_op jit(solution)/shard_map/ppermute | solution.py:253
  70.1 4.5 %add_high.1 = bf16[8,4,2,2,16,512]{5,4,3,2,1,0:T(8,128)(2,1)} custom-call(bf16[8,2,16,2048]{3,2,1,0:T(8,128)(2,1)S(1)} %copy-done, bf16[8,2,16,2048]{3,2,1,0:T(8,128)(2,1)} %collective-permute-done.refs_1_, bf16[8,2,16,2048]{3,2,1,0:T(8,128)(2,1)S(1)} %collective-permute-done.1.refs_2_, bf16[8,2,16,2048]{3,2,1,0:T(8,128)(2,1)S(1)} %collective-permute-done.2.refs_3_), custom_call_target="tpu_custom_call" | custom-call | tf_op jit(solution)/shard_map/add_high/pallas_call | solution.py:161
  74.6 4.8 %all-to-all-start.1 = ((bf16[32,2,2,16,512]{4,3,2,1,0:T(8,128)(2,1)}), bf16[32,2,2,16,512]{4,3,2,1,0:T(8,128)(2,1)}, u32[]{:S(2)}, u32[]{:S(2)}) async-start(bf16[32,2,2,16,512]{4,3,2,1,0:T(8,128)(2,1)} %bitcast.10), calls=%async_computation.1 | async-start | bytes 4194304 | tf_op jit(solution)/shard_map/all_to_all | solution.py:300
  79.4 1.7 %collective-permute-start.7 = (bf16[2,2,64,2048]{3,2,1,0:T(8,128)(2,1)}, bf16[2,2,64,2048]{3,2,1,0:T(8,128)(2,1)S(1)}, u32[]{:S(2)}, u32[]{:S(2)}) collective-permute-start(bf16[2,2,64,2048]{3,2,1,0:T(8,128)(2,1)} %get-tuple-element.45), channel_id=1, source_target_pairs={{0,4},{4,8},{8,12},{12,0},{1,5},{5,9},{9,13},{13,1},{2,6},{6,10},{... | collective-permute-start | bytes 3145736 | tf_op jit(solution)/shard_map/ppermute | solution.py:253
  81.1 1.6 %collective-permute-start.8 = (bf16[2,2,64,2048]{3,2,1,0:T(8,128)(2,1)}, bf16[2,2,64,2048]{3,2,1,0:T(8,128)(2,1)S(1)}, u32[]{:S(2)}, u32[]{:S(2)}) collective-permute-start(bf16[2,2,64,2048]{3,2,1,0:T(8,128)(2,1)} %get-tuple-element.46), channel_id=1, source_target_pairs={{0,12},{4,0},{8,4},{12,8},{1,13},{5,1},{9,5},{13,9},{2,14},{6,2},{... | collective-permute-start | bytes 3145736 | tf_op jit(solution)/shard_map/ppermute | solution.py:253
  82.7 12.5 %collective-permute-done.6.refs_0_.rest_1_ = bf16[2,2,64,2048]{3,2,1,0:T(8,128)(2,1)} collective-permute-done((bf16[2,2,64,2048]{3,2,1,0:T(8,128)(2,1)}, bf16[2,2,64,2048]{3,2,1,0:T(8,128)(2,1)}, u32[]{:S(2)}, u32[]{:S(2)}) %collective-permute-start.6) | collective-permute-done | bytes 1048608 | tf_op jit(solution)/shard_map/ppermute | solution.py:253
  95.8 11.1 %all-to-all-done.1 = bf16[32,2,2,16,512]{4,3,2,1,0:T(8,128)(2,1)} async-done(((bf16[32,2,2,16,512]{4,3,2,1,0:T(8,128)(2,1)}), bf16[32,2,2,16,512]{4,3,2,1,0:T(8,128)(2,1)}, u32[]{:S(2)}, u32[]{:S(2)}) %all-to-all-start.1) | async-done | bytes 2097184 | tf_op jit(solution)/shard_map/all_to_all | solution.py:300
  106.9 4.6 %all-to-all-start.2 = ((bf16[4,2,4,2,2,16,512]{6,5,4,3,2,1,0:T(8,128)(2,1)}), bf16[4,2,4,2,2,16,512]{6,5,4,3,2,1,0:T(8,128)(2,1)}, u32[]{:S(2)}, u32[]{:S(2)}) async-start(bf16[4,2,4,2,2,16,512]{6,5,4,3,2,1,0:T(8,128)(2,1)} %bitcast.11), calls=%async_computation.2 | async-start | bytes 4194304 | tf_op jit(solution)/shard_map/all_to_all | solution.py:304
  111.5 5.0 %collective-permute-done.7.rest_0_ = bf16[2,2,64,2048]{3,2,1,0:T(8,128)(2,1)S(1)} collective-permute-done((bf16[2,2,64,2048]{3,2,1,0:T(8,128)(2,1)}, bf16[2,2,64,2048]{3,2,1,0:T(8,128)(2,1)S(1)}, u32[]{:S(2)}, u32[]{:S(2)}) %collective-permute-start.7) | collective-permute-done | bytes 1048608 | tf_op jit(solution)/shard_map/ppermute | solution.py:253
  116.4 1.1 collective-permute-done.8.rest_2_
  117.5 4.4 %merge_low.1 = (bf16[2,2,64,512]{3,2,1,0:T(8,128)(2,1)S(1)}, bf16[2,2,64,512]{3,2,1,0:T(8,128)(2,1)S(1)}, bf16[2,2,64,512]{3,2,1,0:T(8,128)(2,1)S(1)}, bf16[2,2,64,512]{3,2,1,0:T(8,128)(2,1)S(1)}) custom-call(s32[1]{0:T(128)} %fence.1.passed.rest_1_, bf16[4,2,2,64,2048]{4,3,2,1,0:T(8,128)(2,1)} %bitcast.12.first, ...), custom_call_target="tpu_custom_call" | custom-call | flops 99999997952 | tf_op jit(solution)/shard_map/merge_low/pallas_call | solution.py:131
  121.9 1.6 %collective-permute-start.9 = (bf16[2,2,64,512]{3,2,1,0:T(8,128)(2,1)S(1)}, bf16[2,2,64,512]{3,2,1,0:T(8,128)(2,1)S(1)}, u32[]{:S(2)}, u32[]{:S(2)}) collective-permute-start(bf16[2,2,64,512]{3,2,1,0:T(8,128)(2,1)S(1)} %get-tuple-element.52), channel_id=1, source_target_pairs={{0,1},{1,2},{2,3},{3,0},{4,5},{5,6},{6,7},{7,4},{8,9},{9,10},{10,1... | collective-permute-start | bytes 786440 | tf_op jit(solution)/shard_map/ppermute | solution.py:253
  123.5 2.7 %collective-permute-start.10 = (bf16[2,2,64,512]{3,2,1,0:T(8,128)(2,1)S(1)}, bf16[2,2,64,512]{3,2,1,0:T(8,128)(2,1)S(1)}, u32[]{:S(2)}, u32[]{:S(2)}) collective-permute-start(bf16[2,2,64,512]{3,2,1,0:T(8,128)(2,1)S(1)} %get-tuple-element.53), channel_id=1, source_target_pairs={{0,2},{1,3},{2,0},{3,1},{4,6},{5,7},{6,4},{7,5},{8,10},{9,11},{10,... | collective-permute-start | bytes 786440 | tf_op jit(solution)/shard_map/ppermute | solution.py:253
  126.2 1.4 %collective-permute-start.11 = (bf16[2,2,64,512]{3,2,1,0:T(8,128)(2,1)S(1)}, bf16[2,2,64,512]{3,2,1,0:T(8,128)(2,1)S(1)}, u32[]{:S(2)}, u32[]{:S(2)}) collective-permute-start(bf16[2,2,64,512]{3,2,1,0:T(8,128)(2,1)S(1)} %get-tuple-element.54), channel_id=1, source_target_pairs={{0,3},{1,0},{2,1},{3,2},{4,7},{5,4},{6,5},{7,6},{8,11},{9,8},{10,9... | collective-permute-start | bytes 786440 | tf_op jit(solution)/shard_map/ppermute | solution.py:253
  127.7 3.8 %collective-permute-done.9.refs_1_ = bf16[2,2,64,512]{3,2,1,0:T(8,128)(2,1)S(1)} collective-permute-done((bf16[2,2,64,512]{3,2,1,0:T(8,128)(2,1)S(1)}, bf16[2,2,64,512]{3,2,1,0:T(8,128)(2,1)S(1)}, u32[]{:S(2)}, u32[]{:S(2)}) %collective-permute-start.9) | collective-permute-done | bytes 262176 | tf_op jit(solution)/shard_map/ppermute | solution.py:253
  131.5 5.2 %collective-permute-done.10.refs_2_ = bf16[2,2,64,512]{3,2,1,0:T(8,128)(2,1)S(1)} collective-permute-done((bf16[2,2,64,512]{3,2,1,0:T(8,128)(2,1)S(1)}, bf16[2,2,64,512]{3,2,1,0:T(8,128)(2,1)S(1)}, u32[]{:S(2)}, u32[]{:S(2)}) %collective-permute-start.10) | collective-permute-done | bytes 262176 | tf_op jit(solution)/shard_map/ppermute | solution.py:253
  136.7 1.0 place.1.rest_0_
  137.7 1.0 all-to-all-done.2.got
  138.7 3.6 %merge_high.1 = bf16[2,4,2,128,512]{4,3,2,1,0:T(8,128)(2,1)} custom-call(bf16[4,2,4,2,2,16,512]{6,5,4,3,2,1,0:T(8,128)(2,1)} %all-to-all-done.2.got, bf16[2,4,2,128,512]{4,3,2,1,0:T(8,128)(2,1)} %bitcast.25, bf16[2,4,2,128,512]{4,3,2,1,0:T(8,128)(2,1)} %place.1.rest_0_, s32[1]{0:T(128)} %fence.1.passed.rest_1_), custom_call_target="tpu_custom_call", output_to_operand_aliasing={{}: (2, {})} | custom-call | tf_op jit(solution)/shard_map/merge_high/pallas_call | solution.py:219
  (15 shorter events, 2.1 us)
Async XLA Ops:
  4.8 55.2 %all-to-all-start = ((bf16[8,2,64,2048]{3,2,1,0:T(8,128)(2,1)}), bf16[8,2,64,2048]{3,2,1,0:T(8,128)(2,1)}, u32[]{:S(2)}, u32[]{:S(2)}) async-start(bf16[8,2,64,2048]{3,2,1,0:T(8,128)(2,1)} %bitcast.26), calls=%async_computation | async-start | bytes 8388608 | tf_op jit(solution)/shard_map/all_to_all | solution.py:270
  14.3 49.3 %collective-permute-start.1 = (bf16[8,2,16,2048]{3,2,1,0:T(8,128)(2,1)}, bf16[8,2,16,2048]{3,2,1,0:T(8,128)(2,1)S(1)}, u32[]{:S(2)}, u32[]{:S(2)}) collective-permute-start(bf16[8,2,16,2048]{3,2,1,0:T(8,128)(2,1)} %get-tuple-element.35), channel_id=1, source_target_pairs={{0,8},{4,12},{8,0},{12,4},{1,9},{5,13},{9,1},{13,5},{2,10},{6,14},... | collective-permute-start | bytes 3145736 | tf_op jit(solution)/shard_map/ppermute | solution.py:253
  26.0 41.3 %collective-permute-start.2 = (bf16[8,2,16,2048]{3,2,1,0:T(8,128)(2,1)}, bf16[8,2,16,2048]{3,2,1,0:T(8,128)(2,1)S(1)}, u32[]{:S(2)}, u32[]{:S(2)}) collective-permute-start(bf16[8,2,16,2048]{3,2,1,0:T(8,128)(2,1)} %get-tuple-element.36), channel_id=1, source_target_pairs={{0,12},{4,0},{8,4},{12,8},{1,13},{5,1},{9,5},{13,9},{2,14},{6,2},{... | collective-permute-start | bytes 3145736 | tf_op jit(solution)/shard_map/ppermute | solution.py:253
  26.0 41.3 %collective-permute-start = (bf16[8,2,16,2048]{3,2,1,0:T(8,128)(2,1)}, bf16[8,2,16,2048]{3,2,1,0:T(8,128)(2,1)}, u32[]{:S(2)}, u32[]{:S(2)}) collective-permute-start(bf16[8,2,16,2048]{3,2,1,0:T(8,128)(2,1)} %get-tuple-element.34), channel_id=1, source_target_pairs={{0,4},{4,8},{8,12},{12,0},{1,5},{5,9},{9,13},{13,1},{2,6},{6,10},{... | collective-permute-start | bytes 3145736 | tf_op jit(solution)/shard_map/ppermute | solution.py:253
  30.3 13.4 %collective-permute-start.5 = (bf16[2,2,64,512]{3,2,1,0:T(8,128)(2,1)S(1)}, bf16[2,2,64,512]{3,2,1,0:T(8,128)(2,1)S(1)}, u32[]{:S(2)}, u32[]{:S(2)}) collective-permute-start(bf16[2,2,64,512]{3,2,1,0:T(8,128)(2,1)S(1)} %get-tuple-element.58), channel_id=1, source_target_pairs={{0,3},{1,0},{2,1},{3,2},{4,7},{5,4},{6,5},{7,6},{8,11},{9,8},{10,9... | collective-permute-start | bytes 786440 | tf_op jit(solution)/shard_map/ppermute | solution.py:253
  33.1 30.5 %collective-permute-start.4 = (bf16[2,2,64,512]{3,2,1,0:T(8,128)(2,1)}, bf16[2,2,64,512]{3,2,1,0:T(8,128)(2,1)}, u32[]{:S(2)}, u32[]{:S(2)}) collective-permute-start(bf16[2,2,64,512]{3,2,1,0:T(8,128)(2,1)} %get-tuple-element.59), channel_id=1, source_target_pairs={{0,2},{1,3},{2,0},{3,1},{4,6},{5,7},{6,4},{7,5},{8,10},{9,11},{10,... | collective-permute-start | bytes 786440 | tf_op jit(solution)/shard_map/ppermute | solution.py:253
  43.8 0.7 copy-start.1
  44.5 25.6 %copy-start = (bf16[8,2,16,2048]{3,2,1,0:T(8,128)(2,1)S(1)}, bf16[8,2,16,2048]{3,2,1,0:T(8,128)(2,1)}, u32[]{:S(2)}) copy-start(bf16[8,2,16,2048]{3,2,1,0:T(8,128)(2,1)} %get-tuple-element.38.refs_0_) | copy-start | bytes 3145732
  44.5 19.1 %collective-permute-start.3 = (bf16[2,2,64,512]{3,2,1,0:T(8,128)(2,1)}, bf16[2,2,64,512]{3,2,1,0:T(8,128)(2,1)}, u32[]{:S(2)}, u32[]{:S(2)}) collective-permute-start(bf16[2,2,64,512]{3,2,1,0:T(8,128)(2,1)} %get-tuple-element.60), channel_id=1, source_target_pairs={{0,1},{1,2},{2,3},{3,0},{4,5},{5,6},{6,7},{7,4},{8,9},{9,10},{10,1... | collective-permute-start | bytes 786440 | tf_op jit(solution)/shard_map/ppermute | solution.py:253
  67.3 28.0 %collective-permute-start.6 = (bf16[2,2,64,2048]{3,2,1,0:T(8,128)(2,1)}, bf16[2,2,64,2048]{3,2,1,0:T(8,128)(2,1)}, u32[]{:S(2)}, u32[]{:S(2)}) collective-permute-start(bf16[2,2,64,2048]{3,2,1,0:T(8,128)(2,1)} %get-tuple-element.42), channel_id=1, source_target_pairs={{0,8},{4,12},{8,0},{12,4},{1,9},{5,13},{9,1},{13,5},{2,10},{6,14},... | collective-permute-start | bytes 3145736 | tf_op jit(solution)/shard_map/ppermute | solution.py:253
  74.6 32.3 %all-to-all-start.1 = ((bf16[32,2,2,16,512]{4,3,2,1,0:T(8,128)(2,1)}), bf16[32,2,2,16,512]{4,3,2,1,0:T(8,128)(2,1)}, u32[]{:S(2)}, u32[]{:S(2)}) async-start(bf16[32,2,2,16,512]{4,3,2,1,0:T(8,128)(2,1)} %bitcast.10), calls=%async_computation.1 | async-start | bytes 4194304 | tf_op jit(solution)/shard_map/all_to_all | solution.py:300
  79.4 37.0 %collective-permute-start.7 = (bf16[2,2,64,2048]{3,2,1,0:T(8,128)(2,1)}, bf16[2,2,64,2048]{3,2,1,0:T(8,128)(2,1)S(1)}, u32[]{:S(2)}, u32[]{:S(2)}) collective-permute-start(bf16[2,2,64,2048]{3,2,1,0:T(8,128)(2,1)} %get-tuple-element.45), channel_id=1, source_target_pairs={{0,4},{4,8},{8,12},{12,0},{1,5},{5,9},{9,13},{13,1},{2,6},{6,10},{... | collective-permute-start | bytes 3145736 | tf_op jit(solution)/shard_map/ppermute | solution.py:253
  81.1 36.4 %collective-permute-start.8 = (bf16[2,2,64,2048]{3,2,1,0:T(8,128)(2,1)}, bf16[2,2,64,2048]{3,2,1,0:T(8,128)(2,1)S(1)}, u32[]{:S(2)}, u32[]{:S(2)}) collective-permute-start(bf16[2,2,64,2048]{3,2,1,0:T(8,128)(2,1)} %get-tuple-element.46), channel_id=1, source_target_pairs={{0,12},{4,0},{8,4},{12,8},{1,13},{5,1},{9,5},{13,9},{2,14},{6,2},{... | collective-permute-start | bytes 3145736 | tf_op jit(solution)/shard_map/ppermute | solution.py:253
  106.9 10.6 %copy-start.2 = (bf16[2,2,64,512]{3,2,1,0:T(8,128)(2,1)S(1)}, bf16[2,2,64,512]{3,2,1,0:T(8,128)(2,1)}, u32[]{:S(2)}) copy-start(bf16[2,2,64,512]{3,2,1,0:T(8,128)(2,1)} %copy-done.1) | copy-start | bytes 786436
  106.9 31.8 %all-to-all-start.2 = ((bf16[4,2,4,2,2,16,512]{6,5,4,3,2,1,0:T(8,128)(2,1)}), bf16[4,2,4,2,2,16,512]{6,5,4,3,2,1,0:T(8,128)(2,1)}, u32[]{:S(2)}, u32[]{:S(2)}) async-start(bf16[4,2,4,2,2,16,512]{6,5,4,3,2,1,0:T(8,128)(2,1)} %bitcast.11), calls=%async_computation.2 | async-start | bytes 4194304 | tf_op jit(solution)/shard_map/all_to_all | solution.py:304
  121.9 9.5 %collective-permute-start.9 = (bf16[2,2,64,512]{3,2,1,0:T(8,128)(2,1)S(1)}, bf16[2,2,64,512]{3,2,1,0:T(8,128)(2,1)S(1)}, u32[]{:S(2)}, u32[]{:S(2)}) collective-permute-start(bf16[2,2,64,512]{3,2,1,0:T(8,128)(2,1)S(1)} %get-tuple-element.52), channel_id=1, source_target_pairs={{0,1},{1,2},{2,3},{3,0},{4,5},{5,6},{6,7},{7,4},{8,9},{9,10},{10,1... | collective-permute-start | bytes 786440 | tf_op jit(solution)/shard_map/ppermute | solution.py:253
  123.5 13.2 %collective-permute-start.10 = (bf16[2,2,64,512]{3,2,1,0:T(8,128)(2,1)S(1)}, bf16[2,2,64,512]{3,2,1,0:T(8,128)(2,1)S(1)}, u32[]{:S(2)}, u32[]{:S(2)}) collective-permute-start(bf16[2,2,64,512]{3,2,1,0:T(8,128)(2,1)S(1)} %get-tuple-element.53), channel_id=1, source_target_pairs={{0,2},{1,3},{2,0},{3,1},{4,6},{5,7},{6,4},{7,5},{8,10},{9,11},{10,... | collective-permute-start | bytes 786440 | tf_op jit(solution)/shard_map/ppermute | solution.py:253
  126.2 10.4 %collective-permute-start.11 = (bf16[2,2,64,512]{3,2,1,0:T(8,128)(2,1)S(1)}, bf16[2,2,64,512]{3,2,1,0:T(8,128)(2,1)S(1)}, u32[]{:S(2)}, u32[]{:S(2)}) collective-permute-start(bf16[2,2,64,512]{3,2,1,0:T(8,128)(2,1)S(1)} %get-tuple-element.54), channel_id=1, source_target_pairs={{0,3},{1,0},{2,1},{3,2},{4,7},{5,4},{6,5},{7,6},{8,11},{9,8},{10,9... | collective-permute-start | bytes 786440 | tf_op jit(solution)/shard_map/ppermute | solution.py:253

commit v5 on v4

--- a/solution.py
+++ b/solution.py
@@ -32,37 +32,42 @@
     return tile * TILE, sign.astype(jnp.bfloat16)
 
 
-def pack_body(start, rows, shifts, after, tiles, counts, weights, fisher, *refs):
-    outs, (token, held, came, sent) = refs[after:-4], refs[-4:]
+def pack_body(low, rows, shifts, after, tiles, counts, weights, fisher, *refs):
+    refs = refs[after:]
+    count = int(low) + len(shifts)
+    outs, token, helds, (came, sent) = refs[:count], refs[count], refs[count + 1 : -2], refs[-2:]
     token[0] = 0
-    n = held.shape[0]
+    n = helds[0].shape[0]
     y = lax.axis_index("task")
     reads = []
     for j in range(n):
         first = lax.rem(y + j, n) * 2
         for ec in range(2):
             row, sign = listed(tiles, counts, first + ec)
-            if len(shifts) == 1:
-                row = row + lax.rem(y + shifts[0], n) * rows
-            at = pl.ds(pl.multiple_of(row + start, 8), held.shape[3])
-            for a, src in enumerate((weights, fisher)):
-                read = pltpu.make_async_copy(
-                    src.at[first + ec, at], held.at[j, ec, a], came.at[len(reads)]
-                )
-                reads.append((read, sign))
-                read.start()
-    writes = []
+            for k, held in enumerate(helds):
+                at = row
+                if not low or k:
+                    at = at + LOW
+                    if len(shifts) == 1:
+                        at = at + lax.rem(y + shifts[0], n) * rows
+                at = pl.ds(pl.multiple_of(at, 8), held.shape[3])
+                for a, src in enumerate((weights, fisher)):
+                    read = pltpu.make_async_copy(
+                        src.at[first + ec, at], held.at[j, ec, a], came.at[len(reads)]
+                    )
+                    reads.append((read, held.at[j, ec, a], sign if a else None))
+                    read.start()
+    writes, per = [], len(reads) // n
     for j in range(n):
         first = lax.rem(y + j, n) * 2
-        for ec in range(2):
-            (read, _), (read_fisher, sign) = reads[4 * j + 2 * ec : 4 * j + 2 * ec + 2]
+        for read, held, sign in reads[j * per : (j + 1) * per]:
             read.wait()
-            read_fisher.wait()
-            held[j, ec, 1] = held[j, ec, 1] * sign
-        parts = [(held.at[j], outs[0].at[j])] if not shifts else []
-        for d, out in zip(shifts, outs):
+            if sign is not None:
+                held[...] = held[...] * sign
+        parts = [(helds[0].at[j], outs[0].at[j])] if low else []
+        for d, out in zip(shifts, outs[int(low) :]):
             row = pl.multiple_of(lax.rem(y + d, n) * rows, 8) if len(shifts) > 1 else 0
-            parts.append((held.at[j, :, :, pl.ds(row, rows)], out.at[pl.ds(first, 2)]))
+            parts.append((helds[-1].at[j, :, :, pl.ds(row, rows)], out.at[pl.ds(first, 2)]))
         for src, dst in parts:
             write = pltpu.make_async_copy(src, dst, sent.at[len(writes)])
             writes.append(write)
@@ -71,21 +76,21 @@
         write.wait()
 
 
-def pack(tiles, counts, weights, fisher, n, start, rows, shifts, after):
+def pack(tiles, counts, weights, fisher, n, low, rows, shifts, after):
     experts, _, cols = weights.shape
-    read = n * rows if len(shifts) > 1 else rows
-    shape = (experts, 2, rows, cols) if shifts else (n, 2, 2, rows, cols)
-    count = max(len(shifts), 1)
-    return pl.pallas_call(
-        functools.partial(pack_body, start, rows, shifts, len(after)),
-        out_shape=[jax.ShapeDtypeStruct(shape, weights.dtype)] * count
+    reads = ([LOW] if low else []) + [n * rows if len(shifts) > 1 else rows]
+    shapes = [(n, 2, 2, LOW, cols)] if low else []
+    shapes += [(experts, 2, rows, cols)] * len(shifts)
+    return pl.pallas_call(
+        functools.partial(pack_body, low, rows, shifts, len(after)),
+        out_shape=[jax.ShapeDtypeStruct(shape, weights.dtype) for shape in shapes]
         + [jax.ShapeDtypeStruct((1,), jnp.int32)],
         in_specs=[SMEM, SMEM, HBM, HBM] + [SMEM] * len(after),
-        out_specs=[HBM] * count + [SMEM],
-        scratch_shapes=[
-            pltpu.VMEM((n, 2, 2, read, cols), weights.dtype),
-            pltpu.SemaphoreType.DMA((2 * experts,)),
-            pltpu.SemaphoreType.DMA((n * count,)),
+        out_specs=[HBM] * len(shapes) + [SMEM],
+        scratch_shapes=[pltpu.VMEM((n, 2, 2, r, cols), weights.dtype) for r in reads]
+        + [
+            pltpu.SemaphoreType.DMA((2 * experts * len(reads),)),
+            pltpu.SemaphoreType.DMA((n * len(shapes),)),
         ],
         name="pack",
     )(tiles, counts, weights, fisher, *after)
@@ -202,31 +207,53 @@
     )(*pieces)
 
 
-def merge_high_body(got, base, *rest):
-    out = rest[-1]
-    n, _, _, _, _, rows, _ = got.shape
-    for m in range(n):
-        at = pl.ds(m * rows, rows)
-        for x in range(n):
-            for j in range(2):
-                num, den = (got[m, 0, x, j, k].astype(jnp.float32) for k in range(2))
-                out[0, x, j, at, :] = merged_of(num, den, base[0, x, j, at, :]).astype(out.dtype)
+def merge_high_body(got, base, *refs):
+    out, held, prior, result, came, sent = refs[-6:]
+    n, cores, _, _, _, rows, _ = got.shape
+    high = pl.ds(LOW, TILE - LOW)
+    parts = [(c, pl.ds(x, 2)) for c in range(cores) for x in range(0, n, 2)]
+    reads = []
+    for i, (c, x) in enumerate(parts):
+        pair = [
+            pltpu.make_async_copy(base.at[c, x, :, high], prior.at[i], came.at[2 * i]),
+            pltpu.make_async_copy(got.at[:, c, x], held.at[i], came.at[2 * i + 1]),
+        ]
+        for read in pair:
+            read.start()
+        reads.append(pair)
+    writes = []
+    for i, (c, x) in enumerate(parts):
+        for read in reads[i]:
+            read.wait()
+        for m in range(n):
+            at = pl.ds(m * rows, rows)
+            for k in range(2):
+                for j in range(2):
+                    num, den = (held[i, m, k, j, v].astype(jnp.float32) for v in range(2))
+                    done = merged_of(num, den, prior[i, k, j, at, :])
+                    result[i, k, j, at, :] = done.astype(out.dtype)
+        writes.append(pltpu.make_async_copy(result.at[i], out.at[c, x, :, high], sent.at[i]))
+        writes[-1].start()
+    for write in writes:
+        write.wait()
 
 
 def merge_high(got, base, whole, passed):
-    n, c, _, _, _, rows, cols = got.shape
-    part = pl.BlockSpec((1, n, 2, TILE - LOW, cols), lambda i: (i, 0, 0, LOW // (TILE - LOW), 0))
+    n, cores, _, _, _, rows, cols = got.shape
+    parts = cores * n // 2
+    block = (parts, 2, 2, TILE - LOW, cols)
     return pl.pallas_call(
         merge_high_body,
         out_shape=jax.ShapeDtypeStruct(whole.shape, whole.dtype),
-        grid=(c,),
-        in_specs=[
-            pl.BlockSpec((n, 1, n, 2, 2, rows, cols), lambda i: (0, i, 0, 0, 0, 0, 0)),
-            part,
-            HBM,
-            SMEM,
+        in_specs=[HBM, HBM, HBM, SMEM],
+        out_specs=HBM,
+        scratch_shapes=[
+            pltpu.VMEM((parts, n, 2, 2, 2, rows, cols), got.dtype),
+            pltpu.VMEM(block, base.dtype),
+            pltpu.VMEM(block, whole.dtype),
+            pltpu.SemaphoreType.DMA((2 * parts,)),
+            pltpu.SemaphoreType.DMA((parts,)),
         ],
-        out_specs=part,
         input_output_aliases={2: 0},
         name="merge_high",
     )(got, base, whole, passed)
@@ -280,23 +307,23 @@
     tiles, counts = tile_list[0, :, :, 0], tile_count[0]
     rows = (TILE - LOW) // ny
     args = (tiles, counts, weights, fisher, nz)
-    low, token = pack(*args, 0, LOW, (), ())
-    high_2, token = pack(*args, LOW, rows, (2,), (token,))
-    high_1, high_3, high_0, _ = pack(*args, LOW, rows, (1, 3, 0), (token,))
+    low, high_2, token = pack(*args, True, rows, (2,), ())
+    high_1, high_3, high_0, _ = pack(*args, False, rows, (1, 3, 0), (token,))
     high = [high_0, high_1, high_2, high_3]
 
     got_low = over_z(low)
     got_high = [high[0]] + all_shifted(high, "task")
-    mine = [got_low[m] for m in range(1, ny)]
     base = base_weights.reshape(2, nx, 2, TILE, cols)
     base, packed = hold((base, high[1]))
     prior = []
     for d in range(nx):
         part = lax.dynamic_index_in_dim(base[:, :, :, :LOW], lax.rem(x + d, nx), 1, keepdims=False)
         prior.append(shifted(part, "shard", d) if d else part)
-    mine, got_high, prior = hold((mine, got_high, prior))
-    others = all_shifted([None, *mine], "task")
+    far, got_high, prior = hold((got_low[2], got_high, prior))
+    far = shifted(far, "task", 2)
     added = add_high(got_high)
+    near, added = hold((got_low, added))
+    others = [shifted(near[1], "task", 1), far, shifted(near[3], "task", 3)]
     moved = lax.all_to_all(
         added.reshape(-1, *added.shape[2:]), ("z", "core", "shard"), 0, 0, tiled=True
     )

time: 143 us -> 141 us (0.986)
  local copies, waits for them, and re-layouts: 6.57 us -> 10.7 us
  waiting for transfers between devices: 68.7 us -> 65.1 us
  Pallas kernels: 28.3 us -> 25 us
    ppermute x12, waiting for transfers between devices: 41.2 us -> 31.9 us  [shifted(): return lax.ppermute(x, axis, [(i, (i + by) % n) for i in range(n)])]
    squeeze x0 -> x1, local copies, waits for them, and re-layouts: none -> 3.14 us  [local(): others = [shifted(near[1], 'task', 1), far, shifted(near[3], 'task', 3)]]
    pallas_call x3 -> x2, Pallas kernels: 14.2 us -> 11.2 us  [pack(): pl.pallas_call(functools.partial(pack_body, low, rows, shifts, len(after)...]
    all_to_all x1, waiting for transfers between devices: 11.1 us -> 13.2 us  [local(): lax.all_to_all(added.reshape(-1, *added.shape[2:]), ('z', 'core', 'shard'...]
    all_to_all x1, starting transfers between devices: 4.82 us -> 6.95 us  [local(): lax.all_to_all(added.reshape(-1, *added.shape[2:]), ('z', 'core', 'shard'...]
    all_to_all x1, waiting for transfers between devices: 15.5 us -> 17.5 us  [over_z(): lax.all_to_all(flat, MESH, 0, 0, axis_index_groups=groups, tiled=True)]
    all_to_all x1, waiting for transfers between devices: 1.02 us -> 2.45 us  [local(): lax.all_to_all(moved.reshape(nz, 2, nx, *moved.shape[1:]), 'task', 0, 0,...]
  transfers between devices with their start and end apart: 15 -> 15, of which waited for: 10 -> 9; matrix products, arithmetic and copies ran while one was open for 4% -> 7% of each run, Pallas kernels for 14% -> 11%
where the time goes in v5:
time: 141 us; the launch traced here: 140 us
  waiting for transfers between devices  65.1 us (46%)
  starting transfers between devices  39.6 us (28%)
  Pallas kernels  25 us (18%)
  local copies, waits for them, and re-layouts  10.7 us (8%)
    ppermute x12, waiting for transfers between devices, shifted(): return lax.ppermute(x, axis, [(i, (i + by) % n) for i in range(n)])  31.9 us
    ppermute x12, starting transfers between devices, shifted(): return lax.ppermute(x, axis, [(i, (i + by) % n) for i in range(n)])  22.6 us
    all_to_all x1, waiting for transfers between devices, over_z(): lax.all_to_all(flat, MESH, 0, 0, axis_index_groups=groups, tiled=True)  17.5 us
    all_to_all x1, waiting for transfers between devices, local(): lax.all_to_all(added.reshape(-1, *added.shape[2:]), ('z', 'core', 'shard'...  13.2 us
    pallas_call x2, Pallas kernels, pack(): pl.pallas_call(functools.partial(pack_body, low, rows, shifts, len(after)...  11.2 us
    all_to_all x1, starting transfers between devices, local(): lax.all_to_all(added.reshape(-1, *added.shape[2:]), ('z', 'core', 'shard'...  6.95 us
    all_to_all x1, starting transfers between devices, over_z(): lax.all_to_all(flat, MESH, 0, 0, axis_index_groups=groups, tiled=True)  5.41 us
    all_to_all x1, starting transfers between devices, local(): lax.all_to_all(moved.reshape(nz, 2, nx, *moved.shape[1:]), 'task', 0, 0,...  4.59 us
  transfers between devices with their start and end apart: 15, of which 9 were waited for; matrix products, arithmetic and copies ran while one was open for 7% of the time, Pallas kernels for 11%

profile of v5, /device:TPU:0, one launch (start us, length us, event | category | flops | bytes accessed | tf_op | source)
XLA Modules:
  0.0 140.4 jit_solution(13443079736824655668)
XLA Ops:
  0.0 5.9 %pack.2 = (bf16[4,2,2,64,2048]{4,3,2,1,0:T(8,128)(2,1)}, bf16[8,2,16,2048]{3,2,1,0:T(8,128)(2,1)}, s32[1]{0:T(128)}) custom-call(s32[8,32]{1,0:T(8,128)} %bitcast.29, s32[8,32]{1,0:T(8,128)} %bitcast.31, bf16[8,256,2048]{2,1,0:T(8,128)(2,1)} %bitcast.22, bf16[8,256,2048]{2,1,0:T(8,128)(2,1)} %bitcast.24), custom_call_target="tpu_custom_call" | custom-call | tf_op jit(solution)/shard_map/pack/pallas_call | solution.py:84
  5.9 5.4 %all-to-all-start = ((bf16[8,2,64,2048]{3,2,1,0:T(8,128)(2,1)}), bf16[8,2,64,2048]{3,2,1,0:T(8,128)(2,1)}, u32[]{:S(2)}, u32[]{:S(2)}) async-start(bf16[8,2,64,2048]{3,2,1,0:T(8,128)(2,1)} %bitcast.28), calls=%async_computation | async-start | bytes 8388608 | tf_op jit(solution)/shard_map/all_to_all | solution.py:297
  11.3 6.2 %collective-permute-start.1 = (bf16[8,2,16,2048]{3,2,1,0:T(8,128)(2,1)}, bf16[8,2,16,2048]{3,2,1,0:T(8,128)(2,1)S(1)}, u32[]{:S(2)}, u32[]{:S(2)}) collective-permute-start(bf16[8,2,16,2048]{3,2,1,0:T(8,128)(2,1)} %get-tuple-element.33), channel_id=1, source_target_pairs={{0,8},{4,12},{8,0},{12,4},{1,9},{5,13},{9,1},{13,5},{2,10},{6,14},... | collective-permute-start | bytes 3145736 | tf_op jit(solution)/shard_map/ppermute | solution.py:280
  17.5 5.3 %pack.3 = (bf16[8,2,16,2048]{3,2,1,0:T(8,128)(2,1)}, bf16[8,2,16,2048]{3,2,1,0:T(8,128)(2,1)}, bf16[8,2,16,2048]{3,2,1,0:T(8,128)(2,1)}, s32[1]{0:T(128)}) custom-call(s32[8,32]{1,0:T(8,128)} %bitcast.30, s32[8,32]{1,0:T(8,128)} %bitcast.32, bf16[8,256,2048]{2,1,0:T(8,128)(2,1)} %bitcast.23, bf16[8,256,2048]{2,1,0:T(8,128)(2,1)} %bitcast.25, ...), custom_call_target="tpu_custom_call" | custom-call | tf_op jit(solution)/shard_map/pack/pallas_call | solution.py:84
  22.9 2.0 %collective-permute-start = (bf16[8,2,16,2048]{3,2,1,0:T(8,128)(2,1)}, bf16[8,2,16,2048]{3,2,1,0:T(8,128)(2,1)}, u32[]{:S(2)}, u32[]{:S(2)}) collective-permute-start(bf16[8,2,16,2048]{3,2,1,0:T(8,128)(2,1)} %get-tuple-element.32), channel_id=1, source_target_pairs={{0,4},{4,8},{8,12},{12,0},{1,5},{5,9},{9,13},{13,1},{2,6},{6,10},{... | collective-permute-start | bytes 3145736 | tf_op jit(solution)/shard_map/ppermute | solution.py:280
  24.9 2.4 %slice.17 = bf16[2,4,2,64,512]{4,3,2,1,0:T(8,128)(2,1)} slice(bf16[2,4,2,128,512]{4,3,2,1,0:T(8,128)(2,1)} %bitcast.26), slice={[0:2], [0:4], [0:2], [0:64], [0:512]} | slice | bytes 2097152 | tf_op jit(solution)/shard_map/slice | solution.py:320
  27.3 2.2 %dynamic-slice_bitcast_fusion = (bf16[2,2,64,512]{3,2,1,0:T(8,128)(2,1)S(1)}, bf16[2,2,64,512]{3,2,1,0:T(8,128)(2,1)}, bf16[2,2,64,512]{3,2,1,0:T(8,128)(2,1)}, bf16[2,2,64,512]{3,2,1,0:T(8,128)(2,1)S(1)}) fusion(bf16[2,4,2,64,512]{4,3,2,1,0:T(8,128)(2,1)} %slice.17, s32[]{:T(128)S(6)} %select_n.16, s32[]{:T(128)S(6)} %select_n.15, s32[]{:T(128)S(6)} %select_n.14, ...), kind=kLoop, calls=%fused_computation.2 | loop fusion | bytes 2097168 | tf_op jit(solution)/shard_map/jit(dynamic_index_in_dim)/squeeze | solution.py:320
  29.5 2.8 %collective-permute-start.5 = (bf16[2,2,64,512]{3,2,1,0:T(8,128)(2,1)S(1)}, bf16[2,2,64,512]{3,2,1,0:T(8,128)(2,1)S(1)}, u32[]{:S(2)}, u32[]{:S(2)}) collective-permute-start(bf16[2,2,64,512]{3,2,1,0:T(8,128)(2,1)S(1)} %get-tuple-element.55), channel_id=1, source_target_pairs={{0,3},{1,0},{2,1},{3,2},{4,7},{5,4},{6,5},{7,6},{8,11},{9,8},{10,9... | collective-permute-start | bytes 786440 | tf_op jit(solution)/shard_map/ppermute | solution.py:280
  32.2 0.8 collective-permute-start.4
  33.0 9.9 %collective-permute-done.5.rest_6_ = bf16[2,2,64,512]{3,2,1,0:T(8,128)(2,1)S(1)} collective-permute-done((bf16[2,2,64,512]{3,2,1,0:T(8,128)(2,1)S(1)}, bf16[2,2,64,512]{3,2,1,0:T(8,128)(2,1)S(1)}, u32[]{:S(2)}, u32[]{:S(2)}) %collective-permute-start.5) | collective-permute-done | bytes 262176 | tf_op jit(solution)/shard_map/ppermute | solution.py:280
  42.9 0.7 copy-done.1
  43.6 17.5 %all-to-all-done = bf16[8,2,64,2048]{3,2,1,0:T(8,128)(2,1)} async-done(((bf16[8,2,64,2048]{3,2,1,0:T(8,128)(2,1)}), bf16[8,2,64,2048]{3,2,1,0:T(8,128)(2,1)}, u32[]{:S(2)}, u32[]{:S(2)}) %all-to-all-start) | async-done | bytes 4194336 | tf_op jit(solution)/shard_map/all_to_all | solution.py:297
  61.1 2.3 %slice.20 = bf16[2,2,64,2048]{3,2,1,0:T(8,128)(2,1)} slice(bf16[8,2,64,2048]{3,2,1,0:T(8,128)(2,1)} %all-to-all-done), slice={[4:6], [0:2], [0:64], [0:2048]} | slice | bytes 2097152 | tf_op jit(solution)/shard_map/slice | solution.py:322
  63.4 0.9 collective-permute-done.2.refs_3_
  64.3 2.8 %collective-permute-start.6 = (bf16[2,2,64,2048]{3,2,1,0:T(8,128)(2,1)}, bf16[2,2,64,2048]{3,2,1,0:T(8,128)(2,1)}, u32[]{:S(2)}, u32[]{:S(2)}) collective-permute-start(bf16[2,2,64,2048]{3,2,1,0:T(8,128)(2,1)} %slice.20), channel_id=1, source_target_pairs={{0,8},{4,12},{8,0},{12,4},{1,9},{5,13},{9,1},{13,5},{2,10},{6,14},... | collective-permute-start | bytes 3145736 | tf_op jit(solution)/shard_map/ppermute | solution.py:280
  67.0 4.5 %add_high.1 = bf16[8,4,2,2,16,512]{5,4,3,2,1,0:T(8,128)(2,1)} custom-call(bf16[8,2,16,2048]{3,2,1,0:T(8,128)(2,1)S(1)} %copy-done, bf16[8,2,16,2048]{3,2,1,0:T(8,128)(2,1)} %collective-permute-done.refs_1_, bf16[8,2,16,2048]{3,2,1,0:T(8,128)(2,1)S(1)} %collective-permute-done.1.refs_2_, bf16[8,2,16,2048]{3,2,1,0:T(8,128)(2,1)S(1)} %collective-permute-done.2.refs_3_), custom_call_target="tpu_custom_call" | custom-call | tf_op jit(solution)/shard_map/add_high/pallas_call | solution.py:166
  71.6 6.9 %all-to-all-start.1 = ((bf16[32,2,2,16,512]{4,3,2,1,0:T(8,128)(2,1)}), bf16[32,2,2,16,512]{4,3,2,1,0:T(8,128)(2,1)}, u32[]{:S(2)}, u32[]{:S(2)}) async-start(bf16[32,2,2,16,512]{4,3,2,1,0:T(8,128)(2,1)} %bitcast.11), calls=%async_computation.1 | async-start | bytes 4194304 | tf_op jit(solution)/shard_map/all_to_all | solution.py:327
  78.5 3.1 %slice_bitcast_fusion = (bf16[2,2,64,2048]{3,2,1,0:T(8,128)(2,1)}, bf16[2,2,64,2048]{3,2,1,0:T(8,128)(2,1)}) fusion(bf16[4,2,2,64,2048]{4,3,2,1,0:T(8,128)(2,1)} %bitcast.5.first), kind=kLoop, calls=%fused_computation | loop fusion | bytes 4194304 | tf_op jit(solution)/shard_map/squeeze | solution.py:326
  81.7 2.0 %collective-permute-start.7 = (bf16[2,2,64,2048]{3,2,1,0:T(8,128)(2,1)}, bf16[2,2,64,2048]{3,2,1,0:T(8,128)(2,1)S(1)}, u32[]{:S(2)}, u32[]{:S(2)}) collective-permute-start(bf16[2,2,64,2048]{3,2,1,0:T(8,128)(2,1)} %get-tuple-element.54), channel_id=1, source_target_pairs={{0,4},{4,8},{8,12},{12,0},{1,5},{5,9},{9,13},{13,1},{2,6},{6,10},{... | collective-permute-start | bytes 3145736 | tf_op jit(solution)/shard_map/ppermute | solution.py:280
  83.7 8.5 %collective-permute-done.6.refs_0_.rest_1_ = bf16[2,2,64,2048]{3,2,1,0:T(8,128)(2,1)} collective-permute-done((bf16[2,2,64,2048]{3,2,1,0:T(8,128)(2,1)}, bf16[2,2,64,2048]{3,2,1,0:T(8,128)(2,1)}, u32[]{:S(2)}, u32[]{:S(2)}) %collective-permute-start.6) | collective-permute-done | bytes 1048608 | tf_op jit(solution)/shard_map/ppermute | solution.py:280
  92.7 13.2 %all-to-all-done.1 = bf16[32,2,2,16,512]{4,3,2,1,0:T(8,128)(2,1)} async-done(((bf16[32,2,2,16,512]{4,3,2,1,0:T(8,128)(2,1)}), bf16[32,2,2,16,512]{4,3,2,1,0:T(8,128)(2,1)}, u32[]{:S(2)}, u32[]{:S(2)}) %all-to-all-start.1) | async-done | bytes 2097184 | tf_op jit(solution)/shard_map/all_to_all | solution.py:327
  106.0 4.6 %all-to-all-start.2 = ((bf16[4,2,4,2,2,16,512]{6,5,4,3,2,1,0:T(8,128)(2,1)}), bf16[4,2,4,2,2,16,512]{6,5,4,3,2,1,0:T(8,128)(2,1)}, u32[]{:S(2)}, u32[]{:S(2)}) async-start(bf16[4,2,4,2,2,16,512]{6,5,4,3,2,1,0:T(8,128)(2,1)} %bitcast.12), calls=%async_computation.2 | async-start | bytes 4194304 | tf_op jit(solution)/shard_map/all_to_all | solution.py:331
  110.6 4.2 %collective-permute-done.8.rest_2_ = bf16[2,2,64,2048]{3,2,1,0:T(8,128)(2,1)S(1)} collective-permute-done((bf16[2,2,64,2048]{3,2,1,0:T(8,128)(2,1)}, bf16[2,2,64,2048]{3,2,1,0:T(8,128)(2,1)S(1)}, u32[]{:S(2)}, u32[]{:S(2)}) %collective-permute-start.8) | collective-permute-done | bytes 1048608 | tf_op jit(solution)/shard_map/ppermute | solution.py:280
  114.8 4.4 %merge_low.1 = (bf16[2,2,64,512]{3,2,1,0:T(8,128)(2,1)S(1)}, bf16[2,2,64,512]{3,2,1,0:T(8,128)(2,1)S(1)}, bf16[2,2,64,512]{3,2,1,0:T(8,128)(2,1)S(1)}, bf16[2,2,64,512]{3,2,1,0:T(8,128)(2,1)S(1)}) custom-call(s32[1]{0:T(128)} %fence.1.passed.refs_1_, bf16[4,2,2,64,2048]{4,3,2,1,0:T(8,128)(2,1)} %bitcast.5.first, ...), custom_call_target="tpu_custom_call" | custom-call | flops 99999997952 | tf_op jit(solution)/shard_map/merge_low/pallas_call | solution.py:136
  119.2 1.9 %collective-permute-start.9 = (bf16[2,2,64,512]{3,2,1,0:T(8,128)(2,1)S(1)}, bf16[2,2,64,512]{3,2,1,0:T(8,128)(2,1)S(1)}, u32[]{:S(2)}, u32[]{:S(2)}) collective-permute-start(bf16[2,2,64,512]{3,2,1,0:T(8,128)(2,1)S(1)} %get-tuple-element.50), channel_id=1, source_target_pairs={{0,1},{1,2},{2,3},{3,0},{4,5},{5,6},{6,7},{7,4},{8,9},{9,10},{10,1... | collective-permute-start | bytes 786440 | tf_op jit(solution)/shard_map/ppermute | solution.py:280
  121.1 2.4 %collective-permute-start.10 = (bf16[2,2,64,512]{3,2,1,0:T(8,128)(2,1)S(1)}, bf16[2,2,64,512]{3,2,1,0:T(8,128)(2,1)S(1)}, u32[]{:S(2)}, u32[]{:S(2)}) collective-permute-start(bf16[2,2,64,512]{3,2,1,0:T(8,128)(2,1)S(1)} %get-tuple-element.51), channel_id=1, source_target_pairs={{0,2},{1,3},{2,0},{3,1},{4,6},{5,7},{6,4},{7,5},{8,10},{9,11},{10,... | collective-permute-start | bytes 786440 | tf_op jit(solution)/shard_map/ppermute | solution.py:280
  123.4 1.7 %collective-permute-start.11 = (bf16[2,2,64,512]{3,2,1,0:T(8,128)(2,1)S(1)}, bf16[2,2,64,512]{3,2,1,0:T(8,128)(2,1)S(1)}, u32[]{:S(2)}, u32[]{:S(2)}) collective-permute-start(bf16[2,2,64,512]{3,2,1,0:T(8,128)(2,1)S(1)} %get-tuple-element.52), channel_id=1, source_target_pairs={{0,3},{1,0},{2,1},{3,2},{4,7},{5,4},{6,5},{7,6},{8,11},{9,8},{10,9... | collective-permute-start | bytes 786440 | tf_op jit(solution)/shard_map/ppermute | solution.py:280
  125.1 3.5 %collective-permute-done.9.refs_1_ = bf16[2,2,64,512]{3,2,1,0:T(8,128)(2,1)S(1)} collective-permute-done((bf16[2,2,64,512]{3,2,1,0:T(8,128)(2,1)S(1)}, bf16[2,2,64,512]{3,2,1,0:T(8,128)(2,1)S(1)}, u32[]{:S(2)}, u32[]{:S(2)}) %collective-permute-start.9) | collective-permute-done | bytes 262176 | tf_op jit(solution)/shard_map/ppermute | solution.py:280
  128.7 4.9 %collective-permute-done.10.refs_2_ = bf16[2,2,64,512]{3,2,1,0:T(8,128)(2,1)S(1)} collective-permute-done((bf16[2,2,64,512]{3,2,1,0:T(8,128)(2,1)S(1)}, bf16[2,2,64,512]{3,2,1,0:T(8,128)(2,1)S(1)}, u32[]{:S(2)}, u32[]{:S(2)}) %collective-permute-start.10) | collective-permute-done | bytes 262176 | tf_op jit(solution)/shard_map/ppermute | solution.py:280
  133.5 1.0 place.1.refs_0_
  134.6 2.5 %all-to-all-done.2.got = bf16[4,2,4,2,2,16,512]{6,5,4,3,2,1,0:T(8,128)(2,1)} async-done(((bf16[4,2,4,2,2,16,512]{6,5,4,3,2,1,0:T(8,128)(2,1)}), bf16[4,2,4,2,2,16,512]{6,5,4,3,2,1,0:T(8,128)(2,1)}, u32[]{:S(2)}, u32[]{:S(2)}) %all-to-all-start.2) | async-done | bytes 2097184 | tf_op jit(solution)/shard_map/all_to_all | solution.py:331
  137.0 3.4 %merge_high.1 = bf16[2,4,2,128,512]{4,3,2,1,0:T(8,128)(2,1)} custom-call(bf16[4,2,4,2,2,16,512]{6,5,4,3,2,1,0:T(8,128)(2,1)} %all-to-all-done.2.got, bf16[2,4,2,128,512]{4,3,2,1,0:T(8,128)(2,1)} %bitcast.27, bf16[2,4,2,128,512]{4,3,2,1,0:T(8,128)(2,1)} %place.1.refs_0_, s32[1]{0:T(128)} %fence.1.passed.refs_1_), custom_call_target="tpu_custom_call", output_to_operand_aliasing={{}: (2, {})} | custom-call | tf_op jit(solution)/shard_map/merge_high/pallas_call | solution.py:245
  (15 shorter events, 0.6 us)
Async XLA Ops:
  5.9 55.2 %all-to-all-start = ((bf16[8,2,64,2048]{3,2,1,0:T(8,128)(2,1)}), bf16[8,2,64,2048]{3,2,1,0:T(8,128)(2,1)}, u32[]{:S(2)}, u32[]{:S(2)}) async-start(bf16[8,2,64,2048]{3,2,1,0:T(8,128)(2,1)} %bitcast.28), calls=%async_computation | async-start | bytes 8388608 | tf_op jit(solution)/shard_map/all_to_all | solution.py:297
  11.3 52.1 %collective-permute-start.1 = (bf16[8,2,16,2048]{3,2,1,0:T(8,128)(2,1)}, bf16[8,2,16,2048]{3,2,1,0:T(8,128)(2,1)S(1)}, u32[]{:S(2)}, u32[]{:S(2)}) collective-permute-start(bf16[8,2,16,2048]{3,2,1,0:T(8,128)(2,1)} %get-tuple-element.33), channel_id=1, source_target_pairs={{0,8},{4,12},{8,0},{12,4},{1,9},{5,13},{9,1},{13,5},{2,10},{6,14},... | collective-permute-start | bytes 3145736 | tf_op jit(solution)/shard_map/ppermute | solution.py:280
  22.8 41.4 %collective-permute-start.2 = (bf16[8,2,16,2048]{3,2,1,0:T(8,128)(2,1)}, bf16[8,2,16,2048]{3,2,1,0:T(8,128)(2,1)S(1)}, u32[]{:S(2)}, u32[]{:S(2)}) collective-permute-start(bf16[8,2,16,2048]{3,2,1,0:T(8,128)(2,1)} %get-tuple-element.34), channel_id=1, source_target_pairs={{0,12},{4,0},{8,4},{12,8},{1,13},{5,1},{9,5},{13,9},{2,14},{6,2},{... | collective-permute-start | bytes 3145736 | tf_op jit(solution)/shard_map/ppermute | solution.py:280
  22.9 41.3 %collective-permute-start = (bf16[8,2,16,2048]{3,2,1,0:T(8,128)(2,1)}, bf16[8,2,16,2048]{3,2,1,0:T(8,128)(2,1)}, u32[]{:S(2)}, u32[]{:S(2)}) collective-permute-start(bf16[8,2,16,2048]{3,2,1,0:T(8,128)(2,1)} %get-tuple-element.32), channel_id=1, source_target_pairs={{0,4},{4,8},{8,12},{12,0},{1,5},{5,9},{9,13},{13,1},{2,6},{6,10},{... | collective-permute-start | bytes 3145736 | tf_op jit(solution)/shard_map/ppermute | solution.py:280
  27.3 39.7 %copy-start = (bf16[8,2,16,2048]{3,2,1,0:T(8,128)(2,1)S(1)}, bf16[8,2,16,2048]{3,2,1,0:T(8,128)(2,1)}, u32[]{:S(2)}) copy-start(bf16[8,2,16,2048]{3,2,1,0:T(8,128)(2,1)} %get-tuple-element.36.refs_0_) | copy-start | bytes 3145732
  29.5 13.4 %collective-permute-start.5 = (bf16[2,2,64,512]{3,2,1,0:T(8,128)(2,1)S(1)}, bf16[2,2,64,512]{3,2,1,0:T(8,128)(2,1)S(1)}, u32[]{:S(2)}, u32[]{:S(2)}) collective-permute-start(bf16[2,2,64,512]{3,2,1,0:T(8,128)(2,1)S(1)} %get-tuple-element.55), channel_id=1, source_target_pairs={{0,3},{1,0},{2,1},{3,2},{4,7},{5,4},{6,5},{7,6},{8,11},{9,8},{10,9... | collective-permute-start | bytes 786440 | tf_op jit(solution)/shard_map/ppermute | solution.py:280
  32.2 31.2 %collective-permute-start.4 = (bf16[2,2,64,512]{3,2,1,0:T(8,128)(2,1)}, bf16[2,2,64,512]{3,2,1,0:T(8,128)(2,1)}, u32[]{:S(2)}, u32[]{:S(2)}) collective-permute-start(bf16[2,2,64,512]{3,2,1,0:T(8,128)(2,1)} %get-tuple-element.56), channel_id=1, source_target_pairs={{0,2},{1,3},{2,0},{3,1},{4,6},{5,7},{6,4},{7,5},{8,10},{9,11},{10,... | collective-permute-start | bytes 786440 | tf_op jit(solution)/shard_map/ppermute | solution.py:280
  42.9 0.7 copy-start.1
  43.6 19.8 %collective-permute-start.3 = (bf16[2,2,64,512]{3,2,1,0:T(8,128)(2,1)}, bf16[2,2,64,512]{3,2,1,0:T(8,128)(2,1)}, u32[]{:S(2)}, u32[]{:S(2)}) collective-permute-start(bf16[2,2,64,512]{3,2,1,0:T(8,128)(2,1)} %get-tuple-element.57), channel_id=1, source_target_pairs={{0,1},{1,2},{2,3},{3,0},{4,5},{5,6},{6,7},{7,4},{8,9},{9,10},{10,1... | collective-permute-start | bytes 786440 | tf_op jit(solution)/shard_map/ppermute | solution.py:280
  64.3 28.0 %collective-permute-start.6 = (bf16[2,2,64,2048]{3,2,1,0:T(8,128)(2,1)}, bf16[2,2,64,2048]{3,2,1,0:T(8,128)(2,1)}, u32[]{:S(2)}, u32[]{:S(2)}) collective-permute-start(bf16[2,2,64,2048]{3,2,1,0:T(8,128)(2,1)} %slice.20), channel_id=1, source_target_pairs={{0,8},{4,12},{8,0},{12,4},{1,9},{5,13},{9,1},{13,5},{2,10},{6,14},... | collective-permute-start | bytes 3145736 | tf_op jit(solution)/shard_map/ppermute | solution.py:280
  71.6 34.4 %all-to-all-start.1 = ((bf16[32,2,2,16,512]{4,3,2,1,0:T(8,128)(2,1)}), bf16[32,2,2,16,512]{4,3,2,1,0:T(8,128)(2,1)}, u32[]{:S(2)}, u32[]{:S(2)}) async-start(bf16[32,2,2,16,512]{4,3,2,1,0:T(8,128)(2,1)} %bitcast.11), calls=%async_computation.1 | async-start | bytes 4194304 | tf_op jit(solution)/shard_map/all_to_all | solution.py:327
  81.7 33.1 %collective-permute-start.8 = (bf16[2,2,64,2048]{3,2,1,0:T(8,128)(2,1)}, bf16[2,2,64,2048]{3,2,1,0:T(8,128)(2,1)S(1)}, u32[]{:S(2)}, u32[]{:S(2)}) collective-permute-start(bf16[2,2,64,2048]{3,2,1,0:T(8,128)(2,1)} %get-tuple-element.53), channel_id=1, source_target_pairs={{0,12},{4,0},{8,4},{12,8},{1,13},{5,1},{9,5},{13,9},{2,14},{6,2},{... | collective-permute-start | bytes 3145736 | tf_op jit(solution)/shard_map/ppermute | solution.py:280
  81.7 33.1 %collective-permute-start.7 = (bf16[2,2,64,2048]{3,2,1,0:T(8,128)(2,1)}, bf16[2,2,64,2048]{3,2,1,0:T(8,128)(2,1)S(1)}, u32[]{:S(2)}, u32[]{:S(2)}) collective-permute-start(bf16[2,2,64,2048]{3,2,1,0:T(8,128)(2,1)} %get-tuple-element.54), channel_id=1, source_target_pairs={{0,4},{4,8},{8,12},{12,0},{1,5},{5,9},{9,13},{13,1},{2,6},{6,10},{... | collective-permute-start | bytes 3145736 | tf_op jit(solution)/shard_map/ppermute | solution.py:280
  106.0 8.8 %copy-start.2 = (bf16[2,2,64,512]{3,2,1,0:T(8,128)(2,1)S(1)}, bf16[2,2,64,512]{3,2,1,0:T(8,128)(2,1)}, u32[]{:S(2)}) copy-start(bf16[2,2,64,512]{3,2,1,0:T(8,128)(2,1)} %copy-done.1) | copy-start | bytes 786436
  106.0 31.1 %all-to-all-start.2 = ((bf16[4,2,4,2,2,16,512]{6,5,4,3,2,1,0:T(8,128)(2,1)}), bf16[4,2,4,2,2,16,512]{6,5,4,3,2,1,0:T(8,128)(2,1)}, u32[]{:S(2)}, u32[]{:S(2)}) async-start(bf16[4,2,4,2,2,16,512]{6,5,4,3,2,1,0:T(8,128)(2,1)} %bitcast.12), calls=%async_computation.2 | async-start | bytes 4194304 | tf_op jit(solution)/shard_map/all_to_all | solution.py:331
  119.2 9.5 %collective-permute-start.9 = (bf16[2,2,64,512]{3,2,1,0:T(8,128)(2,1)S(1)}, bf16[2,2,64,512]{3,2,1,0:T(8,128)(2,1)S(1)}, u32[]{:S(2)}, u32[]{:S(2)}) collective-permute-start(bf16[2,2,64,512]{3,2,1,0:T(8,128)(2,1)S(1)} %get-tuple-element.50), channel_id=1, source_target_pairs={{0,1},{1,2},{2,3},{3,0},{4,5},{5,6},{6,7},{7,4},{8,9},{9,10},{10,1... | collective-permute-start | bytes 786440 | tf_op jit(solution)/shard_map/ppermute | solution.py:280
  121.1 12.5 %collective-permute-start.10 = (bf16[2,2,64,512]{3,2,1,0:T(8,128)(2,1)S(1)}, bf16[2,2,64,512]{3,2,1,0:T(8,128)(2,1)S(1)}, u32[]{:S(2)}, u32[]{:S(2)}) collective-permute-start(bf16[2,2,64,512]{3,2,1,0:T(8,128)(2,1)S(1)} %get-tuple-element.51), channel_id=1, source_target_pairs={{0,2},{1,3},{2,0},{3,1},{4,6},{5,7},{6,4},{7,5},{8,10},{9,11},{10,... | collective-permute-start | bytes 786440 | tf_op jit(solution)/shard_map/ppermute | solution.py:280
  123.4 10.1 %collective-permute-start.11 = (bf16[2,2,64,512]{3,2,1,0:T(8,128)(2,1)S(1)}, bf16[2,2,64,512]{3,2,1,0:T(8,128)(2,1)S(1)}, u32[]{:S(2)}, u32[]{:S(2)}) collective-permute-start(bf16[2,2,64,512]{3,2,1,0:T(8,128)(2,1)S(1)} %get-tuple-element.52), channel_id=1, source_target_pairs={{0,3},{1,0},{2,1},{3,2},{4,7},{5,4},{6,5},{7,6},{8,11},{9,8},{10,9... | collective-permute-start | bytes 786440 | tf_op jit(solution)/shard_map/ppermute | solution.py:280

commit v6 on v5

--- a/solution.py
+++ b/solution.py
@@ -162,7 +162,7 @@
 def add_high(got):
     n = len(got)
     experts, _, rows, cols = got[0].shape
-    step = 2
+    step = 4
     return pl.pallas_call(
         functools.partial(add_high_body, n),
         out_shape=jax.ShapeDtypeStruct((experts, n, 2, 2, rows, cols // n), got[0].dtype),

time: 141 us -> 141 us (level)
  no operation moved by 1% of the time
where the time goes in v6:
time: 141 us; the launch traced here: 140 us
  waiting for transfers between devices  65.3 us (46%)
  starting transfers between devices  39.3 us (28%)
  Pallas kernels  24.6 us (17%)
  local copies, waits for them, and re-layouts  10.7 us (8%)
    ppermute x12, waiting for transfers between devices, shifted(): return lax.ppermute(x, axis, [(i, (i + by) % n) for i in range(n)])  33.1 us
    ppermute x12, starting transfers between devices, shifted(): return lax.ppermute(x, axis, [(i, (i + by) % n) for i in range(n)])  22.4 us
    all_to_all x1, waiting for transfers between devices, over_z(): lax.all_to_all(flat, MESH, 0, 0, axis_index_groups=groups, tiled=True)  17.5 us
    all_to_all x1, waiting for transfers between devices, local(): lax.all_to_all(added.reshape(-1, *added.shape[2:]), ('z', 'core', 'shard'...  12.8 us
    pallas_call x2, Pallas kernels, pack(): pl.pallas_call(functools.partial(pack_body, low, rows, shifts, len(after)...  11.2 us
    all_to_all x1, starting transfers between devices, local(): lax.all_to_all(added.reshape(-1, *added.shape[2:]), ('z', 'core', 'shard'...  6.95 us
    all_to_all x1, starting transfers between devices, over_z(): lax.all_to_all(flat, MESH, 0, 0, axis_index_groups=groups, tiled=True)  5.41 us
    all_to_all x1, starting transfers between devices, local(): lax.all_to_all(moved.reshape(nz, 2, nx, *moved.shape[1:]), 'task', 0, 0,...  4.59 us
  transfers between devices with their start and end apart: 15, of which 9 were waited for; matrix products, arithmetic and copies ran while one was open for 7% of the time, Pallas kernels for 11%

profile of v6, /device:TPU:0, one launch (start us, length us, event | category | flops | bytes accessed | tf_op | source)
XLA Modules:
  0.0 140.0 jit_solution(16699983498368982525)
XLA Ops:
  0.0 5.9 %pack.2 = (bf16[4,2,2,64,2048]{4,3,2,1,0:T(8,128)(2,1)}, bf16[8,2,16,2048]{3,2,1,0:T(8,128)(2,1)}, s32[1]{0:T(128)}) custom-call(s32[8,32]{1,0:T(8,128)} %bitcast.29, s32[8,32]{1,0:T(8,128)} %bitcast.31, bf16[8,256,2048]{2,1,0:T(8,128)(2,1)} %bitcast.22, bf16[8,256,2048]{2,1,0:T(8,128)(2,1)} %bitcast.24), custom_call_target="tpu_custom_call" | custom-call | tf_op jit(solution)/shard_map/pack/pallas_call | solution.py:84
  5.9 5.4 %all-to-all-start = ((bf16[8,2,64,2048]{3,2,1,0:T(8,128)(2,1)}), bf16[8,2,64,2048]{3,2,1,0:T(8,128)(2,1)}, u32[]{:S(2)}, u32[]{:S(2)}) async-start(bf16[8,2,64,2048]{3,2,1,0:T(8,128)(2,1)} %bitcast.28), calls=%async_computation | async-start | bytes 8388608 | tf_op jit(solution)/shard_map/all_to_all | solution.py:297
  11.3 6.2 %collective-permute-start.1 = (bf16[8,2,16,2048]{3,2,1,0:T(8,128)(2,1)}, bf16[8,2,16,2048]{3,2,1,0:T(8,128)(2,1)S(1)}, u32[]{:S(2)}, u32[]{:S(2)}) collective-permute-start(bf16[8,2,16,2048]{3,2,1,0:T(8,128)(2,1)} %get-tuple-element.33), channel_id=1, source_target_pairs={{0,8},{4,12},{8,0},{12,4},{1,9},{5,13},{9,1},{13,5},{2,10},{6,14},... | collective-permute-start | bytes 3145736 | tf_op jit(solution)/shard_map/ppermute | solution.py:280
  17.5 5.3 %pack.3 = (bf16[8,2,16,2048]{3,2,1,0:T(8,128)(2,1)}, bf16[8,2,16,2048]{3,2,1,0:T(8,128)(2,1)}, bf16[8,2,16,2048]{3,2,1,0:T(8,128)(2,1)}, s32[1]{0:T(128)}) custom-call(s32[8,32]{1,0:T(8,128)} %bitcast.30, s32[8,32]{1,0:T(8,128)} %bitcast.32, bf16[8,256,2048]{2,1,0:T(8,128)(2,1)} %bitcast.23, bf16[8,256,2048]{2,1,0:T(8,128)(2,1)} %bitcast.25, ...), custom_call_target="tpu_custom_call" | custom-call | tf_op jit(solution)/shard_map/pack/pallas_call | solution.py:84
  22.9 2.0 %collective-permute-start = (bf16[8,2,16,2048]{3,2,1,0:T(8,128)(2,1)}, bf16[8,2,16,2048]{3,2,1,0:T(8,128)(2,1)}, u32[]{:S(2)}, u32[]{:S(2)}) collective-permute-start(bf16[8,2,16,2048]{3,2,1,0:T(8,128)(2,1)} %get-tuple-element.32), channel_id=1, source_target_pairs={{0,4},{4,8},{8,12},{12,0},{1,5},{5,9},{9,13},{13,1},{2,6},{6,10},{... | collective-permute-start | bytes 3145736 | tf_op jit(solution)/shard_map/ppermute | solution.py:280
  24.9 2.4 %slice.17 = bf16[2,4,2,64,512]{4,3,2,1,0:T(8,128)(2,1)} slice(bf16[2,4,2,128,512]{4,3,2,1,0:T(8,128)(2,1)} %bitcast.26), slice={[0:2], [0:4], [0:2], [0:64], [0:512]} | slice | bytes 2097152 | tf_op jit(solution)/shard_map/slice | solution.py:320
  27.3 2.2 %dynamic-slice_bitcast_fusion = (bf16[2,2,64,512]{3,2,1,0:T(8,128)(2,1)S(1)}, bf16[2,2,64,512]{3,2,1,0:T(8,128)(2,1)}, bf16[2,2,64,512]{3,2,1,0:T(8,128)(2,1)}, bf16[2,2,64,512]{3,2,1,0:T(8,128)(2,1)S(1)}) fusion(bf16[2,4,2,64,512]{4,3,2,1,0:T(8,128)(2,1)} %slice.17, s32[]{:T(128)S(6)} %select_n.16, s32[]{:T(128)S(6)} %select_n.15, s32[]{:T(128)S(6)} %select_n.14, ...), kind=kLoop, calls=%fused_computation.2 | loop fusion | bytes 2097168 | tf_op jit(solution)/shard_map/jit(dynamic_index_in_dim)/squeeze | solution.py:320
  29.5 2.8 %collective-permute-start.5 = (bf16[2,2,64,512]{3,2,1,0:T(8,128)(2,1)S(1)}, bf16[2,2,64,512]{3,2,1,0:T(8,128)(2,1)S(1)}, u32[]{:S(2)}, u32[]{:S(2)}) collective-permute-start(bf16[2,2,64,512]{3,2,1,0:T(8,128)(2,1)S(1)} %get-tuple-element.55), channel_id=1, source_target_pairs={{0,3},{1,0},{2,1},{3,2},{4,7},{5,4},{6,5},{7,6},{8,11},{9,8},{10,9... | collective-permute-start | bytes 786440 | tf_op jit(solution)/shard_map/ppermute | solution.py:280
  32.2 0.8 collective-permute-start.4
  33.0 9.9 %collective-permute-done.5.rest_6_ = bf16[2,2,64,512]{3,2,1,0:T(8,128)(2,1)S(1)} collective-permute-done((bf16[2,2,64,512]{3,2,1,0:T(8,128)(2,1)S(1)}, bf16[2,2,64,512]{3,2,1,0:T(8,128)(2,1)S(1)}, u32[]{:S(2)}, u32[]{:S(2)}) %collective-permute-start.5) | collective-permute-done | bytes 262176 | tf_op jit(solution)/shard_map/ppermute | solution.py:280
  42.9 0.7 copy-done.1
  43.6 17.5 %all-to-all-done = bf16[8,2,64,2048]{3,2,1,0:T(8,128)(2,1)} async-done(((bf16[8,2,64,2048]{3,2,1,0:T(8,128)(2,1)}), bf16[8,2,64,2048]{3,2,1,0:T(8,128)(2,1)}, u32[]{:S(2)}, u32[]{:S(2)}) %all-to-all-start) | async-done | bytes 4194336 | tf_op jit(solution)/shard_map/all_to_all | solution.py:297
  61.1 2.3 %slice.20 = bf16[2,2,64,2048]{3,2,1,0:T(8,128)(2,1)} slice(bf16[8,2,64,2048]{3,2,1,0:T(8,128)(2,1)} %all-to-all-done), slice={[4:6], [0:2], [0:64], [0:2048]} | slice | bytes 2097152 | tf_op jit(solution)/shard_map/slice | solution.py:322
  63.4 0.9 collective-permute-done.2.refs_3_
  64.3 2.8 %collective-permute-start.6 = (bf16[2,2,64,2048]{3,2,1,0:T(8,128)(2,1)}, bf16[2,2,64,2048]{3,2,1,0:T(8,128)(2,1)}, u32[]{:S(2)}, u32[]{:S(2)}) collective-permute-start(bf16[2,2,64,2048]{3,2,1,0:T(8,128)(2,1)} %slice.20), channel_id=1, source_target_pairs={{0,8},{4,12},{8,0},{12,4},{1,9},{5,13},{9,1},{13,5},{2,10},{6,14},... | collective-permute-start | bytes 3145736 | tf_op jit(solution)/shard_map/ppermute | solution.py:280
  67.0 4.1 %add_high.1 = bf16[8,4,2,2,16,512]{5,4,3,2,1,0:T(8,128)(2,1)} custom-call(bf16[8,2,16,2048]{3,2,1,0:T(8,128)(2,1)S(1)} %copy-done, bf16[8,2,16,2048]{3,2,1,0:T(8,128)(2,1)} %collective-permute-done.refs_1_, bf16[8,2,16,2048]{3,2,1,0:T(8,128)(2,1)S(1)} %collective-permute-done.1.refs_2_, bf16[8,2,16,2048]{3,2,1,0:T(8,128)(2,1)S(1)} %collective-permute-done.2.refs_3_), custom_call_target="tpu_custom_call" | custom-call | tf_op jit(solution)/shard_map/add_high/pallas_call | solution.py:166
  71.1 6.9 %all-to-all-start.1 = ((bf16[32,2,2,16,512]{4,3,2,1,0:T(8,128)(2,1)}), bf16[32,2,2,16,512]{4,3,2,1,0:T(8,128)(2,1)}, u32[]{:S(2)}, u32[]{:S(2)}) async-start(bf16[32,2,2,16,512]{4,3,2,1,0:T(8,128)(2,1)} %bitcast.11), calls=%async_computation.1 | async-start | bytes 4194304 | tf_op jit(solution)/shard_map/all_to_all | solution.py:327
  78.1 3.1 %slice_bitcast_fusion = (bf16[2,2,64,2048]{3,2,1,0:T(8,128)(2,1)}, bf16[2,2,64,2048]{3,2,1,0:T(8,128)(2,1)}) fusion(bf16[4,2,2,64,2048]{4,3,2,1,0:T(8,128)(2,1)} %bitcast.5.first), kind=kLoop, calls=%fused_computation | loop fusion | bytes 4194304 | tf_op jit(solution)/shard_map/squeeze | solution.py:326
  81.2 2.0 %collective-permute-start.7 = (bf16[2,2,64,2048]{3,2,1,0:T(8,128)(2,1)}, bf16[2,2,64,2048]{3,2,1,0:T(8,128)(2,1)S(1)}, u32[]{:S(2)}, u32[]{:S(2)}) collective-permute-start(bf16[2,2,64,2048]{3,2,1,0:T(8,128)(2,1)} %get-tuple-element.54), channel_id=1, source_target_pairs={{0,4},{4,8},{8,12},{12,0},{1,5},{5,9},{9,13},{13,1},{2,6},{6,10},{... | collective-permute-start | bytes 3145736 | tf_op jit(solution)/shard_map/ppermute | solution.py:280
  83.2 9.0 %collective-permute-done.6.refs_0_.rest_1_ = bf16[2,2,64,2048]{3,2,1,0:T(8,128)(2,1)} collective-permute-done((bf16[2,2,64,2048]{3,2,1,0:T(8,128)(2,1)}, bf16[2,2,64,2048]{3,2,1,0:T(8,128)(2,1)}, u32[]{:S(2)}, u32[]{:S(2)}) %collective-permute-start.6) | collective-permute-done | bytes 1048608 | tf_op jit(solution)/shard_map/ppermute | solution.py:280
  92.7 12.8 %all-to-all-done.1 = bf16[32,2,2,16,512]{4,3,2,1,0:T(8,128)(2,1)} async-done(((bf16[32,2,2,16,512]{4,3,2,1,0:T(8,128)(2,1)}), bf16[32,2,2,16,512]{4,3,2,1,0:T(8,128)(2,1)}, u32[]{:S(2)}, u32[]{:S(2)}) %all-to-all-start.1) | async-done | bytes 2097184 | tf_op jit(solution)/shard_map/all_to_all | solution.py:327
  105.5 4.6 %all-to-all-start.2 = ((bf16[4,2,4,2,2,16,512]{6,5,4,3,2,1,0:T(8,128)(2,1)}), bf16[4,2,4,2,2,16,512]{6,5,4,3,2,1,0:T(8,128)(2,1)}, u32[]{:S(2)}, u32[]{:S(2)}) async-start(bf16[4,2,4,2,2,16,512]{6,5,4,3,2,1,0:T(8,128)(2,1)} %bitcast.12), calls=%async_computation.2 | async-start | bytes 4194304 | tf_op jit(solution)/shard_map/all_to_all | solution.py:331
  110.1 5.2 %collective-permute-done.8.rest_2_ = bf16[2,2,64,2048]{3,2,1,0:T(8,128)(2,1)S(1)} collective-permute-done((bf16[2,2,64,2048]{3,2,1,0:T(8,128)(2,1)}, bf16[2,2,64,2048]{3,2,1,0:T(8,128)(2,1)S(1)}, u32[]{:S(2)}, u32[]{:S(2)}) %collective-permute-start.8) | collective-permute-done | bytes 1048608 | tf_op jit(solution)/shard_map/ppermute | solution.py:280
  115.3 4.4 %merge_low.1 = (bf16[2,2,64,512]{3,2,1,0:T(8,128)(2,1)S(1)}, bf16[2,2,64,512]{3,2,1,0:T(8,128)(2,1)S(1)}, bf16[2,2,64,512]{3,2,1,0:T(8,128)(2,1)S(1)}, bf16[2,2,64,512]{3,2,1,0:T(8,128)(2,1)S(1)}) custom-call(s32[1]{0:T(128)} %fence.1.passed.refs_1_, bf16[4,2,2,64,2048]{4,3,2,1,0:T(8,128)(2,1)} %bitcast.5.first, ...), custom_call_target="tpu_custom_call" | custom-call | flops 99999997952 | tf_op jit(solution)/shard_map/merge_low/pallas_call | solution.py:136
  119.6 1.6 %collective-permute-start.9 = (bf16[2,2,64,512]{3,2,1,0:T(8,128)(2,1)S(1)}, bf16[2,2,64,512]{3,2,1,0:T(8,128)(2,1)S(1)}, u32[]{:S(2)}, u32[]{:S(2)}) collective-permute-start(bf16[2,2,64,512]{3,2,1,0:T(8,128)(2,1)S(1)} %get-tuple-element.50), channel_id=1, source_target_pairs={{0,1},{1,2},{2,3},{3,0},{4,5},{5,6},{6,7},{7,4},{8,9},{9,10},{10,1... | collective-permute-start | bytes 786440 | tf_op jit(solution)/shard_map/ppermute | solution.py:280
  121.2 2.7 %collective-permute-start.10 = (bf16[2,2,64,512]{3,2,1,0:T(8,128)(2,1)S(1)}, bf16[2,2,64,512]{3,2,1,0:T(8,128)(2,1)S(1)}, u32[]{:S(2)}, u32[]{:S(2)}) collective-permute-start(bf16[2,2,64,512]{3,2,1,0:T(8,128)(2,1)S(1)} %get-tuple-element.51), channel_id=1, source_target_pairs={{0,2},{1,3},{2,0},{3,1},{4,6},{5,7},{6,4},{7,5},{8,10},{9,11},{10,... | collective-permute-start | bytes 786440 | tf_op jit(solution)/shard_map/ppermute | solution.py:280
  123.9 1.5 %collective-permute-start.11 = (bf16[2,2,64,512]{3,2,1,0:T(8,128)(2,1)S(1)}, bf16[2,2,64,512]{3,2,1,0:T(8,128)(2,1)S(1)}, u32[]{:S(2)}, u32[]{:S(2)}) collective-permute-start(bf16[2,2,64,512]{3,2,1,0:T(8,128)(2,1)S(1)} %get-tuple-element.52), channel_id=1, source_target_pairs={{0,3},{1,0},{2,1},{3,2},{4,7},{5,4},{6,5},{7,6},{8,11},{9,8},{10,9... | collective-permute-start | bytes 786440 | tf_op jit(solution)/shard_map/ppermute | solution.py:280
  125.4 4.5 %collective-permute-done.9.refs_1_ = bf16[2,2,64,512]{3,2,1,0:T(8,128)(2,1)S(1)} collective-permute-done((bf16[2,2,64,512]{3,2,1,0:T(8,128)(2,1)S(1)}, bf16[2,2,64,512]{3,2,1,0:T(8,128)(2,1)S(1)}, u32[]{:S(2)}, u32[]{:S(2)}) %collective-permute-start.9) | collective-permute-done | bytes 262176 | tf_op jit(solution)/shard_map/ppermute | solution.py:280
  129.8 3.7 %collective-permute-done.10.refs_2_ = bf16[2,2,64,512]{3,2,1,0:T(8,128)(2,1)S(1)} collective-permute-done((bf16[2,2,64,512]{3,2,1,0:T(8,128)(2,1)S(1)}, bf16[2,2,64,512]{3,2,1,0:T(8,128)(2,1)S(1)}, u32[]{:S(2)}, u32[]{:S(2)}) %collective-permute-start.10) | collective-permute-done | bytes 262176 | tf_op jit(solution)/shard_map/ppermute | solution.py:280
  133.5 1.0 place.1.refs_0_
  134.6 2.0 %all-to-all-done.2.got = bf16[4,2,4,2,2,16,512]{6,5,4,3,2,1,0:T(8,128)(2,1)} async-done(((bf16[4,2,4,2,2,16,512]{6,5,4,3,2,1,0:T(8,128)(2,1)}), bf16[4,2,4,2,2,16,512]{6,5,4,3,2,1,0:T(8,128)(2,1)}, u32[]{:S(2)}, u32[]{:S(2)}) %all-to-all-start.2) | async-done | bytes 2097184 | tf_op jit(solution)/shard_map/all_to_all | solution.py:331
  136.6 3.4 %merge_high.1 = bf16[2,4,2,128,512]{4,3,2,1,0:T(8,128)(2,1)} custom-call(bf16[4,2,4,2,2,16,512]{6,5,4,3,2,1,0:T(8,128)(2,1)} %all-to-all-done.2.got, bf16[2,4,2,128,512]{4,3,2,1,0:T(8,128)(2,1)} %bitcast.27, bf16[2,4,2,128,512]{4,3,2,1,0:T(8,128)(2,1)} %place.1.refs_0_, s32[1]{0:T(128)} %fence.1.passed.refs_1_), custom_call_target="tpu_custom_call", output_to_operand_aliasing={{}: (2, {})} | custom-call | tf_op jit(solution)/shard_map/merge_high/pallas_call | solution.py:245
  (15 shorter events, 0.6 us)
Async XLA Ops:
  5.9 55.2 %all-to-all-start = ((bf16[8,2,64,2048]{3,2,1,0:T(8,128)(2,1)}), bf16[8,2,64,2048]{3,2,1,0:T(8,128)(2,1)}, u32[]{:S(2)}, u32[]{:S(2)}) async-start(bf16[8,2,64,2048]{3,2,1,0:T(8,128)(2,1)} %bitcast.28), calls=%async_computation | async-start | bytes 8388608 | tf_op jit(solution)/shard_map/all_to_all | solution.py:297
  11.3 52.1 %collective-permute-start.1 = (bf16[8,2,16,2048]{3,2,1,0:T(8,128)(2,1)}, bf16[8,2,16,2048]{3,2,1,0:T(8,128)(2,1)S(1)}, u32[]{:S(2)}, u32[]{:S(2)}) collective-permute-start(bf16[8,2,16,2048]{3,2,1,0:T(8,128)(2,1)} %get-tuple-element.33), channel_id=1, source_target_pairs={{0,8},{4,12},{8,0},{12,4},{1,9},{5,13},{9,1},{13,5},{2,10},{6,14},... | collective-permute-start | bytes 3145736 | tf_op jit(solution)/shard_map/ppermute | solution.py:280
  22.8 41.4 %collective-permute-start.2 = (bf16[8,2,16,2048]{3,2,1,0:T(8,128)(2,1)}, bf16[8,2,16,2048]{3,2,1,0:T(8,128)(2,1)S(1)}, u32[]{:S(2)}, u32[]{:S(2)}) collective-permute-start(bf16[8,2,16,2048]{3,2,1,0:T(8,128)(2,1)} %get-tuple-element.34), channel_id=1, source_target_pairs={{0,12},{4,0},{8,4},{12,8},{1,13},{5,1},{9,5},{13,9},{2,14},{6,2},{... | collective-permute-start | bytes 3145736 | tf_op jit(solution)/shard_map/ppermute | solution.py:280
  22.9 41.3 %collective-permute-start = (bf16[8,2,16,2048]{3,2,1,0:T(8,128)(2,1)}, bf16[8,2,16,2048]{3,2,1,0:T(8,128)(2,1)}, u32[]{:S(2)}, u32[]{:S(2)}) collective-permute-start(bf16[8,2,16,2048]{3,2,1,0:T(8,128)(2,1)} %get-tuple-element.32), channel_id=1, source_target_pairs={{0,4},{4,8},{8,12},{12,0},{1,5},{5,9},{9,13},{13,1},{2,6},{6,10},{... | collective-permute-start | bytes 3145736 | tf_op jit(solution)/shard_map/ppermute | solution.py:280
  27.3 39.7 %copy-start = (bf16[8,2,16,2048]{3,2,1,0:T(8,128)(2,1)S(1)}, bf16[8,2,16,2048]{3,2,1,0:T(8,128)(2,1)}, u32[]{:S(2)}) copy-start(bf16[8,2,16,2048]{3,2,1,0:T(8,128)(2,1)} %get-tuple-element.36.refs_0_) | copy-start | bytes 3145732
  29.5 13.4 %collective-permute-start.5 = (bf16[2,2,64,512]{3,2,1,0:T(8,128)(2,1)S(1)}, bf16[2,2,64,512]{3,2,1,0:T(8,128)(2,1)S(1)}, u32[]{:S(2)}, u32[]{:S(2)}) collective-permute-start(bf16[2,2,64,512]{3,2,1,0:T(8,128)(2,1)S(1)} %get-tuple-element.55), channel_id=1, source_target_pairs={{0,3},{1,0},{2,1},{3,2},{4,7},{5,4},{6,5},{7,6},{8,11},{9,8},{10,9... | collective-permute-start | bytes 786440 | tf_op jit(solution)/shard_map/ppermute | solution.py:280
  32.2 31.2 %collective-permute-start.4 = (bf16[2,2,64,512]{3,2,1,0:T(8,128)(2,1)}, bf16[2,2,64,512]{3,2,1,0:T(8,128)(2,1)}, u32[]{:S(2)}, u32[]{:S(2)}) collective-permute-start(bf16[2,2,64,512]{3,2,1,0:T(8,128)(2,1)} %get-tuple-element.56), channel_id=1, source_target_pairs={{0,2},{1,3},{2,0},{3,1},{4,6},{5,7},{6,4},{7,5},{8,10},{9,11},{10,... | collective-permute-start | bytes 786440 | tf_op jit(solution)/shard_map/ppermute | solution.py:280
  42.9 0.7 copy-start.1
  43.6 19.8 %collective-permute-start.3 = (bf16[2,2,64,512]{3,2,1,0:T(8,128)(2,1)}, bf16[2,2,64,512]{3,2,1,0:T(8,128)(2,1)}, u32[]{:S(2)}, u32[]{:S(2)}) collective-permute-start(bf16[2,2,64,512]{3,2,1,0:T(8,128)(2,1)} %get-tuple-element.57), channel_id=1, source_target_pairs={{0,1},{1,2},{2,3},{3,0},{4,5},{5,6},{6,7},{7,4},{8,9},{9,10},{10,1... | collective-permute-start | bytes 786440 | tf_op jit(solution)/shard_map/ppermute | solution.py:280
  64.3 28.0 %collective-permute-start.6 = (bf16[2,2,64,2048]{3,2,1,0:T(8,128)(2,1)}, bf16[2,2,64,2048]{3,2,1,0:T(8,128)(2,1)}, u32[]{:S(2)}, u32[]{:S(2)}) collective-permute-start(bf16[2,2,64,2048]{3,2,1,0:T(8,128)(2,1)} %slice.20), channel_id=1, source_target_pairs={{0,8},{4,12},{8,0},{12,4},{1,9},{5,13},{9,1},{13,5},{2,10},{6,14},... | collective-permute-start | bytes 3145736 | tf_op jit(solution)/shard_map/ppermute | solution.py:280
  71.1 34.4 %all-to-all-start.1 = ((bf16[32,2,2,16,512]{4,3,2,1,0:T(8,128)(2,1)}), bf16[32,2,2,16,512]{4,3,2,1,0:T(8,128)(2,1)}, u32[]{:S(2)}, u32[]{:S(2)}) async-start(bf16[32,2,2,16,512]{4,3,2,1,0:T(8,128)(2,1)} %bitcast.11), calls=%async_computation.1 | async-start | bytes 4194304 | tf_op jit(solution)/shard_map/all_to_all | solution.py:327
  81.2 34.1 %collective-permute-start.8 = (bf16[2,2,64,2048]{3,2,1,0:T(8,128)(2,1)}, bf16[2,2,64,2048]{3,2,1,0:T(8,128)(2,1)S(1)}, u32[]{:S(2)}, u32[]{:S(2)}) collective-permute-start(bf16[2,2,64,2048]{3,2,1,0:T(8,128)(2,1)} %get-tuple-element.53), channel_id=1, source_target_pairs={{0,12},{4,0},{8,4},{12,8},{1,13},{5,1},{9,5},{13,9},{2,14},{6,2},{... | collective-permute-start | bytes 3145736 | tf_op jit(solution)/shard_map/ppermute | solution.py:280
  81.2 34.1 %collective-permute-start.7 = (bf16[2,2,64,2048]{3,2,1,0:T(8,128)(2,1)}, bf16[2,2,64,2048]{3,2,1,0:T(8,128)(2,1)S(1)}, u32[]{:S(2)}, u32[]{:S(2)}) collective-permute-start(bf16[2,2,64,2048]{3,2,1,0:T(8,128)(2,1)} %get-tuple-element.54), channel_id=1, source_target_pairs={{0,4},{4,8},{8,12},{12,0},{1,5},{5,9},{9,13},{13,1},{2,6},{6,10},{... | collective-permute-start | bytes 3145736 | tf_op jit(solution)/shard_map/ppermute | solution.py:280
  105.5 9.8 %copy-start.2 = (bf16[2,2,64,512]{3,2,1,0:T(8,128)(2,1)S(1)}, bf16[2,2,64,512]{3,2,1,0:T(8,128)(2,1)}, u32[]{:S(2)}) copy-start(bf16[2,2,64,512]{3,2,1,0:T(8,128)(2,1)} %copy-done.1) | copy-start | bytes 786436
  105.5 31.1 %all-to-all-start.2 = ((bf16[4,2,4,2,2,16,512]{6,5,4,3,2,1,0:T(8,128)(2,1)}), bf16[4,2,4,2,2,16,512]{6,5,4,3,2,1,0:T(8,128)(2,1)}, u32[]{:S(2)}, u32[]{:S(2)}) async-start(bf16[4,2,4,2,2,16,512]{6,5,4,3,2,1,0:T(8,128)(2,1)} %bitcast.12), calls=%async_computation.2 | async-start | bytes 4194304 | tf_op jit(solution)/shard_map/all_to_all | solution.py:331
  119.6 10.2 %collective-permute-start.9 = (bf16[2,2,64,512]{3,2,1,0:T(8,128)(2,1)S(1)}, bf16[2,2,64,512]{3,2,1,0:T(8,128)(2,1)S(1)}, u32[]{:S(2)}, u32[]{:S(2)}) collective-permute-start(bf16[2,2,64,512]{3,2,1,0:T(8,128)(2,1)S(1)} %get-tuple-element.50), channel_id=1, source_target_pairs={{0,1},{1,2},{2,3},{3,0},{4,5},{5,6},{6,7},{7,4},{8,9},{9,10},{10,1... | collective-permute-start | bytes 786440 | tf_op jit(solution)/shard_map/ppermute | solution.py:280
  121.2 12.3 %collective-permute-start.10 = (bf16[2,2,64,512]{3,2,1,0:T(8,128)(2,1)S(1)}, bf16[2,2,64,512]{3,2,1,0:T(8,128)(2,1)S(1)}, u32[]{:S(2)}, u32[]{:S(2)}) collective-permute-start(bf16[2,2,64,512]{3,2,1,0:T(8,128)(2,1)S(1)} %get-tuple-element.51), channel_id=1, source_target_pairs={{0,2},{1,3},{2,0},{3,1},{4,6},{5,7},{6,4},{7,5},{8,10},{9,11},{10,... | collective-permute-start | bytes 786440 | tf_op jit(solution)/shard_map/ppermute | solution.py:280
  123.9 9.7 %collective-permute-start.11 = (bf16[2,2,64,512]{3,2,1,0:T(8,128)(2,1)S(1)}, bf16[2,2,64,512]{3,2,1,0:T(8,128)(2,1)S(1)}, u32[]{:S(2)}, u32[]{:S(2)}) collective-permute-start(bf16[2,2,64,512]{3,2,1,0:T(8,128)(2,1)S(1)} %get-tuple-element.52), channel_id=1, source_target_pairs={{0,3},{1,0},{2,1},{3,2},{4,7},{5,4},{6,5},{7,6},{8,11},{9,8},{10,9... | collective-permute-start | bytes 786440 | tf_op jit(solution)/shard_map/ppermute | solution.py:280

commit v7 on v6

--- a/solution.py
+++ b/solution.py
@@ -259,6 +259,25 @@
     )(got, base, whole, passed)
 
 
+def cut_body(which, whole, out, sem):
+    copy = pltpu.make_async_copy(whole.at[which], out, sem)
+    copy.start()
+    copy.wait()
+
+
+def cut(whole, which):
+    return pl.pallas_call(
+        functools.partial(cut_body, which),
+        out_shape=jax.ShapeDtypeStruct(whole.shape[1:], whole.dtype),
+        in_specs=[HBM],
+        out_specs=VMEM,
+        scratch_shapes=[pltpu.SemaphoreType.DMA],
+        compiler_params=PARAMS,
+        cost_estimate=SHORT,
+        name="cut",
+    )(whole)
+
+
 def fence_body(*refs):
     refs[-1][0] = 0
 
@@ -319,7 +338,7 @@
     for d in range(nx):
         part = lax.dynamic_index_in_dim(base[:, :, :, :LOW], lax.rem(x + d, nx), 1, keepdims=False)
         prior.append(shifted(part, "shard", d) if d else part)
-    far, got_high, prior = hold((got_low[2], got_high, prior))
+    far, got_high, prior = hold((cut(got_low, 2), got_high, prior))
     far = shifted(far, "task", 2)
     added = add_high(got_high)
     near, added = hold((got_low, added))

time: 141 us -> 140 us (level)
  local copies, waits for them, and re-layouts: 10.7 us -> 6.08 us
  waiting for transfers between devices: 65.3 us -> 68.5 us
    ppermute x12, waiting for transfers between devices: 33.1 us -> 35.5 us  [shifted(): return lax.ppermute(x, axis, [(i, (i + by) % n) for i in range(n)])]
    slice x1 -> x0, local copies, waits for them, and re-layouts: 2.3 us -> none  [local(): far, got_high, prior = hold((got_low[2], got_high, prior))]
    all_to_all x1, waiting for transfers between devices: 17.5 us -> 19.7 us  [over_z(): lax.all_to_all(flat, MESH, 0, 0, axis_index_groups=groups, tiled=True)]
  transfers between devices with their start and end apart: 15 -> 15, of which waited for: 9 -> 9; matrix products, arithmetic and copies ran while one was open for 7% -> 4% of each run, Pallas kernels for 11% -> 12%
where the time goes in v7:
time: 140 us; the launch traced here: 139 us
  waiting for transfers between devices  68.5 us (49%)
  starting transfers between devices  38.4 us (27%)
  Pallas kernels  25.9 us (18%)
  local copies, waits for them, and re-layouts  6.08 us (4%)
    ppermute x12, waiting for transfers between devices, shifted(): return lax.ppermute(x, axis, [(i, (i + by) % n) for i in range(n)])  35.5 us
    ppermute x12, starting transfers between devices, shifted(): return lax.ppermute(x, axis, [(i, (i + by) % n) for i in range(n)])  22.4 us
    all_to_all x1, waiting for transfers between devices, over_z(): lax.all_to_all(flat, MESH, 0, 0, axis_index_groups=groups, tiled=True)  19.7 us
    all_to_all x1, waiting for transfers between devices, local(): lax.all_to_all(added.reshape(-1, *added.shape[2:]), ('z', 'core', 'shard'...  12 us
    pallas_call x2, Pallas kernels, pack(): pl.pallas_call(functools.partial(pack_body, low, rows, shifts, len(after)...  11.2 us
    all_to_all x1, starting transfers between devices, local(): lax.all_to_all(added.reshape(-1, *added.shape[2:]), ('z', 'core', 'shard'...  6 us
    all_to_all x1, starting transfers between devices, over_z(): lax.all_to_all(flat, MESH, 0, 0, axis_index_groups=groups, tiled=True)  5.41 us
    all_to_all x1, starting transfers between devices, local(): lax.all_to_all(moved.reshape(nz, 2, nx, *moved.shape[1:]), 'task', 0, 0,...  4.59 us
  transfers between devices with their start and end apart: 15, of which 9 were waited for; matrix products, arithmetic and copies ran while one was open for 4% of the time, Pallas kernels for 12%

profile of v7, /device:TPU:0, one launch (start us, length us, event | category | flops | bytes accessed | tf_op | source)
XLA Modules:
  0.0 139.0 jit_solution(17855787090969595485)
XLA Ops:
  0.0 5.9 %pack.2 = (bf16[4,2,2,64,2048]{4,3,2,1,0:T(8,128)(2,1)}, bf16[8,2,16,2048]{3,2,1,0:T(8,128)(2,1)}, s32[1]{0:T(128)}) custom-call(s32[8,32]{1,0:T(8,128)} %bitcast.29, s32[8,32]{1,0:T(8,128)} %bitcast.31, bf16[8,256,2048]{2,1,0:T(8,128)(2,1)} %bitcast.22, bf16[8,256,2048]{2,1,0:T(8,128)(2,1)} %bitcast.24), custom_call_target="tpu_custom_call" | custom-call | tf_op jit(solution)/shard_map/pack/pallas_call | solution.py:84
  5.9 5.4 %all-to-all-start = ((bf16[8,2,64,2048]{3,2,1,0:T(8,128)(2,1)}), bf16[8,2,64,2048]{3,2,1,0:T(8,128)(2,1)}, u32[]{:S(2)}, u32[]{:S(2)}) async-start(bf16[8,2,64,2048]{3,2,1,0:T(8,128)(2,1)} %bitcast.28), calls=%async_computation | async-start | bytes 8388608 | tf_op jit(solution)/shard_map/all_to_all | solution.py:316
  11.3 6.2 %collective-permute-start.1 = (bf16[8,2,16,2048]{3,2,1,0:T(8,128)(2,1)}, bf16[8,2,16,2048]{3,2,1,0:T(8,128)(2,1)S(1)}, u32[]{:S(2)}, u32[]{:S(2)}) collective-permute-start(bf16[8,2,16,2048]{3,2,1,0:T(8,128)(2,1)} %get-tuple-element.33), channel_id=1, source_target_pairs={{0,8},{4,12},{8,0},{12,4},{1,9},{5,13},{9,1},{13,5},{2,10},{6,14},... | collective-permute-start | bytes 3145736 | tf_op jit(solution)/shard_map/ppermute | solution.py:299
  17.5 5.3 %pack.3 = (bf16[8,2,16,2048]{3,2,1,0:T(8,128)(2,1)}, bf16[8,2,16,2048]{3,2,1,0:T(8,128)(2,1)}, bf16[8,2,16,2048]{3,2,1,0:T(8,128)(2,1)}, s32[1]{0:T(128)}) custom-call(s32[8,32]{1,0:T(8,128)} %bitcast.30, s32[8,32]{1,0:T(8,128)} %bitcast.32, bf16[8,256,2048]{2,1,0:T(8,128)(2,1)} %bitcast.23, bf16[8,256,2048]{2,1,0:T(8,128)(2,1)} %bitcast.25, ...), custom_call_target="tpu_custom_call" | custom-call | tf_op jit(solution)/shard_map/pack/pallas_call | solution.py:84
  22.9 2.0 %collective-permute-start = (bf16[8,2,16,2048]{3,2,1,0:T(8,128)(2,1)}, bf16[8,2,16,2048]{3,2,1,0:T(8,128)(2,1)}, u32[]{:S(2)}, u32[]{:S(2)}) collective-permute-start(bf16[8,2,16,2048]{3,2,1,0:T(8,128)(2,1)} %get-tuple-element.32), channel_id=1, source_target_pairs={{0,4},{4,8},{8,12},{12,0},{1,5},{5,9},{9,13},{13,1},{2,6},{6,10},{... | collective-permute-start | bytes 3145736 | tf_op jit(solution)/shard_map/ppermute | solution.py:299
  24.9 1.3 slice.12
  26.3 0.9 dynamic-slice_bitcast_fusion
  27.2 2.8 %collective-permute-start.5 = (bf16[2,2,64,512]{3,2,1,0:T(8,128)(2,1)S(1)}, bf16[2,2,64,512]{3,2,1,0:T(8,128)(2,1)S(1)}, u32[]{:S(2)}, u32[]{:S(2)}) collective-permute-start(bf16[2,2,64,512]{3,2,1,0:T(8,128)(2,1)S(1)} %get-tuple-element.55), channel_id=1, source_target_pairs={{0,3},{1,0},{2,1},{3,2},{4,7},{5,4},{6,5},{7,6},{8,11},{9,8},{10,9... | collective-permute-start | bytes 786440 | tf_op jit(solution)/shard_map/ppermute | solution.py:299
  30.0 0.8 collective-permute-start.4
  30.8 9.9 %collective-permute-done.5.rest_6_ = bf16[2,2,64,512]{3,2,1,0:T(8,128)(2,1)S(1)} collective-permute-done((bf16[2,2,64,512]{3,2,1,0:T(8,128)(2,1)S(1)}, bf16[2,2,64,512]{3,2,1,0:T(8,128)(2,1)S(1)}, u32[]{:S(2)}, u32[]{:S(2)}) %collective-permute-start.5) | collective-permute-done | bytes 262176 | tf_op jit(solution)/shard_map/ppermute | solution.py:299
  40.6 0.7 copy-done.1
  41.3 19.7 %all-to-all-done = bf16[8,2,64,2048]{3,2,1,0:T(8,128)(2,1)} async-done(((bf16[8,2,64,2048]{3,2,1,0:T(8,128)(2,1)}), bf16[8,2,64,2048]{3,2,1,0:T(8,128)(2,1)}, u32[]{:S(2)}, u32[]{:S(2)}) %all-to-all-start) | async-done | bytes 4194336 | tf_op jit(solution)/shard_map/all_to_all | solution.py:316
  61.1 1.3 cut.1
  62.5 1.8 %collective-permute-done.2.refs_3_ = bf16[8,2,16,2048]{3,2,1,0:T(8,128)(2,1)S(1)} collective-permute-done((bf16[8,2,16,2048]{3,2,1,0:T(8,128)(2,1)}, bf16[8,2,16,2048]{3,2,1,0:T(8,128)(2,1)S(1)}, u32[]{:S(2)}, u32[]{:S(2)}) %collective-permute-start.2) | collective-permute-done | bytes 1048608 | tf_op jit(solution)/shard_map/ppermute | solution.py:299
  64.3 2.8 %collective-permute-start.6 = (bf16[2,2,64,2048]{3,2,1,0:T(8,128)(2,1)S(1)}, bf16[2,2,64,2048]{3,2,1,0:T(8,128)(2,1)}, u32[]{:S(2)}, u32[]{:S(2)}) collective-permute-start(bf16[2,2,64,2048]{3,2,1,0:T(8,128)(2,1)S(1)} %cut.1), channel_id=1, source_target_pairs={{0,8},{4,12},{8,0},{12,4},{1,9},{5,13},{9,1},{13,5},{2,10},{6,14},... | collective-permute-start | bytes 3145736 | tf_op jit(solution)/shard_map/ppermute | solution.py:299
  67.0 4.1 %add_high.1 = bf16[8,4,2,2,16,512]{5,4,3,2,1,0:T(8,128)(2,1)} custom-call(bf16[8,2,16,2048]{3,2,1,0:T(8,128)(2,1)S(1)} %copy-done, bf16[8,2,16,2048]{3,2,1,0:T(8,128)(2,1)} %collective-permute-done.refs_1_, bf16[8,2,16,2048]{3,2,1,0:T(8,128)(2,1)S(1)} %collective-permute-done.1.refs_2_, bf16[8,2,16,2048]{3,2,1,0:T(8,128)(2,1)S(1)} %collective-permute-done.2.refs_3_), custom_call_target="tpu_custom_call" | custom-call | tf_op jit(solution)/shard_map/add_high/pallas_call | solution.py:166
  71.1 6.0 %all-to-all-start.1 = ((bf16[32,2,2,16,512]{4,3,2,1,0:T(8,128)(2,1)}), bf16[32,2,2,16,512]{4,3,2,1,0:T(8,128)(2,1)}, u32[]{:S(2)}, u32[]{:S(2)}) async-start(bf16[32,2,2,16,512]{4,3,2,1,0:T(8,128)(2,1)} %bitcast.11), calls=%async_computation.1 | async-start | bytes 4194304 | tf_op jit(solution)/shard_map/all_to_all | solution.py:346
  77.1 3.1 %slice_bitcast_fusion = (bf16[2,2,64,2048]{3,2,1,0:T(8,128)(2,1)}, bf16[2,2,64,2048]{3,2,1,0:T(8,128)(2,1)}) fusion(bf16[4,2,2,64,2048]{4,3,2,1,0:T(8,128)(2,1)} %bitcast.5.whole.first), kind=kLoop, calls=%fused_computation | loop fusion | bytes 4194304 | tf_op jit(solution)/shard_map/squeeze | solution.py:345
  80.3 2.0 %collective-permute-start.7 = (bf16[2,2,64,2048]{3,2,1,0:T(8,128)(2,1)}, bf16[2,2,64,2048]{3,2,1,0:T(8,128)(2,1)S(1)}, u32[]{:S(2)}, u32[]{:S(2)}) collective-permute-start(bf16[2,2,64,2048]{3,2,1,0:T(8,128)(2,1)} %get-tuple-element.54), channel_id=1, source_target_pairs={{0,4},{4,8},{8,12},{12,0},{1,5},{5,9},{9,13},{13,1},{2,6},{6,10},{... | collective-permute-start | bytes 3145736 | tf_op jit(solution)/shard_map/ppermute | solution.py:299
  82.3 9.7 %collective-permute-done.6.refs_0_.rest_1_ = bf16[2,2,64,2048]{3,2,1,0:T(8,128)(2,1)} collective-permute-done((bf16[2,2,64,2048]{3,2,1,0:T(8,128)(2,1)S(1)}, bf16[2,2,64,2048]{3,2,1,0:T(8,128)(2,1)}, u32[]{:S(2)}, u32[]{:S(2)}) %collective-permute-start.6) | collective-permute-done | bytes 1048608 | tf_op jit(solution)/shard_map/ppermute | solution.py:299
  92.5 12.0 %all-to-all-done.1 = bf16[32,2,2,16,512]{4,3,2,1,0:T(8,128)(2,1)} async-done(((bf16[32,2,2,16,512]{4,3,2,1,0:T(8,128)(2,1)}), bf16[32,2,2,16,512]{4,3,2,1,0:T(8,128)(2,1)}, u32[]{:S(2)}, u32[]{:S(2)}) %all-to-all-start.1) | async-done | bytes 2097184 | tf_op jit(solution)/shard_map/all_to_all | solution.py:346
  104.5 4.6 %all-to-all-start.2 = ((bf16[4,2,4,2,2,16,512]{6,5,4,3,2,1,0:T(8,128)(2,1)}), bf16[4,2,4,2,2,16,512]{6,5,4,3,2,1,0:T(8,128)(2,1)}, u32[]{:S(2)}, u32[]{:S(2)}) async-start(bf16[4,2,4,2,2,16,512]{6,5,4,3,2,1,0:T(8,128)(2,1)} %bitcast.12), calls=%async_computation.2 | async-start | bytes 4194304 | tf_op jit(solution)/shard_map/all_to_all | solution.py:350
  109.1 5.1 %collective-permute-done.8.rest_2_ = bf16[2,2,64,2048]{3,2,1,0:T(8,128)(2,1)S(1)} collective-permute-done((bf16[2,2,64,2048]{3,2,1,0:T(8,128)(2,1)}, bf16[2,2,64,2048]{3,2,1,0:T(8,128)(2,1)S(1)}, u32[]{:S(2)}, u32[]{:S(2)}) %collective-permute-start.8) | collective-permute-done | bytes 1048608 | tf_op jit(solution)/shard_map/ppermute | solution.py:299
  114.3 4.4 %merge_low.1 = (bf16[2,2,64,512]{3,2,1,0:T(8,128)(2,1)S(1)}, bf16[2,2,64,512]{3,2,1,0:T(8,128)(2,1)S(1)}, bf16[2,2,64,512]{3,2,1,0:T(8,128)(2,1)S(1)}, bf16[2,2,64,512]{3,2,1,0:T(8,128)(2,1)S(1)}) custom-call(s32[1]{0:T(128)} %fence.1.passed.refs_1_, bf16[4,2,2,64,2048]{4,3,2,1,0:T(8,128)(2,1)} %bitcast.5.whole.first, ...), custom_call_target="tpu_custom_call" | custom-call | flops 99999997952 | tf_op jit(solution)/shard_map/merge_low/pallas_call | solution.py:136
  118.6 1.6 %collective-permute-start.9 = (bf16[2,2,64,512]{3,2,1,0:T(8,128)(2,1)S(1)}, bf16[2,2,64,512]{3,2,1,0:T(8,128)(2,1)S(1)}, u32[]{:S(2)}, u32[]{:S(2)}) collective-permute-start(bf16[2,2,64,512]{3,2,1,0:T(8,128)(2,1)S(1)} %get-tuple-element.50), channel_id=1, source_target_pairs={{0,1},{1,2},{2,3},{3,0},{4,5},{5,6},{6,7},{7,4},{8,9},{9,10},{10,1... | collective-permute-start | bytes 786440 | tf_op jit(solution)/shard_map/ppermute | solution.py:299
  120.2 2.7 %collective-permute-start.10 = (bf16[2,2,64,512]{3,2,1,0:T(8,128)(2,1)S(1)}, bf16[2,2,64,512]{3,2,1,0:T(8,128)(2,1)S(1)}, u32[]{:S(2)}, u32[]{:S(2)}) collective-permute-start(bf16[2,2,64,512]{3,2,1,0:T(8,128)(2,1)S(1)} %get-tuple-element.51), channel_id=1, source_target_pairs={{0,2},{1,3},{2,0},{3,1},{4,6},{5,7},{6,4},{7,5},{8,10},{9,11},{10,... | collective-permute-start | bytes 786440 | tf_op jit(solution)/shard_map/ppermute | solution.py:299
  122.9 1.4 %collective-permute-start.11 = (bf16[2,2,64,512]{3,2,1,0:T(8,128)(2,1)S(1)}, bf16[2,2,64,512]{3,2,1,0:T(8,128)(2,1)S(1)}, u32[]{:S(2)}, u32[]{:S(2)}) collective-permute-start(bf16[2,2,64,512]{3,2,1,0:T(8,128)(2,1)S(1)} %get-tuple-element.52), channel_id=1, source_target_pairs={{0,3},{1,0},{2,1},{3,2},{4,7},{5,4},{6,5},{7,6},{8,11},{9,8},{10,9... | collective-permute-start | bytes 786440 | tf_op jit(solution)/shard_map/ppermute | solution.py:299
  124.4 3.8 %collective-permute-done.9.refs_1_ = bf16[2,2,64,512]{3,2,1,0:T(8,128)(2,1)S(1)} collective-permute-done((bf16[2,2,64,512]{3,2,1,0:T(8,128)(2,1)S(1)}, bf16[2,2,64,512]{3,2,1,0:T(8,128)(2,1)S(1)}, u32[]{:S(2)}, u32[]{:S(2)}) %collective-permute-start.9) | collective-permute-done | bytes 262176 | tf_op jit(solution)/shard_map/ppermute | solution.py:299
  128.2 5.2 %collective-permute-done.10.refs_2_ = bf16[2,2,64,512]{3,2,1,0:T(8,128)(2,1)S(1)} collective-permute-done((bf16[2,2,64,512]{3,2,1,0:T(8,128)(2,1)S(1)}, bf16[2,2,64,512]{3,2,1,0:T(8,128)(2,1)S(1)}, u32[]{:S(2)}, u32[]{:S(2)}) %collective-permute-start.10) | collective-permute-done | bytes 262176 | tf_op jit(solution)/shard_map/ppermute | solution.py:299
  133.3 1.0 place.1.refs_0_
  134.4 1.2 all-to-all-done.2.got
  135.6 3.4 %merge_high.1 = bf16[2,4,2,128,512]{4,3,2,1,0:T(8,128)(2,1)} custom-call(bf16[4,2,4,2,2,16,512]{6,5,4,3,2,1,0:T(8,128)(2,1)} %all-to-all-done.2.got, bf16[2,4,2,128,512]{4,3,2,1,0:T(8,128)(2,1)} %bitcast.27, bf16[2,4,2,128,512]{4,3,2,1,0:T(8,128)(2,1)} %place.1.refs_0_, s32[1]{0:T(128)} %fence.1.passed.refs_1_), custom_call_target="tpu_custom_call", output_to_operand_aliasing={{}: (2, {})} | custom-call | tf_op jit(solution)/shard_map/merge_high/pallas_call | solution.py:245
  (15 shorter events, 0.7 us)
Async XLA Ops:
  5.9 55.2 %all-to-all-start = ((bf16[8,2,64,2048]{3,2,1,0:T(8,128)(2,1)}), bf16[8,2,64,2048]{3,2,1,0:T(8,128)(2,1)}, u32[]{:S(2)}, u32[]{:S(2)}) async-start(bf16[8,2,64,2048]{3,2,1,0:T(8,128)(2,1)} %bitcast.28), calls=%async_computation | async-start | bytes 8388608 | tf_op jit(solution)/shard_map/all_to_all | solution.py:316
  11.3 51.1 %collective-permute-start.1 = (bf16[8,2,16,2048]{3,2,1,0:T(8,128)(2,1)}, bf16[8,2,16,2048]{3,2,1,0:T(8,128)(2,1)S(1)}, u32[]{:S(2)}, u32[]{:S(2)}) collective-permute-start(bf16[8,2,16,2048]{3,2,1,0:T(8,128)(2,1)} %get-tuple-element.33), channel_id=1, source_target_pairs={{0,8},{4,12},{8,0},{12,4},{1,9},{5,13},{9,1},{13,5},{2,10},{6,14},... | collective-permute-start | bytes 3145736 | tf_op jit(solution)/shard_map/ppermute | solution.py:299
  22.8 41.4 %collective-permute-start.2 = (bf16[8,2,16,2048]{3,2,1,0:T(8,128)(2,1)}, bf16[8,2,16,2048]{3,2,1,0:T(8,128)(2,1)S(1)}, u32[]{:S(2)}, u32[]{:S(2)}) collective-permute-start(bf16[8,2,16,2048]{3,2,1,0:T(8,128)(2,1)} %get-tuple-element.34), channel_id=1, source_target_pairs={{0,12},{4,0},{8,4},{12,8},{1,13},{5,1},{9,5},{13,9},{2,14},{6,2},{... | collective-permute-start | bytes 3145736 | tf_op jit(solution)/shard_map/ppermute | solution.py:299
  22.9 41.3 %collective-permute-start = (bf16[8,2,16,2048]{3,2,1,0:T(8,128)(2,1)}, bf16[8,2,16,2048]{3,2,1,0:T(8,128)(2,1)}, u32[]{:S(2)}, u32[]{:S(2)}) collective-permute-start(bf16[8,2,16,2048]{3,2,1,0:T(8,128)(2,1)} %get-tuple-element.32), channel_id=1, source_target_pairs={{0,4},{4,8},{8,12},{12,0},{1,5},{5,9},{9,13},{13,1},{2,6},{6,10},{... | collective-permute-start | bytes 3145736 | tf_op jit(solution)/shard_map/ppermute | solution.py:299
  27.2 13.4 %collective-permute-start.5 = (bf16[2,2,64,512]{3,2,1,0:T(8,128)(2,1)S(1)}, bf16[2,2,64,512]{3,2,1,0:T(8,128)(2,1)S(1)}, u32[]{:S(2)}, u32[]{:S(2)}) collective-permute-start(bf16[2,2,64,512]{3,2,1,0:T(8,128)(2,1)S(1)} %get-tuple-element.55), channel_id=1, source_target_pairs={{0,3},{1,0},{2,1},{3,2},{4,7},{5,4},{6,5},{7,6},{8,11},{9,8},{10,9... | collective-permute-start | bytes 786440 | tf_op jit(solution)/shard_map/ppermute | solution.py:299
  30.0 32.5 %collective-permute-start.4 = (bf16[2,2,64,512]{3,2,1,0:T(8,128)(2,1)}, bf16[2,2,64,512]{3,2,1,0:T(8,128)(2,1)}, u32[]{:S(2)}, u32[]{:S(2)}) collective-permute-start(bf16[2,2,64,512]{3,2,1,0:T(8,128)(2,1)} %get-tuple-element.56), channel_id=1, source_target_pairs={{0,2},{1,3},{2,0},{3,1},{4,6},{5,7},{6,4},{7,5},{8,10},{9,11},{10,... | collective-permute-start | bytes 786440 | tf_op jit(solution)/shard_map/ppermute | solution.py:299
  40.6 0.7 copy-start.1
  41.3 21.1 %collective-permute-start.3 = (bf16[2,2,64,512]{3,2,1,0:T(8,128)(2,1)}, bf16[2,2,64,512]{3,2,1,0:T(8,128)(2,1)}, u32[]{:S(2)}, u32[]{:S(2)}) collective-permute-start(bf16[2,2,64,512]{3,2,1,0:T(8,128)(2,1)} %get-tuple-element.57), channel_id=1, source_target_pairs={{0,1},{1,2},{2,3},{3,0},{4,5},{5,6},{6,7},{7,4},{8,9},{9,10},{10,1... | collective-permute-start | bytes 786440 | tf_op jit(solution)/shard_map/ppermute | solution.py:299
  61.1 5.9 %copy-start = (bf16[8,2,16,2048]{3,2,1,0:T(8,128)(2,1)S(1)}, bf16[8,2,16,2048]{3,2,1,0:T(8,128)(2,1)}, u32[]{:S(2)}) copy-start(bf16[8,2,16,2048]{3,2,1,0:T(8,128)(2,1)} %get-tuple-element.36.refs_0_) | copy-start | bytes 3145732
  64.3 27.7 %collective-permute-start.6 = (bf16[2,2,64,2048]{3,2,1,0:T(8,128)(2,1)S(1)}, bf16[2,2,64,2048]{3,2,1,0:T(8,128)(2,1)}, u32[]{:S(2)}, u32[]{:S(2)}) collective-permute-start(bf16[2,2,64,2048]{3,2,1,0:T(8,128)(2,1)S(1)} %cut.1), channel_id=1, source_target_pairs={{0,8},{4,12},{8,0},{12,4},{1,9},{5,13},{9,1},{13,5},{2,10},{6,14},... | collective-permute-start | bytes 3145736 | tf_op jit(solution)/shard_map/ppermute | solution.py:299
  71.1 33.4 %all-to-all-start.1 = ((bf16[32,2,2,16,512]{4,3,2,1,0:T(8,128)(2,1)}), bf16[32,2,2,16,512]{4,3,2,1,0:T(8,128)(2,1)}, u32[]{:S(2)}, u32[]{:S(2)}) async-start(bf16[32,2,2,16,512]{4,3,2,1,0:T(8,128)(2,1)} %bitcast.11), calls=%async_computation.1 | async-start | bytes 4194304 | tf_op jit(solution)/shard_map/all_to_all | solution.py:346
  80.2 34.0 %collective-permute-start.8 = (bf16[2,2,64,2048]{3,2,1,0:T(8,128)(2,1)}, bf16[2,2,64,2048]{3,2,1,0:T(8,128)(2,1)S(1)}, u32[]{:S(2)}, u32[]{:S(2)}) collective-permute-start(bf16[2,2,64,2048]{3,2,1,0:T(8,128)(2,1)} %get-tuple-element.53), channel_id=1, source_target_pairs={{0,12},{4,0},{8,4},{12,8},{1,13},{5,1},{9,5},{13,9},{2,14},{6,2},{... | collective-permute-start | bytes 3145736 | tf_op jit(solution)/shard_map/ppermute | solution.py:299
  80.3 34.0 %collective-permute-start.7 = (bf16[2,2,64,2048]{3,2,1,0:T(8,128)(2,1)}, bf16[2,2,64,2048]{3,2,1,0:T(8,128)(2,1)S(1)}, u32[]{:S(2)}, u32[]{:S(2)}) collective-permute-start(bf16[2,2,64,2048]{3,2,1,0:T(8,128)(2,1)} %get-tuple-element.54), channel_id=1, source_target_pairs={{0,4},{4,8},{8,12},{12,0},{1,5},{5,9},{9,13},{13,1},{2,6},{6,10},{... | collective-permute-start | bytes 3145736 | tf_op jit(solution)/shard_map/ppermute | solution.py:299
  104.5 9.7 %copy-start.2 = (bf16[2,2,64,512]{3,2,1,0:T(8,128)(2,1)S(1)}, bf16[2,2,64,512]{3,2,1,0:T(8,128)(2,1)}, u32[]{:S(2)}) copy-start(bf16[2,2,64,512]{3,2,1,0:T(8,128)(2,1)} %copy-done.1) | copy-start | bytes 786436
  104.5 31.1 %all-to-all-start.2 = ((bf16[4,2,4,2,2,16,512]{6,5,4,3,2,1,0:T(8,128)(2,1)}), bf16[4,2,4,2,2,16,512]{6,5,4,3,2,1,0:T(8,128)(2,1)}, u32[]{:S(2)}, u32[]{:S(2)}) async-start(bf16[4,2,4,2,2,16,512]{6,5,4,3,2,1,0:T(8,128)(2,1)} %bitcast.12), calls=%async_computation.2 | async-start | bytes 4194304 | tf_op jit(solution)/shard_map/all_to_all | solution.py:350
  118.6 9.5 %collective-permute-start.9 = (bf16[2,2,64,512]{3,2,1,0:T(8,128)(2,1)S(1)}, bf16[2,2,64,512]{3,2,1,0:T(8,128)(2,1)S(1)}, u32[]{:S(2)}, u32[]{:S(2)}) collective-permute-start(bf16[2,2,64,512]{3,2,1,0:T(8,128)(2,1)S(1)} %get-tuple-element.50), channel_id=1, source_target_pairs={{0,1},{1,2},{2,3},{3,0},{4,5},{5,6},{6,7},{7,4},{8,9},{9,10},{10,1... | collective-permute-start | bytes 786440 | tf_op jit(solution)/shard_map/ppermute | solution.py:299
  120.2 13.1 %collective-permute-start.10 = (bf16[2,2,64,512]{3,2,1,0:T(8,128)(2,1)S(1)}, bf16[2,2,64,512]{3,2,1,0:T(8,128)(2,1)S(1)}, u32[]{:S(2)}, u32[]{:S(2)}) collective-permute-start(bf16[2,2,64,512]{3,2,1,0:T(8,128)(2,1)S(1)} %get-tuple-element.51), channel_id=1, source_target_pairs={{0,2},{1,3},{2,0},{3,1},{4,6},{5,7},{6,4},{7,5},{8,10},{9,11},{10,... | collective-permute-start | bytes 786440 | tf_op jit(solution)/shard_map/ppermute | solution.py:299
  122.9 10.4 %collective-permute-start.11 = (bf16[2,2,64,512]{3,2,1,0:T(8,128)(2,1)S(1)}, bf16[2,2,64,512]{3,2,1,0:T(8,128)(2,1)S(1)}, u32[]{:S(2)}, u32[]{:S(2)}) collective-permute-start(bf16[2,2,64,512]{3,2,1,0:T(8,128)(2,1)S(1)} %get-tuple-element.52), channel_id=1, source_target_pairs={{0,3},{1,0},{2,1},{3,2},{4,7},{5,4},{6,5},{7,6},{8,11},{9,8},{10,9... | collective-permute-start | bytes 786440 | tf_op jit(solution)/shard_map/ppermute | solution.py:299
